TPU v7x, 128 devices: a whole 4x4x4 slice. The times are simulated.
128 devices in a mesh: dp: 2 (over core), expert: 64 (over x, y, z).
Axes of the slice: x: 4, y: 4, z: 4, core: 2. Of those that a mesh axis runs over, the one named last changes fastest.
Arguments:
- tokens: bfloat16 [64, 512, 1024], P('expert', 'dp'), may hold values from -6 to 6
- teacher: bfloat16 [64, 512, 1024], P('expert', 'dp'), may hold values from -6 to 6
- lengths: int32 [64], P('expert'), may hold values from 128 to 512, as said below
- routes: int32 [64, 512, 1], P('expert', 'dp'), may hold values from 0 to 63; in each aligned block of 256 rows (0 to 255, 256 to 511, ..., all dimensions but the last counted through in order) at most 8 rows name the same one
- ln1_gain: bfloat16 [1024], P(('dp', 'expert')), may hold values from 0.5 to 1.5
- ln1_bias: bfloat16 [1024], P(('dp', 'expert')), may hold values from -1.75 to 1.75
- query_key_value_weight: bfloat16 [1024, 3072], P(('dp', 'expert')), may hold values from -0.1875 to 0.1875
- output_weight: bfloat16 [1024, 1024], P(('dp', 'expert')), may hold values from -1.5 to 1.5
- ln2_gain: bfloat16 [1024], P(('dp', 'expert')), may hold values from 0.5 to 1.5
- ln2_bias: bfloat16 [1024], P(('dp', 'expert')), may hold values from -1.75 to 1.75
- router_weight: bfloat16 [1024, 64], P(('dp', 'expert')), may hold values from -0.125 to 0.125
- w_in: bfloat16 [64, 1024, 4096], P('expert', 'dp'), may hold values from -0.1875 to 0.1875
- w_down: bfloat16 [64, 4096, 1024], P('expert', 'dp'), may hold values from -6 to 6
Outputs:
- mixed_out: bfloat16 [64, 512, 1024], P('expert', 'dp')
- loss_value: float32 [], replicated
- grad_tokens: float32 [64, 512, 1024], P('expert', 'dp')
- grad_ln1_gain: float32 [1024], P(('dp', 'expert'))
- grad_ln1_bias: float32 [1024], P(('dp', 'expert'))
- grad_w_qkv: float32 [1024, 3072], P(('dp', 'expert'))
- grad_w_out: float32 [1024, 1024], P(('dp', 'expert'))
- grad_ln2_gain: float32 [1024], P(('dp', 'expert'))
- grad_ln2_bias: float32 [1024], P(('dp', 'expert'))
- grad_w_router: float32 [1024, 64], P(('dp', 'expert'))
- grad_w_in: float32 [64, 1024, 4096], P('expert', 'dp')
- grad_w_down: float32 [64, 4096, 1024], P('expert', 'dp')
Inputs may be any that keep to these rules, and one draw needn't show every extreme that they name: `lengths`: some slot has exactly 512 valid tokens in every draw; the tokens of a slot past its length are padding. `routes`: within the rows of one device (aligned blocks of 256 positions of a slot) no expert is named more than 8 times, and 8 is reached.
All inputs are finite; a program needn't handle non-finite values.
Results may differ from a plain program's by a relative error of at most 0.012.
Values may be sent and summed in bfloat16 or wider, within the bound.
A program may use at most 192 MiB of HBM per device.

v0:
```python
import jax
import jax.numpy as jnp
from jax import lax
from jax.experimental import pallas as pl
from jax.experimental.pallas import tpu as pltpu
from jax.sharding import PartitionSpec as P

MESH = pl.DeviceIdType.MESH
SIDE = 4
FULL = slice(None)

AG_COLS = 4224
AG_PIECES = ((0, 768, 1408), (1408, 2176, 2816), (2816, 3584, 4224))


def place(region, c0, c1):
    return tuple(region) + (FULL, pl.ds(c0, c1 - c0))


def coords():
    e = lax.axis_index("expert")
    return [e // 16, (e // 4) % 4, e % 4]


def shifted(pos, axis, by):
    out = list(pos)
    out[axis] = (pos[axis] + by) % SIDE
    return out


def chip(pos):
    return {"expert": pos[0] * 16 + pos[1] * 4 + pos[2]}


def neighbours(pos):
    return [chip(shifted(pos, axis, by)) for axis in range(3) for by in (1, 3)]


def greet(pos, core):
    barrier = pltpu.get_barrier_semaphore()
    for other in neighbours(pos) + [{"dp": 1 - core}]:
        pl.semaphore_signal(barrier, inc=1, device_id=other, device_id_type=MESH)
    pl.semaphore_wait(barrier, 7)


class Sender:
    def __init__(self, send_sems, recv_sems):
        self.send_sems, self.recv_sems, self.count, self.sent = send_sems, recv_sems, 0, []

    def __call__(self, src, dst, device):
        copy = pltpu.make_async_remote_copy(
            src_ref=src,
            dst_ref=dst,
            send_sem=self.send_sems.at[self.count],
            recv_sem=self.recv_sems.at[self.count],
            device_id=device,
            device_id_type=MESH,
        )
        copy.start()
        self.count += 1
        self.sent.append(copy)
        return copy


def gather_kernel(shard, w_in, w_down, whole, in_other, down_other, own_sem, send_sems, recv_sems):
    pos = coords()
    core = lax.axis_index("dp")
    partner = {"dp": 1 - core}
    own = pltpu.make_async_copy(shard, whole.at[(core, *pos)], own_sem)
    own.start()
    greet(pos, core)
    send = Sender(send_sems, recv_sems)
    across = [send(w_in, in_other, partner), send(w_down, down_other, partner)]
    own.wait()

    def share(region, c0, c1, device):
        spot = whole.at[place([core] + region, c0, c1)]
        return send(spot, spot, device)

    for stage in range(3):
        first = []
        for piece, (c0, mid, c1) in enumerate(AG_PIECES):
            order = [(piece + step) % 3 for step in range(3)]
            axis = order[stage]
            done = order[:stage]
            region = [FULL if a in done else pos[a] for a in range(3)]
            up, down = chip(shifted(pos, axis, 1)), chip(shifted(pos, axis, 3))
            first.append((axis, region, up, down, share(region, c0, c1, up), share(region, c0, c1, down)))
        if stage == 2:
            for (c0, mid, c1), (axis, region, up, down, _, _) in zip(AG_PIECES, first):
                across.append(share(region, c0, c1, partner))
        second = []
        for (c0, mid, c1), (axis, region, up, down, to_up, to_down) in zip(AG_PIECES, first):
            below, above = list(region), list(region)
            below[axis], above[axis] = (pos[axis] + 3) % SIDE, (pos[axis] + 1) % SIDE
            to_up.wait_recv()
            on_up = share(below, c0, mid, up)
            to_down.wait_recv()
            on_down = share(above, mid, c1, down)
            second.append((on_up, on_down))
            if stage == 2:
                across.append(share(below, c0, c1, partner))
                across.append(share(above, c0, c1, partner))
        for (c0, mid, c1), (axis, region, up, down, _, _), (on_up, on_down) in zip(AG_PIECES, first, second):
            on_up.wait_recv()
            on_down.wait_recv()
            if stage == 2:
                far = list(region)
                far[axis] = (pos[axis] + 2) % SIDE
                across.append(share(far, c0, c1, partner))
    for copy in across:
        copy.wait_recv()
    for copy in send.sent:
        copy.wait_send()


def gather_layer(shard, w_in, w_down):
    copies = 3 * 3 * 4 + 3 * 4 + 2
    anywhere = pl.BlockSpec(memory_space=pl.ANY)
    whole, in_other, down_other = pl.pallas_call(
        gather_kernel,
        out_shape=(
            jax.ShapeDtypeStruct((2, SIDE, SIDE, SIDE, 8, AG_COLS), jnp.bfloat16),
            jax.ShapeDtypeStruct(w_in.shape, w_in.dtype),
            jax.ShapeDtypeStruct(w_down.shape, w_down.dtype),
        ),
        in_specs=[anywhere] * 3,
        out_specs=(anywhere,) * 3,
        scratch_shapes=[
            pltpu.SemaphoreType.DMA,
            pltpu.SemaphoreType.DMA((copies,)),
            pltpu.SemaphoreType.DMA((copies,)),
        ],
        compiler_params=pltpu.CompilerParams(collective_id=0, has_side_effects=True),
        name="gather_layer",
    )(shard, w_in, w_down)
    return whole.reshape(1024, AG_COLS), in_other, down_other


RS_COLS = (3072, 1024, 256)
RS_KINDS = (jnp.bfloat16, jnp.bfloat16, jnp.float32)
RS_HALVES = (
    (((0, 0, 768),), ((0, 768, 1536),)),
    (((0, 1536, 2304),), ((0, 2304, 3072),)),
    (((1, 0, 768),), ((1, 768, 1024), (2, 0, 256))),
)
RS_PIECES = tuple(h0 + h1 for h0, h1 in RS_HALVES)


def reduce_kernel(*rest):
    source, outs, rest = rest[:3], rest[3:6], rest[6:]
    refs, (send_sems, recv_sems) = list(rest[:-2]), rest[-2:]
    take = iter(refs)
    pos = coords()
    core = lax.axis_index("dp")
    partner = {"dp": 1 - core}
    greet(pos, core)
    send = Sender(send_sems, recv_sems)
    landed = (next(take), next(take), next(take))

    opening = []
    for piece in range(3):
        copies = []
        for kind, c0, c1 in RS_PIECES[piece]:
            copies.append(
                send(
                    source[kind].at[place([1 - core, FULL, FULL, FULL], c0, c1)],
                    landed[kind].at[place([FULL, FULL, FULL], c0, c1)],
                    partner,
                )
            )
        opening.append(copies)

    def whole_sum(kind, index, c0, c1):
        spot = index + (FULL, pl.ds(c0, c1 - c0))
        mine = source[kind][(core,) + spot].astype(jnp.float32)
        return mine + landed[kind][spot].astype(jnp.float32)

    sums = []
    for piece in range(3):
        sums.append(whole_sum)

    for stage in range(3):
        plans = []
        for piece in range(3):
            order = [(piece + step) % 3 for step in range(3)]
            axis = order[stage]
            free = sorted(order[stage + 1:])
            fixed = order[:stage]
            bufs = {}
            for half in range(2):
                for n, (kind, c0, c1) in enumerate(RS_HALVES[piece][half]):
                    for what in ("sendA", "recvA"):
                        bufs[what, half, n] = next(take)
            for way in range(2):
                for n, (kind, c0, c1) in enumerate(RS_PIECES[piece]):
                    for what in ("sendB", "recvB"):
                        bufs[what, way, n] = next(take)
            up, down = chip(shifted(pos, axis, 1)), chip(shifted(pos, axis, 3))
            plans.append((axis, free, fixed, bufs, (up, down)))

        def each(free, body):
            total = SIDE ** len(free)

            @pl.loop(0, total)
            def _(i):
                if len(free) == 2:
                    body((i // SIDE, i % SIDE))
                elif len(free) == 1:
                    body((i,))
                else:
                    body(())

        def index_of(axis, free, fixed, at, spots):
            index = [None] * 3
            for a in fixed:
                index[a] = pos[a]
            index[axis] = at
            for a, s in zip(free, spots):
                index[a] = s
            return tuple(index)

        firsts = []
        for piece, (axis, free, fixed, bufs, ways) in enumerate(plans):
            if stage == 0:
                for copy in opening[piece]:
                    copy.wait_recv()
            far = (pos[axis] + 2) % SIDE
            copies = []
            for half in range(2):
                def fill(spots, half=half, axis=axis, free=free, fixed=fixed, bufs=bufs, piece=piece, far=far):
                    for n, (kind, c0, c1) in enumerate(RS_HALVES[piece][half]):
                        block = sums[piece](kind, index_of(axis, free, fixed, far, spots), c0, c1)
                        buf = bufs["sendA", half, n]
                        buf[spots + (FULL, FULL)] = block.astype(buf.dtype)

                each(free, fill)
                for n in range(len(RS_HALVES[piece][half])):
                    copies.append(send(bufs["sendA", half, n], bufs["recvA", half, n], ways[half]))
            firsts.append(copies)
        seconds = []
        for piece, (axis, free, fixed, bufs, ways) in enumerate(plans):
            for copy in firsts[piece]:
                copy.wait_recv()
            copies = []
            for way in range(2):
                at = (pos[axis] + (1, 3)[way]) % SIDE

                def fill(spots, way=way, axis=axis, free=free, fixed=fixed, bufs=bufs, piece=piece, at=at):
                    index = index_of(axis, free, fixed, at, spots)
                    n = 0
                    for half in range(2):
                        for m, (kind, c0, c1) in enumerate(RS_HALVES[piece][half]):
                            block = sums[piece](kind, index, c0, c1)
                            if half == way:
                                block = block + bufs["recvA", half, m][spots + (FULL, FULL)].astype(jnp.float32)
                            buf = bufs["sendB", way, n]
                            buf[spots + (FULL, FULL)] = block.astype(buf.dtype)
                            n += 1

                each(free, fill)
                for n in range(len(RS_PIECES[piece])):
                    copies.append(send(bufs["sendB", way, n], bufs["recvB", way, n], ways[way]))
            seconds.append(copies)
        for piece, (axis, free, fixed, bufs, ways) in enumerate(plans):
            for copy in seconds[piece]:
                copy.wait_recv()
            if stage < 2:
                total = {n: next(take) for n in range(len(RS_PIECES[piece]))}
            else:
                total = None

            def fill(spots, axis=axis, free=free, fixed=fixed, bufs=bufs, piece=piece, total=total):
                index = index_of(axis, free, fixed, pos[axis], spots)
                for n, (kind, c0, c1) in enumerate(RS_PIECES[piece]):
                    block = sums[piece](kind, index, c0, c1)
                    for way in range(2):
                        block = block + bufs["recvB", way, n][spots + (FULL, FULL)].astype(jnp.float32)
                    if total is None:
                        outs[kind][:, c0:c1] = block
                    else:
                        total[n][spots + (FULL, FULL)] = block

            each(free, fill)
            if total is not None:
                def partial(kind, index, c0, c1, total=total, piece=piece, free=free):
                    spots = tuple(index[a] for a in free)
                    for n, (k, s0, s1) in enumerate(RS_PIECES[piece]):
                        if k == kind and s0 <= c0 and c1 <= s1:
                            return total[n][spots + (FULL, pl.ds(c0 - s0, c1 - c0))]

                sums[piece] = partial
    for copy in send.sent:
        copy.wait_send()


def reduce_layer(*parts):
    parts = [p.reshape(2, SIDE, SIDE, SIDE, 8, c).astype(k) for p, c, k in zip(parts, RS_COLS, RS_KINDS)]
    scratch = [pltpu.VMEM((SIDE, SIDE, SIDE, 8, c), k) for c, k in zip(RS_COLS, RS_KINDS)]
    copies = sum(len(p) for p in RS_PIECES)
    for stage in range(3):
        lead = (SIDE,) * (2 - stage)
        for piece in range(3):
            for half in range(2):
                for kind, c0, c1 in RS_HALVES[piece][half]:
                    scratch += [pltpu.VMEM(lead + (8, c1 - c0), RS_KINDS[kind])] * 2
                    copies += 1
            for way in range(2):
                for kind, c0, c1 in RS_PIECES[piece]:
                    scratch += [pltpu.VMEM(lead + (8, c1 - c0), RS_KINDS[kind])] * 2
                    copies += 1
        if stage < 2:
            for piece in range(3):
                for kind, c0, c1 in RS_PIECES[piece]:
                    scratch += [pltpu.VMEM(lead + (8, c1 - c0), jnp.float32)]
    vmem = pl.BlockSpec(memory_space=pltpu.VMEM)
    return pl.pallas_call(
        reduce_kernel,
        out_shape=tuple(jax.ShapeDtypeStruct((8, c), jnp.float32) for c in RS_COLS),
        in_specs=[vmem] * 3,
        out_specs=(vmem,) * 3,
        scratch_shapes=scratch + [pltpu.SemaphoreType.DMA((copies,)), pltpu.SemaphoreType.DMA((copies,))],
        compiler_params=pltpu.CompilerParams(
            collective_id=1, has_side_effects=True, vmem_limit_bytes=60 * 1024 * 1024
        ),
        name="reduce_layer",
    )(*parts)


ROWS = 512
WIDTH = 1024
HIDDEN = 4096
HALF_IN = WIDTH // 2
HALF_FF = HIDDEN // 2
EXTRA = 128
TILE = 512
N_TILES = HIDDEN // TILE
HALF_TILES = N_TILES // 2
CURVE = 0.7978845608028654


def dot_nt(a, b):
    return lax.dot_general(a, b, (((1,), (1,)), ((), ())), preferred_element_type=jnp.float32)


def dot_nn(a, b):
    return lax.dot_general(a, b, (((1,), (0,)), ((), ())), preferred_element_type=jnp.float32)


def dot_tn(a, b):
    return lax.dot_general(a, b, (((0,), (0,)), ((), ())), preferred_element_type=jnp.float32)


def to_chips(pos, me, source, target, send_sem, recv_sem):
    @pl.loop(0, 64)
    def _(n):
        there = [(pos[0] + 2 + n // 16) % 4, (pos[1] + 2 + (n // 4) % 4) % 4, (pos[2] + 2 + n % 4) % 4]
        d = there[0] * 16 + there[1] * 4 + there[2]

        @pl.when(n != 42)
        def _():
            pltpu.make_async_remote_copy(
                src_ref=source.at[d],
                dst_ref=target.at[me],
                send_sem=send_sem,
                recv_sem=recv_sem,
                device_id={"expert": d},
                device_id_type=MESH,
            ).start()


def all_but_one(ref, sem):
    pltpu.make_async_copy(ref.at[pl.ds(0, 63)], ref.at[pl.ds(0, 63)], sem).wait()


def expert_kernel(
    x, r, w1_own, w1_other, w2_own, w2_other,
    y_back, d_back, g1, g2,
    w1, w2, x_in, r_in, xb, xt, act, slope, d_pre, acc, d_exp, out_rows,
    sent1, sent2, got1, got2, stage,
    w_sems, x_sems, r_sems, y_sems, d_sems, own_sems, pass_s, pass_r, out_sems,
):
    pos = coords()
    me = lax.axis_index("expert")
    core = lax.axis_index("dp")
    loads = [
        pltpu.make_async_copy(w1_own, w1.at[core], w_sems.at[0]),
        pltpu.make_async_copy(w1_other, w1.at[1 - core], w_sems.at[1]),
        pltpu.make_async_copy(w2_own, w2.at[core], w_sems.at[2]),
        pltpu.make_async_copy(w2_other, w2.at[1 - core], w_sems.at[3]),
    ]
    barrier = pltpu.get_barrier_semaphore()

    @pl.loop(1, 64)
    def _(n):
        pl.semaphore_signal(barrier, inc=1, device_id={"expert": (me + n) % 64}, device_id_type=MESH)

    pl.semaphore_signal(barrier, inc=1, device_id={"dp": 1 - core}, device_id_type=MESH)
    own_x = pltpu.make_async_copy(x.at[me], x_in.at[me], own_sems.at[0])
    own_r = pltpu.make_async_copy(r.at[me], r_in.at[me], own_sems.at[1])
    own_x.start()
    own_r.start()
    for load in loads:
        load.start()
    pl.semaphore_wait(barrier, 64)
    to_chips(pos, me, x, x_in, x_sems.at[0], x_sems.at[1])
    to_chips(pos, me, r, r_in, r_sems.at[0], r_sems.at[1])
    own_x.wait()
    all_but_one(x_in, x_sems.at[1])
    for load in loads:
        load.wait()

    @pl.loop(0, 8)
    def _(i):
        rows = x_in[pl.ds(i * 8, 8)].astype(jnp.float32).reshape(64, WIDTH)
        xb[pl.ds(pl.multiple_of(i * 64, 64), 64), :] = rows.astype(jnp.bfloat16)

    acc[...] = jnp.zeros_like(acc)

    @pl.loop(0, N_TILES)
    def _(c):
        cols = pl.ds(pl.multiple_of(c * TILE, TILE), TILE)
        pre = dot_nn(xb[:, :HALF_IN], w1[0, :, cols]) + dot_nn(xb[:, HALF_IN:], w1[1, :, cols])
        square = pre * pre
        t = jnp.tanh(CURVE * pre * (1.0 + 0.044715 * square))
        low = (0.5 * pre * (1.0 + t)).astype(jnp.bfloat16)
        act[:, cols] = low
        slope[:, cols] = 0.5 * (1.0 + t) + (0.5 * CURVE) * pre * (1.0 - t * t) * (1.0 + (3 * 0.044715) * square)
        half = c // HALF_TILES
        ff = pl.ds(pl.multiple_of((c % HALF_TILES) * TILE, TILE), TILE)
        acc[...] += dot_nn(low, w2[half, ff, :])

    own_r.wait()
    all_but_one(r_in, r_sems.at[1])

    @pl.loop(0, 8)
    def _(i):
        rows = pl.ds(pl.multiple_of(i * 64, 64), 64)
        low = acc[rows, :].astype(jnp.bfloat16)
        out = low.astype(jnp.float32)
        out_rows[pl.ds(i * 8, 8)] = out.reshape(8, 8, WIDTH).astype(jnp.bfloat16)
        parted = r_in[pl.ds(i * 8, 8)].astype(jnp.float32).reshape(64, WIDTH + EXTRA)
        gate = parted[:, WIDTH : WIDTH + 1] + parted[:, WIDTH + 1 : WIDTH + 2]
        valid = parted[:, WIDTH + 2 : WIDTH + 3]
        d_exp[rows, :] = (gate * valid * (parted[:, :WIDTH] + gate * out)).astype(jnp.bfloat16)

    own_y = pltpu.make_async_copy(out_rows.at[me], y_back.at[me], own_sems.at[2])
    own_y.start()
    to_chips(pos, me, out_rows, y_back, y_sems.at[0], y_sems.at[1])
    acc[...] = jnp.zeros_like(acc)

    @pl.loop(0, N_TILES)
    def _(c):
        cols = pl.ds(pl.multiple_of(c * TILE, TILE), TILE)
        half = c // HALF_TILES
        ff = pl.ds(pl.multiple_of((c % HALF_TILES) * TILE, TILE), TILE)
        d_act = dot_nt(d_exp[...], w2[half, ff, :])
        low = (slope[:, cols] * d_act).astype(jnp.bfloat16)
        d_pre[:, cols] = low
        acc[:, :HALF_IN] += dot_nt(low, w1[0, :, cols])
        acc[:, HALF_IN:] += dot_nt(low, w1[1, :, cols])

    own_y.wait()
    all_but_one(out_rows, y_sems.at[0])

    @pl.loop(0, 8)
    def _(i):
        rows = pl.ds(pl.multiple_of(i * 64, 64), 64)
        out_rows[pl.ds(i * 8, 8)] = acc[rows, :].reshape(8, 8, WIDTH).astype(jnp.bfloat16)

    own_d = pltpu.make_async_copy(out_rows.at[me], d_back.at[me], own_sems.at[3])
    own_d.start()
    to_chips(pos, me, out_rows, d_back, d_sems.at[0], d_sems.at[1])

    xt[...] = xb[...].astype(jnp.float32).T.astype(jnp.bfloat16)

    def passed(buf, got, c, base):
        return pltpu.make_async_remote_copy(
            src_ref=buf.at[c],
            dst_ref=got.at[c],
            send_sem=pass_s.at[base + c],
            recv_sem=pass_r.at[base + c],
            device_id={"dp": 1 - core},
            device_id_type=MESH,
        )

    def in_rows(half):
        return xt[pl.ds(pl.multiple_of(half * HALF_IN, HALF_IN), HALF_IN), :]

    @pl.loop(0, N_TILES)
    def _(c):
        cols = pl.ds(pl.multiple_of(c * TILE, TILE), TILE)
        sent1[c] = dot_nn(in_rows(1 - core), d_pre[:, cols]).astype(jnp.bfloat16)
        passed(sent1, got1, c, 0).start()

    @pl.loop(0, HALF_TILES)
    def _(c):
        cols = pl.ds(pl.multiple_of((1 - core) * HALF_FF + c * TILE, TILE), TILE)
        sent2[c] = dot_tn(act[:, cols], d_exp[...]).astype(jnp.bfloat16)
        passed(sent2, got2, c, N_TILES).start()

    def out1(c, slot):
        cols = pl.ds(pl.multiple_of(c * TILE, TILE), TILE)
        return pltpu.make_async_copy(stage.at[slot, :, pl.ds(0, TILE)], g1.at[:, cols], out_sems.at[slot])

    def out2(c, slot):
        rows = pl.ds(pl.multiple_of(c * TILE, TILE), TILE)
        return pltpu.make_async_copy(stage.at[slot], g2.at[rows, :], out_sems.at[slot])

    @pl.loop(0, N_TILES)
    def _(c):
        slot = c % 2
        cols = pl.ds(pl.multiple_of(c * TILE, TILE), TILE)

        @pl.when(c >= 2)
        def _():
            out1(c - 2, slot).wait()

        passed(sent1, got1, c, 0).wait_recv()
        stage[slot, :, pl.ds(0, TILE)] = dot_nn(in_rows(core), d_pre[:, cols]) + got1[c].astype(jnp.float32)
        out1(c, slot).start()

    out1(N_TILES - 2, 0).wait()
    out1(N_TILES - 1, 1).wait()

    @pl.loop(0, HALF_TILES)
    def _(c):
        slot = c % 2
        cols = pl.ds(pl.multiple_of(core * HALF_FF + c * TILE, TILE), TILE)

        @pl.when(c >= 2)
        def _():
            out2(c - 2, slot).wait()

        passed(sent2, got2, c, N_TILES).wait_recv()
        stage[slot] = dot_tn(act[:, cols], d_exp[...]) + got2[c].astype(jnp.float32)
        out2(c, slot).start()

    out2(HALF_TILES - 2, 0).wait()
    out2(HALF_TILES - 1, 1).wait()

    @pl.loop(0, N_TILES)
    def _(c):
        passed(sent1, got1, c, 0).wait_send()

    @pl.loop(0, HALF_TILES)
    def _(c):
        passed(sent2, got2, c, N_TILES).wait_send()

    own_d.wait()
    all_but_one(x_in, x_sems.at[0])
    all_but_one(r_in, r_sems.at[0])
    all_but_one(out_rows, d_sems.at[0])
    all_but_one(out_rows, y_sems.at[1])
    all_but_one(out_rows, d_sems.at[1])


def experts(x, r, w1_own, w1_other, w2_own, w2_other):
    low, wide = jnp.bfloat16, jnp.float32
    anywhere = pl.BlockSpec(memory_space=pl.ANY)
    return pl.pallas_call(
        expert_kernel,
        out_shape=(
            jax.ShapeDtypeStruct((64, 8, WIDTH), low),
            jax.ShapeDtypeStruct((64, 8, WIDTH), low),
            jax.ShapeDtypeStruct((HALF_IN, HIDDEN), wide),
            jax.ShapeDtypeStruct((HALF_FF, WIDTH), wide),
        ),
        in_specs=[anywhere] * 6,
        out_specs=(anywhere,) * 4,
        scratch_shapes=[
            pltpu.VMEM((2, HALF_IN, HIDDEN), low),
            pltpu.VMEM((2, HALF_FF, WIDTH), low),
            pltpu.VMEM((64, 8, WIDTH), low),
            pltpu.VMEM((64, 8, WIDTH + EXTRA), low),
            pltpu.VMEM((ROWS, WIDTH), low),
            pltpu.VMEM((WIDTH, ROWS), low),
            pltpu.VMEM((ROWS, HIDDEN), low),
            pltpu.VMEM((ROWS, HIDDEN), wide),
            pltpu.VMEM((ROWS, HIDDEN), low),
            pltpu.VMEM((ROWS, WIDTH), wide),
            pltpu.VMEM((ROWS, WIDTH), low),
            pltpu.VMEM((64, 8, WIDTH), low),
            pltpu.VMEM((N_TILES, HALF_IN, TILE), low),
            pltpu.VMEM((HALF_TILES, TILE, WIDTH), low),
            pltpu.VMEM((N_TILES, HALF_IN, TILE), low),
            pltpu.VMEM((HALF_TILES, TILE, WIDTH), low),
            pltpu.VMEM((2, HALF_IN, WIDTH), wide),
            pltpu.SemaphoreType.DMA((4,)),
            pltpu.SemaphoreType.DMA((2,)),
            pltpu.SemaphoreType.DMA((2,)),
            pltpu.SemaphoreType.DMA((2,)),
            pltpu.SemaphoreType.DMA((2,)),
            pltpu.SemaphoreType.DMA((4,)),
            pltpu.SemaphoreType.DMA((N_TILES + HALF_TILES,)),
            pltpu.SemaphoreType.DMA((N_TILES + HALF_TILES,)),
            pltpu.SemaphoreType.DMA((2,)),
        ],
        compiler_params=pltpu.CompilerParams(
            collective_id=2, has_side_effects=True, vmem_limit_bytes=63 * 1024 * 1024
        ),
        name="experts",
    )(x, r, w1_own, w1_other, w2_own, w2_other)


HEADS = 16


def layer_norm(values, scale_vec, offset):
    center = jnp.mean(values, -1, keepdims=True)
    centred = values - center
    spread = jnp.mean(centred * centred, -1, keepdims=True)
    inverse = lax.rsqrt(spread + 1e-05)
    normed = centred * inverse
    return (normed * scale_vec + offset, normed, inverse)


def norm_back(upstream, normed, inverse, scale_vec):
    scaled = upstream * scale_vec
    average = jnp.mean(scaled, -1, keepdims=True)
    project = jnp.mean(scaled * normed, -1, keepdims=True)
    return (
        inverse * (scaled - average - normed * project),
        jnp.sum(upstream * normed, 0),
        jnp.sum(upstream, 0),
    )


def times_transposed(left_mat, right_mat):
    return lax.dot_general(
        left_mat, right_mat, (((1,), (1,)), ((), ())), preferred_element_type=jnp.float32
    )


def transposed_times(left_mat, right_mat):
    return lax.dot_general(
        left_mat, right_mat, (((0,), (0,)), ((), ())), preferred_element_type=jnp.float32
    )


def per_device(
    tokens,
    teacher,
    lengths,
    routes,
    ln1_gain,
    ln1_bias,
    query_key_value_weight,
    output_weight,
    ln2_gain,
    ln2_bias,
    router_weight,
    w_in,
    w_down,
):
    group = tokens.shape[1]
    width = tokens.shape[2]
    head_dim = width // HEADS
    sources = lax.axis_size("expert")
    seq_len = group * lax.axis_size("dp")
    capacity = max(2, 2 * group // sources)
    core = lax.axis_index("dp")
    device = core * sources + lax.axis_index("expert")
    vectors = jnp.tile(jnp.stack([ln1_gain, ln1_bias, ln2_gain, ln2_bias]), (1, 8))
    vectors = jnp.where(jnp.arange(64)[None, :] // 8 == device % 8, vectors, 0)
    vectors = jnp.concatenate([vectors, jnp.zeros_like(vectors)], 0)
    layer, in_other, down_other = gather_layer(
        jnp.concatenate([query_key_value_weight, output_weight, router_weight, vectors], 1),
        w_in[0],
        w_down[0],
    )
    w_qkv = layer[:, : 3 * width]
    w_out = layer[:, 3 * width : 4 * width]
    w_router = layer[:, 4 * width : 4 * width + sources]
    vectors = layer[:, 4 * width + sources :].astype(jnp.float32)
    vectors = jnp.sum(vectors.reshape(16, 8, 8, 64), 1)
    gain_one, bias_one, gain_two, bias_two = [vectors[:, n].reshape(width) for n in range(4)]
    inputs = tokens[0].astype(jnp.float32)
    norm_full, normed_one, inverse_one = layer_norm(inputs, gain_one, bias_one)
    first_norm = norm_full.astype(jnp.bfloat16)
    query_key_value_rows = jnp.dot(
        first_norm, w_qkv, preferred_element_type=jnp.float32
    ).astype(jnp.bfloat16)
    queries = query_key_value_rows[:, :width].reshape(group, HEADS, head_dim)
    kv_whole = lax.all_gather(query_key_value_rows[:, width:], "dp", axis=0, tiled=True)
    key_rows = kv_whole[:, :width].reshape(seq_len, HEADS, head_dim)
    value_rows = kv_whole[:, width:].reshape(seq_len, HEADS, head_dim)
    query_pos = lax.axis_index("dp") * group + jnp.arange(group)
    key_pos = jnp.arange(seq_len)
    allowed = (key_pos[None, :] <= query_pos[:, None]) & (key_pos[None, :] < lengths[0])

    def score_block():
        scaled_raw = (
            jnp.einsum("qhd,khd->hqk", queries, key_rows, preferred_element_type=jnp.float32)
            * 0.125
        )
        return jnp.where(allowed[None], scaled_raw, -1e30)

    scores = score_block()
    maximum = jnp.max(scores, -1, keepdims=True)
    exponent = jnp.exp(scores - maximum)
    denominator = jnp.sum(exponent, -1, keepdims=True)
    log_total = maximum + jnp.log(denominator)
    probs_low = (exponent / denominator).astype(jnp.bfloat16)
    attention_result = jnp.einsum(
        "hqk,khd->qhd", probs_low, value_rows, preferred_element_type=jnp.float32
    )
    attention_result = attention_result.reshape(group, width).astype(jnp.bfloat16)
    residual_branch = jnp.dot(attention_result, w_out, preferred_element_type=jnp.float32)
    residual = inputs + residual_branch
    norm_two_full, normed_two, inverse_two = layer_norm(residual, gain_two, bias_two)
    second_norm = norm_two_full.astype(jnp.bfloat16)
    router_scores = jnp.dot(second_norm, w_router, preferred_element_type=jnp.float32)
    router_probs = jax.nn.softmax(router_scores, -1)
    route_ids = routes[0, :, 0]
    chosen = route_ids[:, None] == jnp.arange(sources)[None, :]
    gate_prob = jnp.sum(jnp.where(chosen, router_probs, 0.0), -1)
    ranking = jnp.cumsum(chosen.astype(jnp.int32), 0) - 1
    slot_ids = route_ids * capacity + jnp.sum(jnp.where(chosen, ranking, 0), -1)
    placing = (jnp.arange(sources * capacity)[:, None] == slot_ids[None, :]).astype(jnp.bfloat16)
    outgoing = jnp.dot(placing, second_norm, preferred_element_type=jnp.float32).astype(
        jnp.bfloat16
    )
    outgoing = outgoing.reshape(sources, capacity, width)
    valid_rows = (query_pos < lengths[0]).astype(jnp.float32)
    taught = teacher[0].astype(jnp.float32)
    gate_high = gate_prob.astype(jnp.bfloat16)
    gate_low = (gate_prob - gate_high.astype(jnp.float32)).astype(jnp.bfloat16)
    extras = jnp.stack([gate_high, gate_low, valid_rows.astype(jnp.bfloat16)], 1)
    extras = jnp.pad(extras, ((0, 0), (0, 125)))
    parting = jnp.concatenate([(residual - taught).astype(jnp.bfloat16), extras], 1)
    parting = jnp.dot(placing, parting, preferred_element_type=jnp.float32).astype(jnp.bfloat16)
    returned, d_back, grad_in_out, grad_down_out = experts(
        outgoing,
        parting.reshape(sources, capacity, width + 128),
        w_in[0],
        in_other,
        w_down[0],
        down_other,
    )
    expert_out = transposed_times(placing, returned.reshape(-1, width))
    mixed_out = (residual + gate_prob[:, None] * expert_out).astype(jnp.bfloat16)
    errors = mixed_out.astype(jnp.float32) - taught
    squares = jnp.sum(valid_rows[:, None] * errors * errors)
    count = jnp.sum(valid_rows)
    d_mixed = valid_rows[:, None] * errors
    d_gate = jnp.sum(d_mixed * expert_out, -1)
    d_norm_expert = transposed_times(placing, d_back.reshape(-1, width))
    d_logits = (d_gate * gate_prob)[:, None] * (chosen.astype(jnp.float32) - router_probs)
    router_full = w_router.astype(jnp.float32)
    grad_router = jnp.dot(
        second_norm.astype(jnp.float32).T, d_logits, precision=lax.Precision.HIGHEST
    )
    d_norm_two = d_norm_expert + jnp.dot(d_logits, router_full.T, precision=lax.Precision.HIGHEST)
    d_resid_part, grad_gain_two, grad_bias_two = norm_back(
        d_norm_two, normed_two, inverse_two, gain_two
    )
    d_resid = d_mixed + d_resid_part
    d_branch = d_resid.astype(jnp.bfloat16)
    grad_out = transposed_times(attention_result, d_branch)
    d_attended = (
        times_transposed(d_branch, w_out)
        .astype(jnp.bfloat16)
        .reshape(group, HEADS, head_dim)
    )
    probs_again = jnp.exp(score_block() - log_total)
    d_probs = jnp.einsum("qhd,khd->hqk", d_attended, value_rows, preferred_element_type=jnp.float32)
    delta_sum = jnp.sum(probs_again * d_probs, -1, keepdims=True)
    d_scores = (probs_again * (d_probs - delta_sum)).astype(jnp.bfloat16)
    d_queries = (
        jnp.einsum("hqk,khd->qhd", d_scores, key_rows, preferred_element_type=jnp.float32) * 0.125
    )
    d_keys = (
        jnp.einsum("hqk,qhd->khd", d_scores, queries, preferred_element_type=jnp.float32) * 0.125
    )
    d_values = jnp.einsum("hqk,qhd->khd", probs_low, d_attended, preferred_element_type=jnp.float32)
    d_kv_whole = jnp.concatenate(
        [d_keys.reshape(seq_len, width), d_values.reshape(seq_len, width)], 1
    )
    d_kv = lax.psum_scatter(d_kv_whole.astype(jnp.bfloat16), "dp", scatter_dimension=0, tiled=True)
    d_qkv = jnp.concatenate([d_queries.reshape(group, width).astype(jnp.bfloat16), d_kv], 1)
    grad_qkv = transposed_times(first_norm, d_qkv)
    d_norm_one = times_transposed(d_qkv, w_qkv)
    d_input_part, grad_gain_one, grad_bias_one = norm_back(
        d_norm_one, normed_one, inverse_one, gain_one
    )
    grad_tokens = d_resid + d_input_part
    vector_grads = jnp.stack(
        [grad_gain_one, grad_bias_one, grad_gain_two, grad_bias_two]
    ).reshape(4, 128, 8)
    vector_grads = jnp.pad(vector_grads.transpose(1, 0, 2), ((0, 0), (0, 4), (0, 56)))
    totals = jnp.zeros((8, 128), jnp.float32).at[0, 0].set(squares).at[1, 0].set(count)
    side = jnp.concatenate(
        [grad_router.reshape(128, 8, sources), vector_grads, jnp.broadcast_to(totals[None], (128, 8, 128))], 2
    )
    grad_qkv, grad_out, side = reduce_layer(grad_qkv, grad_out, side)
    grad_router = side[:, :sources]
    vector_grads = side[:4, sources : sources + 8]
    loss_value = side[0, 128] / (side[1, 128] * width)
    return (
        mixed_out[None],
        loss_value,
        grad_tokens[None],
        vector_grads[0],
        vector_grads[1],
        grad_qkv,
        grad_out,
        vector_grads[2],
        vector_grads[3],
        grad_router,
        grad_in_out[None],
        grad_down_out[None],
    )


def solution(mesh):
    placed = (
        P("expert", "dp", None),
        P("expert", "dp", None),
        P("expert"),
        P("expert", "dp", None),
        P(("dp", "expert")),
        P(("dp", "expert")),
        P(("dp", "expert"), None),
        P(("dp", "expert"), None),
        P(("dp", "expert")),
        P(("dp", "expert")),
        P(("dp", "expert"), None),
        P("expert", "dp", None),
        P("expert", "dp", None),
    )
    return jax.shard_map(
        per_device,
        mesh=mesh,
        in_specs=placed,
        out_specs=(
            P("expert", "dp", None),
            P(),
            P("expert", "dp", None),
            P(("dp", "expert")),
            P(("dp", "expert")),
            P(("dp", "expert"), None),
            P(("dp", "expert"), None),
            P(("dp", "expert")),
            P(("dp", "expert")),
            P(("dp", "expert"), None),
            P("expert", "dp", None),
            P("expert", "dp", None),
        ),
        check_vma=False,
    )
```

profile of v0, /device:TPU:0, one launch (start us, length us, event | category | flops | bytes accessed | tf_op | source)
XLA Modules:
  0.0 335.1 jit_solution(3147739064279186042)
XLA Ops:
  12.2 42.3 %gather_layer.1 = (bf16[2,4,4,4,8,4224]{5,4,3,2,1,0:T(8,128)(2,1)}, bf16[512,4096]{1,0:T(8,128)(2,1)}, bf16[2048,1024]{1,0:T(8,128)(2,1)}) custom-call(bf16[8,4224]{1,0:T(8,128)(2,1)} %concatenate.30.shard, bf16[512,4096]{1,0:T(8,128)(2,1)} %bitcast.162, bf16[2048,1024]{1,0:T(8,128)(2,1)} %bitcast.164), custom_call_target="tpu_custom_call" | custom-call | tf_op jit(solution)/shard_map/gather_layer/pallas_call | solution.py:120
  55.9 4.7 %fusion.6 = bf16[256,3072]{1,0:T(8,128)(2,1)S(1)} fusion(bf16[1024,4224]{1,0:T(8,128)(2,1)} %bitcast.186, bf16[1,256,1024]{2,1,0:T(8,128)(2,1)S(1)} %copy-done.8, f32[1024]{0:T(1024)S(1)} %add.122, f32[1024]{0:T(1024)S(1)} %mul.185, f32[256]{0:T(256)S(1)} %add_rsqrt_fusion.1, f32[256]{0:T(256)S(1)} %broadcast_multiply_fusion.5), kind=kOutput, calls=%fused_computation.13 | convolution fusion | flops 1612972032 | bytes 8398848 | tf_op jit(solution)/shard_map/dot_general | solution.py:681
  64.2 8.9 %all-gather.2.cloned.1.call-done = bf16[512,2048]{1,0:T(8,128)(2,1)} async-done(((bf16[256,2048]{1,0:T(8,128)(2,1)}), bf16[512,2048]{1,0:T(8,128)(2,1)}) %all-gather.2.cloned.1.call-update) | async-done | bytes 2097168 | tf_op jit(solution)/shard_map/all_gather | solution.py:685
  73.1 3.0 fusion.86
  79.4 2.2 fusion
  81.7 3.6 %divide_convert_fusion = bf16[16,256,512]{2,1,0:T(8,128)(2,1)} fusion(f32[16,256,512]{2,1,0:T(8,128)S(1)} %get-tuple-element.84, f32[16,256]{1,0:T(8,128)S(1)} %fusion, f32[16,256]{1,0:T(8,128)S(1)} %get-tuple-element.83, pred[256,512]{1,0:T(8,128)(4,1)S(1)} %fusion.52), kind=kLoop, calls=%fused_computation.3 | loop fusion | flops 10485760 | bytes 12746752 | tf_op jit(solution)/shard_map/convert_element_type | solution.py:704
  85.9 4.0 %convolution_convert_fusion.5 = bf16[16,64,256]{2,1,0:T(8,128)(2,1)S(1)} fusion(bf16[512,16,64]{0,2,1:T(8,128)(2,1)S(1)} %bitcast.168, bf16[16,256,512]{2,1,0:T(8,128)(2,1)} %divide_convert_fusion), kind=kOutput, calls=%fused_computation.39 | convolution fusion | flops 268697600 | bytes 5767168 | tf_op jit(solution)/shard_map/hqk,khd->qhd/dot_general | solution.py:705
  89.9 2.6 fusion.88
  97.7 2.6 fusion.9.r
  100.3 78.8 %experts.1 = (bf16[64,8,1024]{2,1,0:T(8,128)(2,1)}, bf16[64,8,1024]{2,1,0:T(8,128)(2,1)}, f32[512,4096]{1,0:T(8,128)}, f32[2048,1024]{1,0:T(8,128)}) custom-call(bf16[64,8,1024]{2,1,0:T(8,128)(2,1)} %fusion.15.x, bf16[64,8,1152]{2,1,0:T(8,128)(2,1)} %fusion.9.r, bf16[512,4096]{1,0:T(8,128)(2,1)} %bitcast.163, bf16[512,4096]{1,0:T(8,128)(2,1)} %get-tuple-element.47.w1_other, ...), custom_call_target="tpu_custom_call" | custom-call | tf_op jit(solution)/shard_map/experts/pallas_call | solution.py:561
  179.2 3.2 fusion.42
  182.4 1.8 fusion.60
  184.2 2.4 multiply_reduce_fusion.1
  187.1 3.2 fusion.20
  190.3 2.1 copy.58
  192.4 4.2 %convolution_convert_fusion.3 = bf16[16,64,512]{2,1,0:T(8,128)(2,1)} fusion(bf16[256,16,64]{0,2,1:T(8,128)(2,1)} %bitcast.176, bf16[16,256,512]{2,1,0:T(8,128)(2,1)} %divide_convert_fusion), kind=kOutput, calls=%fused_computation.25 | convolution fusion | flops 268959744 | bytes 5767168 | tf_op jit(solution)/shard_map/hqk,qhd->khd/dot_general | solution.py:776
  196.5 2.3 copy.60
  198.9 5.8 %multiply_reduce_fusion = (f32[16,256]{1,0:T(8,128)S(1)}, f32[16,256,512]{2,1,0:T(8,128)S(1)}) fusion(f32[16,256,512]{2,1,0:T(8,128)} %copy-done, f32[16,256]{1,0:T(8,128)S(1)} %log_add_fusion, pred[256,512]{1,0:T(8,128)(4,1)S(1)} %fusion.52, bf16[256,16,64]{0,2,1:T(8,128)(2,1)} %bitcast.177, bf16[512,16,64]{0,2,1:T(8,128)(2,1)S(1)} %bitcast.169), kind=kOutput, calls=%fused_computation.1 | convolution fusion | flops 278917120 | bytes 18513920 | tf_op jit(solution)/shard_map/qhd,khd->hqk/dot_general | solution.py:767
  204.6 4.7 %multiply_convert_fusion = bf16[16,256,512]{2,1,0:T(8,128)(2,1)S(1)} fusion(f32[16,256,512]{2,1,0:T(8,128)S(1)} %get-tuple-element.91, f32[16,256,512]{2,1,0:T(8,128)} %copy-done, f32[16,256]{1,0:T(8,128)S(1)} %get-tuple-element.90, f32[16,256]{1,0:T(8,128)S(1)} %log_add_fusion, pred[256,512]{1,0:T(8,128)(4,1)S(1)} %fusion.52), kind=kLoop, calls=%fused_computation | loop fusion | flops 12582912 | bytes 21135360 | tf_op jit(solution)/shard_map/convert_element_type | solution.py:769
  209.4 2.0 copy-done.1
  211.4 1.8 multiply_convert_fusion.1
  213.2 2.3 copy.59
  215.4 3.1 pad_maximum_fusion
  219.5 4.4 %fusion.23 = bf16[16,64,256]{2,1,0:T(8,128)(2,1)} fusion(bf16[512,16,64]{0,2,1:T(8,128)(2,1)S(1)} %bitcast.167, bf16[16,256,512]{2,1,0:T(8,128)(2,1)} %copy-done.1), kind=kOutput, calls=%fused_computation.41 | convolution fusion | flops 268959744 | bytes 5767168 | tf_op jit(solution)/shard_map/hqk,khd->qhd/dot_general | solution.py:771
  228.5 3.2 convolution_convert_fusion.2.rest_1_
  231.7 6.1 %fusion.34 = (f32[256]{0:T(256)S(1)}, f32[1024]{0:T(1024)S(1)}, f32[256]{0:T(256)S(1)}, f32[1024]{0:T(1024)S(1)}, f32[256,1024]{1,0:T(8,128)}) fusion(bf16[1,256,1024]{2,1,0:T(8,128)(2,1)S(1)} %copy-done.8, f32[1024]{0:T(1024)S(1)} %mul.185, f32[256]{0:T(256)S(1)} %add_rsqrt_fusion.1, f32[256]{0:T(256)S(1)} %broadcast_multiply_fusion.5, ...), kind=kOutput, calls=%fused_computation.53 | convolution fusion | flops 1616377344 | bytes 9453568 | tf_op jit(solution)/shard_map/dot_general | solution.py:630
  239.1 2.8 fusion.38
  243.3 2.4 pad_maximum_fusion.2.rest_2_
  245.6 5.7 %convolution_convert_fusion.rest_0_ = bf16[2,4,4,4,8,3072]{5,4,3,2,1,0:T(8,128)(2,1)} fusion(bf16[2,4,4,4,8,256]{5,4,3,2,1,0:T(8,128)(2,1)S(1)} %bitcast.180, bf16[256,2048]{1,0:T(8,128)(2,1)} %reduce-scatter.2.cloned.1.call-done, bf16[256,1024]{1,0:T(8,128)(2,1)S(1)} %copy.61), kind=kOutput, calls=%fused_computation.7 | convolution fusion | flops 1616904192 | bytes 8388608 | tf_op jit(solution)/shard_map/dot_general | solution.py:636
  251.3 51.4 %reduce_layer.1 = (f32[8,3072]{1,0:T(8,128)}, f32[8,1024]{1,0:T(8,128)}, f32[8,256]{1,0:T(8,128)}) custom-call(bf16[2,4,4,4,8,3072]{5,4,3,2,1,0:T(8,128)(2,1)} %convolution_convert_fusion.rest_0_, bf16[2,4,4,4,8,1024]{5,4,3,2,1,0:T(8,128)(2,1)} %convolution_convert_fusion.2.rest_1_, f32[2,4,4,4,8,256]{5,4,3,2,1,0:T(8,128)} %pad_maximum_fusion.2.rest_2_), custom_call_target="tpu_custom_call" | custom-call | tf_op jit(solution)/shard_map/reduce_layer/pallas_call | solution.py:317
  310.9 7.8 %copy.82 = f32[1,512,4096]{2,1,0:T(8,128)} copy(f32[1,512,4096]{2,1,0:T(8,128)} %bitcast.171) | data formatting | bytes 16777216
  318.7 8.4 %copy.83 = f32[1,2048,1024]{2,1,0:T(8,128)} copy(f32[1,2048,1024]{2,1,0:T(8,128)} %bitcast.170) | data formatting | bytes 16777216
  (117 shorter events, 33.7 us)
Async XLA Ops:
  7.2 48.7 %copy-start.8 = (bf16[1,256,1024]{2,1,0:T(8,128)(2,1)S(1)}, bf16[1,256,1024]{2,1,0:T(8,128)(2,1)}, u32[]{:S(2)}) copy-start(bf16[1,256,1024]{2,1,0:T(8,128)(2,1)} %param.17) | copy-start | bytes 1572868
  7.2 65.9 %all-gather.2.cloned.1.call-start = ((), (), s32[]{:S(2)}) async-start(), calls=%async_computation.1 | async-start | bytes 3145728 | tf_op jit(solution)/shard_map/all_gather | solution.py:685
  55.9 6.7 %copy-start.17 = (s32[1,256,1]{1,2,0:T(1,128)S(1)}, s32[1,256,1]{1,2,0:T(1,128)}, u32[]{:S(2)}) copy-start(s32[1,256,1]{1,2,0:T(1,128)} %param.20) | copy-start | bytes 3076
  61.7 170.0 %reduce-scatter.2.cloned.1.call-start = ((), (), s32[]{:S(2)}) async-start(), calls=%async_computation.2 | async-start | bytes 3145728 | tf_op jit(solution)/shard_map/reduce_scatter | solution.py:780
  63.9 15.6 %copy-start.11 = (bf16[256,1024]{0,1:T(8,128)(2,1)}, bf16[256,1024]{0,1:T(8,128)(2,1)S(1)}, u32[]{:S(2)}) copy-start(bf16[256,1024]{0,1:T(8,128)(2,1)S(1)} %copy.53) | copy-start | bytes 1572868
  77.7 4.0 %copy-start.4 = (bf16[512,1024]{0,1:T(8,128)(2,1)}, bf16[512,1024]{0,1:T(8,128)(2,1)S(1)}, u32[]{:S(2)}) copy-start(bf16[512,1024]{0,1:T(8,128)(2,1)S(1)} %copy.54) | copy-start | bytes 3145732
  79.4 5.9 %copy-start = (f32[16,256,512]{2,1,0:T(8,128)}, f32[16,256,512]{2,1,0:T(8,128)S(1)}, u32[]{:S(2)}) copy-start(f32[16,256,512]{2,1,0:T(8,128)S(1)} %get-tuple-element.84) | copy-start | bytes 25165828
  81.7 3.6 %copy-start.13 = (bf16[512,1024]{1,0:T(8,128)(2,1)S(1)}, bf16[512,1024]{1,0:T(8,128)(2,1)}, u32[]{:S(2)}) copy-start(bf16[512,1024]{1,0:T(8,128)(2,1)} %get-tuple-element.72) | copy-start | bytes 3145732
  85.9 8.7 %copy-start.6 = (bf16[512,1024]{0,1:T(8,128)(2,1)}, bf16[512,1024]{0,1:T(8,128)(2,1)S(1)}, u32[]{:S(2)}) copy-start(bf16[512,1024]{0,1:T(8,128)(2,1)S(1)} %copy.52) | copy-start | bytes 3145732
  85.9 7.6 %copy-start.14 = (bf16[1,256,1024]{2,1,0:T(8,128)(2,1)S(1)}, bf16[1,256,1024]{2,1,0:T(8,128)(2,1)}, u32[]{:S(2)}) copy-start(bf16[1,256,1024]{2,1,0:T(8,128)(2,1)} %param.18) | copy-start | bytes 1572868
  89.9 2.9 copy-start.10
  92.5 1.0 copy-start.2
  94.5 1.7 copy-start.9
  179.2 7.4 %copy-start.3 = (f32[256,1024]{1,0:T(8,128)S(1)}, f32[256,1024]{1,0:T(8,128)}, u32[]{:S(2)}) copy-start(f32[256,1024]{1,0:T(8,128)} %copy-done.2) | copy-start | bytes 3145732
  179.2 7.4 %copy-start.15 = (bf16[1,256,1024]{2,1,0:T(8,128)(2,1)S(1)}, bf16[1,256,1024]{2,1,0:T(8,128)(2,1)}, u32[]{:S(2)}) copy-start(bf16[1,256,1024]{2,1,0:T(8,128)(2,1)} %param.18) | copy-start | bytes 1572868
  182.4 4.7 %copy-start.16 = (bf16[256,1024]{1,0:T(8,128)(2,1)}, bf16[256,1024]{1,0:T(8,128)(2,1)S(1)}, u32[]{:S(2)}) copy-start(bf16[256,1024]{1,0:T(8,128)(2,1)S(1)} %get-tuple-element.70) | copy-start | bytes 1572868
  187.1 11.8 %copy-start.7 = (bf16[512,1024]{0,1:T(8,128)(2,1)S(1)}, bf16[512,1024]{0,1:T(8,128)(2,1)}, u32[]{:S(2)}) copy-start(bf16[512,1024]{0,1:T(8,128)(2,1)} %copy-done.6) | copy-start | bytes 3145732
  204.6 6.7 %copy-start.12 = (bf16[256,1024]{0,1:T(8,128)(2,1)S(1)}, bf16[256,1024]{0,1:T(8,128)(2,1)}, u32[]{:S(2)}) copy-start(bf16[256,1024]{0,1:T(8,128)(2,1)} %copy-done.11) | copy-start | bytes 1572868
  209.3 2.0 copy-start.1
  211.4 8.1 %copy-start.5 = (bf16[512,1024]{0,1:T(8,128)(2,1)S(1)}, bf16[512,1024]{0,1:T(8,128)(2,1)}, u32[]{:S(2)}) copy-start(bf16[512,1024]{0,1:T(8,128)(2,1)} %copy-done.4) | copy-start | bytes 3145732
Sparse Core Ops, SparseCore 0:
  61.8 11.2 all-gather.1
  218.7 11.6 reduce-scatter.1
where the time goes:
time: 336 us; the launch traced here: 335 us
  Pallas kernels  172 us (51%)
  matrix products  62 us (18%)
  local copies, waits for them, and re-layouts  48 us (14%)
  other arithmetic  25.7 us (8%)
  between operations  17.7 us (5%)
  waiting for transfers between devices  8.97 us (3%)
    pallas_call x1, Pallas kernels, experts(): pl.pallas_call(expert_kernel, out_shape=(jax.ShapeDtypeStruct((64, 8, WID...  78.8 us
    pallas_call x1, Pallas kernels, reduce_layer(): pl.pallas_call(reduce_kernel, out_shape=tuple((jax.ShapeDtypeStruct((8, c...  51.4 us
    pallas_call x1, Pallas kernels, gather_layer(): pl.pallas_call(gather_kernel, out_shape=(jax.ShapeDtypeStruct((2, SIDE, S...  42.3 us
    unnamed x41, local copies, waits for them, and re-layouts  22.1 us
    dot_general x4, matrix products, transposed_times(): lax.dot_general(left_mat, right_mat, (((0,), (0,)), ((), ())), preferred_...  14.4 us
    dot_general x2, matrix products, times_transposed(): lax.dot_general(left_mat, right_mat, (((1,), (1,)), ((), ())), preferred_...  9.36 us
    all_gather x1, waiting for transfers between devices, per_device(): lax.all_gather(query_key_value_rows[:, width:], 'dp', axis=0, tiled=True)  8.94 us
  transfers between devices with their start and end apart: 2, of which 1 were waited for; matrix products, arithmetic and copies ran while one was open for 4% of the time, Pallas kernels for 0%

commit v1 on v0

--- a/solution.py
+++ b/solution.py
@@ -147,14 +147,10 @@
 RS_PIECES = tuple(h0 + h1 for h0, h1 in RS_HALVES)
 
 
-def reduce_kernel(*rest):
-    source, outs, rest = rest[:3], rest[3:6], rest[6:]
+def reduce_all(pos, core, source, outs, rest):
     refs, (send_sems, recv_sems) = list(rest[:-2]), rest[-2:]
     take = iter(refs)
-    pos = coords()
-    core = lax.axis_index("dp")
     partner = {"dp": 1 - core}
-    greet(pos, core)
     send = Sender(send_sems, recv_sems)
     landed = (next(take), next(take), next(take))
 
@@ -294,8 +290,7 @@
         copy.wait_send()
 
 
-def reduce_layer(*parts):
-    parts = [p.reshape(2, SIDE, SIDE, SIDE, 8, c).astype(k) for p, c, k in zip(parts, RS_COLS, RS_KINDS)]
+def reduce_scratch():
     scratch = [pltpu.VMEM((SIDE, SIDE, SIDE, 8, c), k) for c, k in zip(RS_COLS, RS_KINDS)]
     copies = sum(len(p) for p in RS_PIECES)
     for stage in range(3):
@@ -313,18 +308,7 @@
             for piece in range(3):
                 for kind, c0, c1 in RS_PIECES[piece]:
                     scratch += [pltpu.VMEM(lead + (8, c1 - c0), jnp.float32)]
-    vmem = pl.BlockSpec(memory_space=pltpu.VMEM)
-    return pl.pallas_call(
-        reduce_kernel,
-        out_shape=tuple(jax.ShapeDtypeStruct((8, c), jnp.float32) for c in RS_COLS),
-        in_specs=[vmem] * 3,
-        out_specs=(vmem,) * 3,
-        scratch_shapes=scratch + [pltpu.SemaphoreType.DMA((copies,)), pltpu.SemaphoreType.DMA((copies,))],
-        compiler_params=pltpu.CompilerParams(
-            collective_id=1, has_side_effects=True, vmem_limit_bytes=60 * 1024 * 1024
-        ),
-        name="reduce_layer",
-    )(*parts)
+    return scratch, copies
 
 
 ROWS = 512
@@ -603,39 +587,522 @@
     )(x, r, w1_own, w1_other, w2_own, w2_other)
 
 
+GROUP = 256
 HEADS = 16
-
-
-def layer_norm(values, scale_vec, offset):
-    center = jnp.mean(values, -1, keepdims=True)
-    centred = values - center
-    spread = jnp.mean(centred * centred, -1, keepdims=True)
-    inverse = lax.rsqrt(spread + 1e-05)
-    normed = centred * inverse
-    return (normed * scale_vec + offset, normed, inverse)
-
-
-def norm_back(upstream, normed, inverse, scale_vec):
-    scaled = upstream * scale_vec
-    average = jnp.mean(scaled, -1, keepdims=True)
-    project = jnp.mean(scaled * normed, -1, keepdims=True)
-    return (
-        inverse * (scaled - average - normed * project),
-        jnp.sum(upstream * normed, 0),
-        jnp.sum(upstream, 0),
+PAIRS = HEADS // 2
+SLOTS = 512
+BLOCK = 32
+EPS = 1e-05
+MASKED = -1e30
+
+
+def lanes(start, size):
+    return pl.ds(pl.multiple_of(start, 128), size)
+
+
+def row_blocks(body, size=BLOCK):
+    @pl.loop(0, GROUP // size)
+    def _(i):
+        body(pl.ds(pl.multiple_of(i * size, size), size), i * size)
+
+
+def normed(v):
+    centred = v - jnp.mean(v, -1, keepdims=True)
+    inverse = lax.rsqrt(jnp.mean(centred * centred, -1, keepdims=True) + EPS)
+    return centred * inverse, inverse
+
+
+def lane_ids(rows, columns):
+    return lax.broadcasted_iota(jnp.int32, (rows, columns), 1)
+
+
+def row_ids(rows, columns):
+    return lax.broadcasted_iota(jnp.int32, (rows, columns), 0)
+
+
+def allowed_keys(core, length):
+    query, key = row_ids(GROUP, GROUP), lane_ids(GROUP, GROUP)
+    own = (key <= query) & (key + core * GROUP < length)
+    other = (key < length) & (core == 1)
+    return own, other
+
+
+def head_scores(q, k_own, k_other, own, other):
+    s_own = jnp.where(own, dot_nt(q, k_own) * 0.125, MASKED)
+    s_other = jnp.where(other, dot_nt(q, k_other) * 0.125, MASKED)
+    return s_own, s_other
+
+
+def forward_kernel(
+    tokens, teacher, routes, lengths, layer,
+    x_out, parting_out, qkv_out, kv_other_out, attended_out, norm1_out, norm2_out, residual_out,
+    lse_out, probs_out, placing_out, vectors_out,
+    weights, norm1, qkv, kv_other, attended, norm2, residual, lse, probs, placing, vectors, parted, packed_x, packed_r,
+    load_sems, out_sems, kv_sems,
+):
+    core = lax.axis_index("dp")
+    length = lengths[0]
+    spans = ((4096, 128), (1024, 1024), (2048, 1024), (0, 1024), (3072, 1024))
+    loads = [
+        pltpu.make_async_copy(layer.at[:, pl.ds(c, n)], weights.at[:, pl.ds(c, n)], load_sems.at[i])
+        for i, (c, n) in enumerate(spans)
+    ]
+    for load in loads:
+        load.start()
+    outs = []
+
+    def save(src, dst):
+        copy = pltpu.make_async_copy(src, dst, out_sems.at[len(outs)])
+        copy.start()
+        outs.append(copy)
+
+    barrier = pltpu.get_barrier_semaphore()
+    pl.semaphore_signal(barrier, inc=1, device_id={"dp": 1 - core}, device_id_type=MESH)
+
+    loads[0].wait()
+    for g in range(16):
+        part = weights[pl.ds(g * 64, 64), pl.ds(4096, 128)].astype(jnp.float32)
+        part = jnp.sum(part.reshape(8, 8, 128), 0)
+        vectors[:, g * 64 : (g + 1) * 64] = part[:, 64:]
+    save(vectors, vectors_out)
+
+    def first_norm(rows, _):
+        n, _ = normed(tokens[rows, :].astype(jnp.float32))
+        norm1[rows, :] = (n * vectors[0:1, :] + vectors[1:2, :]).astype(jnp.bfloat16)
+
+    row_blocks(first_norm)
+    save(norm1, norm1_out)
+
+    def project(block):
+        @pl.loop(0, 2)
+        def _(i):
+            cols = lanes(block * 1024 + i * 512, 512)
+            qkv[:, cols] = dot_nn(norm1[...], weights[:, cols]).astype(jnp.bfloat16)
+
+    loads[1].wait()
+    project(1)
+    loads[2].wait()
+    project(2)
+    pl.semaphore_wait(barrier, 1)
+    passed = pltpu.make_async_remote_copy(
+        src_ref=qkv.at[:, pl.ds(1024, 2048)],
+        dst_ref=kv_other,
+        send_sem=kv_sems.at[0],
+        recv_sem=kv_sems.at[1],
+        device_id={"dp": 1 - core},
+        device_id_type=MESH,
     )
-
-
-def times_transposed(left_mat, right_mat):
-    return lax.dot_general(
-        left_mat, right_mat, (((1,), (1,)), ((), ())), preferred_element_type=jnp.float32
+    passed.start()
+    loads[3].wait()
+    project(0)
+    save(qkv, qkv_out)
+    passed.wait_recv()
+    save(kv_other, kv_other_out)
+
+    own, other = allowed_keys(core, length)
+    lse[...] = jnp.zeros_like(lse)
+
+    @pl.loop(0, PAIRS)
+    def _(pair):
+        q = qkv[:, lanes(pair * 128, 128)]
+        k_own, v_own = qkv[:, lanes(1024 + pair * 128, 128)], qkv[:, lanes(2048 + pair * 128, 128)]
+        k_other, v_other = kv_other[:, lanes(pair * 128, 128)], kv_other[:, lanes(1024 + pair * 128, 128)]
+        left = lane_ids(GROUP, 128) < 64
+        results = []
+        for h in range(2):
+            qh = jnp.where(left == (h == 0), q, jnp.zeros_like(q))
+            s_own, s_other = head_scores(qh, k_own, k_other, own, other)
+            top = jnp.max(jnp.maximum(s_own, s_other), -1, keepdims=True)
+            e_own, e_other = jnp.exp(s_own - top), jnp.exp(s_other - top)
+            total = jnp.sum(e_own + e_other, -1, keepdims=True)
+            scale = 1.0 / total
+            p_own, p_other = (e_own * scale).astype(jnp.bfloat16), (e_other * scale).astype(jnp.bfloat16)
+            results.append(dot_nn(p_own, v_own) + dot_nn(p_other, v_other))
+            lse[...] = jnp.where(lane_ids(GROUP, 128) == pair * 2 + h, top + jnp.log(total), lse[...])
+        attended[:, lanes(pair * 128, 128)] = jnp.where(left, results[0], results[1]).astype(jnp.bfloat16)
+
+    save(attended, attended_out)
+    save(lse, lse_out)
+    loads[4].wait()
+
+    @pl.loop(0, 2)
+    def _(i):
+        cols = lanes(i * 512, 512)
+        branch = dot_nn(attended[...], weights[:, lanes(3072 + i * 512, 512)])
+        residual[:, cols] = tokens[:, cols].astype(jnp.float32) + branch
+
+    save(residual, residual_out)
+
+    def second_norm(rows, _):
+        n, _ = normed(residual[rows, :])
+        norm2[rows, :] = (n * vectors[2:3, :] + vectors[3:4, :]).astype(jnp.bfloat16)
+        parted[rows, :WIDTH] = (residual[rows, :] - teacher[rows, :].astype(jnp.float32)).astype(jnp.bfloat16)
+
+    row_blocks(second_norm)
+    save(norm2, norm2_out)
+    logits = dot_nn(norm2[...], weights[:, pl.ds(4096, 128)])
+    ids = lane_ids(GROUP, 128)
+    logits = jnp.where(ids < 64, logits, MASKED)
+    e = jnp.exp(logits - jnp.max(logits, -1, keepdims=True))
+    share = e / jnp.sum(e, -1, keepdims=True)
+    probs[...] = share
+    save(probs, probs_out)
+    chosen = ids == routes[...]
+    gate = jnp.sum(jnp.where(chosen, share, 0.0), -1, keepdims=True)
+    low_gate = gate.astype(jnp.bfloat16).astype(jnp.float32)
+    valid = (row_ids(GROUP, 128) + core * GROUP < length).astype(jnp.float32)
+    extras = jnp.where(ids == 0, low_gate, jnp.where(ids == 1, gate - low_gate, jnp.where(ids == 2, valid, 0.0)))
+    parted[:, WIDTH:] = extras.astype(jnp.bfloat16)
+    marks = chosen.astype(jnp.float32).astype(jnp.bfloat16)
+    before = (lane_ids(GROUP, GROUP) < row_ids(GROUP, GROUP)).astype(jnp.float32).astype(jnp.bfloat16)
+    rank = jnp.sum(jnp.where(chosen, dot_nn(before, marks), 0.0), -1, keepdims=True)
+    slot = routes[...].astype(jnp.float32) * 8.0 + rank
+    placing[...] = (lane_ids(GROUP, SLOTS).astype(jnp.float32) == slot).astype(jnp.float32).astype(jnp.bfloat16)
+    save(placing, placing_out)
+    for half in range(2):
+        spread = placing[:, half * 256 : (half + 1) * 256].astype(jnp.float32).T.astype(jnp.bfloat16)
+        sent = dot_nn(spread, norm2[...])
+        packed_x[half * 32 : (half + 1) * 32] = sent.reshape(32, 8, WIDTH).astype(jnp.bfloat16)
+        sent = dot_nn(spread, parted[...])
+        packed_r[half * 32 : (half + 1) * 32] = sent.reshape(32, 8, WIDTH + EXTRA).astype(jnp.bfloat16)
+    save(packed_x, x_out)
+    save(packed_r, parting_out)
+    passed.wait_send()
+    for copy in outs:
+        copy.wait()
+
+
+def forward(tokens, teacher, routes, lengths, layer):
+    low, wide = jnp.bfloat16, jnp.float32
+    anywhere = pl.BlockSpec(memory_space=pl.ANY)
+    vmem = pl.BlockSpec(memory_space=pltpu.VMEM)
+    saved = [
+        ((64, 8, WIDTH), low),
+        ((64, 8, WIDTH + EXTRA), low),
+        ((GROUP, 3 * WIDTH), low),
+        ((GROUP, 2 * WIDTH), low),
+        ((GROUP, WIDTH), low),
+        ((GROUP, WIDTH), low),
+        ((GROUP, WIDTH), low),
+        ((GROUP, WIDTH), wide),
+        ((GROUP, 128), wide),
+        ((GROUP, 128), wide),
+        ((GROUP, SLOTS), low),
+        ((8, WIDTH), wide),
+    ]
+    return pl.pallas_call(
+        forward_kernel,
+        out_shape=tuple(jax.ShapeDtypeStruct(s, t) for s, t in saved),
+        in_specs=[vmem, vmem, vmem, pl.BlockSpec(memory_space=pltpu.SMEM), anywhere],
+        out_specs=(anywhere,) * len(saved),
+        scratch_shapes=[
+            pltpu.VMEM((WIDTH, AG_COLS), low),
+            pltpu.VMEM((GROUP, WIDTH), low),
+            pltpu.VMEM((GROUP, 3 * WIDTH), low),
+            pltpu.VMEM((GROUP, 2 * WIDTH), low),
+            pltpu.VMEM((GROUP, WIDTH), low),
+            pltpu.VMEM((GROUP, WIDTH), low),
+            pltpu.VMEM((GROUP, WIDTH), wide),
+            pltpu.VMEM((GROUP, 128), wide),
+            pltpu.VMEM((GROUP, 128), wide),
+            pltpu.VMEM((GROUP, SLOTS), low),
+            pltpu.VMEM((8, WIDTH), wide),
+            pltpu.VMEM((GROUP, WIDTH + EXTRA), low),
+            pltpu.VMEM((64, 8, WIDTH), low),
+            pltpu.VMEM((64, 8, WIDTH + EXTRA), low),
+            pltpu.SemaphoreType.DMA((5,)),
+            pltpu.SemaphoreType.DMA((len(saved),)),
+            pltpu.SemaphoreType.DMA((2,)),
+        ],
+        compiler_params=pltpu.CompilerParams(
+            collective_id=3, has_side_effects=True, vmem_limit_bytes=56 * 1024 * 1024
+        ),
+        name="forward",
+    )(tokens, teacher, routes, lengths, layer)
+
+
+def backward_kernel(
+    y_back, d_back, teacher, routes, lengths, layer, qkv, kv_other, attended, norm2, residual, lse, probs,
+    placing, vectors, g1, g2,
+    mixed_out, d_resid, dq, dkv_own, dkv_other, grad_out, grad_router, norm_grads, g1_out, g2_out,
+    w_out, w_router, eo, dn, sums, d_branch, d_attended, attended_t, delta, logit_parts,
+    held1, held2, pass_sems, load_sems,
+):
+    core = lax.axis_index("dp")
+    length = lengths[0]
+    passing = [
+        pltpu.make_async_copy(g1, held1, pass_sems.at[0]),
+        pltpu.make_async_copy(g2, held2, pass_sems.at[1]),
+    ]
+    passed_on = [
+        pltpu.make_async_copy(held1, g1_out, pass_sems.at[2]),
+        pltpu.make_async_copy(held2, g2_out, pass_sems.at[3]),
+    ]
+    loads = [
+        pltpu.make_async_copy(layer.at[:, pl.ds(3072, 1024)], w_out, load_sems.at[0]),
+        pltpu.make_async_copy(layer.at[:, pl.ds(4096, 128)], w_router, load_sems.at[1]),
+    ]
+    for copy in loads + passing:
+        copy.start()
+    rows_back = y_back[...].astype(jnp.float32).reshape(SLOTS, WIDTH).astype(jnp.bfloat16)
+    eo[...] = dot_nn(placing[...], rows_back)
+    rows_back = d_back[...].astype(jnp.float32).reshape(SLOTS, WIDTH).astype(jnp.bfloat16)
+    dn[...] = dot_nn(placing[...], rows_back)
+    sums[...] = jnp.zeros_like(sums)
+
+    def loss(rows, first):
+        ids = lane_ids(BLOCK, 128)
+        share = probs[rows, :]
+        chosen = ids == routes[rows, :]
+        gate = jnp.sum(jnp.where(chosen, share, 0.0), -1, keepdims=True)
+        out = eo[rows, :]
+        mixed = (residual[rows, :] + gate * out).astype(jnp.bfloat16)
+        mixed_out[rows, :] = mixed
+        valid = (row_ids(BLOCK, 1) + first + core * GROUP < length).astype(jnp.float32)
+        d_mixed = valid * (mixed.astype(jnp.float32) - teacher[rows, :].astype(jnp.float32))
+        d_resid[rows, :] = d_mixed
+        d_gate = jnp.sum(d_mixed * out, -1, keepdims=True)
+        d_logits = d_gate * gate * (chosen.astype(jnp.float32) - share)
+        high = d_logits.astype(jnp.bfloat16)
+        logit_parts[rows, :128] = high
+        logit_parts[rows, 128:] = (d_logits - high.astype(jnp.float32)).astype(jnp.bfloat16)
+        square = jnp.sum((d_mixed * d_mixed).reshape(BLOCK // 8, 8, WIDTH), 0)
+        sums[0] += square
+
+    row_blocks(loss)
+    loads[0].wait()
+    loads[1].wait()
+    dn[...] += dot_nt(logit_parts[:, :128], w_router[...]) + dot_nt(logit_parts[:, 128:], w_router[...])
+    both = dot_tn(norm2[...], logit_parts[...])
+    grad_router[...] = both[:, :128] + both[:, 128:]
+
+    def norm_back(rows, _):
+        n, inverse = normed(residual[rows, :])
+        u = dn[rows, :]
+        scaled = u * vectors[2:3, :]
+        average = jnp.mean(scaled, -1, keepdims=True)
+        project = jnp.mean(scaled * n, -1, keepdims=True)
+        d = d_resid[rows, :] + inverse * (scaled - average - n * project)
+        d_resid[rows, :] = d
+        d_branch[rows, :] = d.astype(jnp.bfloat16)
+        sums[1] += jnp.sum((u * n).reshape(BLOCK // 8, 8, WIDTH), 0)
+        sums[2] += jnp.sum(u.reshape(BLOCK // 8, 8, WIDTH), 0)
+
+    row_blocks(norm_back)
+    valid_all = jnp.clip(length - core * GROUP, 0, GROUP).astype(jnp.float32)
+    ids = row_ids(8, WIDTH)
+    square = jnp.sum(sums[0])
+    norm_grads[...] = jnp.where(
+        ids == 2,
+        jnp.sum(sums[1], 0, keepdims=True),
+        jnp.where(
+            ids == 3,
+            jnp.sum(sums[2], 0, keepdims=True),
+            jnp.where(ids == 4, square, jnp.where(ids == 5, valid_all, 0.0)),
+        ),
     )
-
-
-def transposed_times(left_mat, right_mat):
-    return lax.dot_general(
-        left_mat, right_mat, (((0,), (0,)), ((), ())), preferred_element_type=jnp.float32
+    attended_t[...] = attended[...].astype(jnp.float32).T.astype(jnp.bfloat16)
+
+    @pl.loop(0, 2)
+    def _(i):
+        cols = lanes(i * 512, 512)
+        grad_out[:, cols] = dot_nn(attended_t[...], d_branch[:, cols]).astype(jnp.bfloat16)
+        rows = pl.ds(pl.multiple_of(i * 512, 512), 512)
+        d_attended[:, cols] = dot_nt(d_branch[...], w_out[rows, :]).astype(jnp.bfloat16)
+
+    own, other = allowed_keys(core, length)
+    for copy, onward in zip(passing, passed_on):
+        copy.wait()
+        onward.start()
+
+    @pl.loop(0, PAIRS)
+    def _(pair):
+        q, do = qkv[:, lanes(pair * 128, 128)], d_attended[:, lanes(pair * 128, 128)]
+        k_own, v_own = qkv[:, lanes(1024 + pair * 128, 128)], qkv[:, lanes(2048 + pair * 128, 128)]
+        k_other, v_other = kv_other[:, lanes(pair * 128, 128)], kv_other[:, lanes(1024 + pair * 128, 128)]
+        left = lane_ids(GROUP, 128) < 64
+        zero = jnp.zeros_like(q)
+        parts = []
+        for h in range(2):
+            qh = jnp.where(left == (h == 0), q, zero)
+            doh = jnp.where(left == (h == 0), do, zero)
+            s_own, s_other = head_scores(qh, k_own, k_other, own, other)
+            log_total = jnp.sum(jnp.where(lane_ids(GROUP, 128) == pair * 2 + h, lse[...], 0.0), -1, keepdims=True)
+            p_own, p_other = jnp.exp(s_own - log_total), jnp.exp(s_other - log_total)
+            dp_own, dp_other = dot_nt(doh, v_own), dot_nt(doh, v_other)
+            total = jnp.sum(p_own * dp_own + p_other * dp_other, -1, keepdims=True)
+            ds_own = (p_own * (dp_own - total)).astype(jnp.bfloat16)
+            ds_other = (p_other * (dp_other - total)).astype(jnp.bfloat16)
+            p_own, p_other = p_own.astype(jnp.bfloat16), p_other.astype(jnp.bfloat16)
+            parts.append((
+                dot_nn(ds_own, k_own) + dot_nn(ds_other, k_other),
+                dot_tn(ds_own, q),
+                dot_tn(ds_other, q),
+                dot_tn(p_own, do),
+                dot_tn(p_other, do),
+            ))
+        d_q, d_k, d_k_other, d_v, d_v_other = [jnp.where(left, a, b) for a, b in zip(*parts)]
+        dq[:, lanes(pair * 128, 128)] = (d_q * 0.125).astype(jnp.bfloat16)
+        dkv_own[:, lanes(pair * 128, 128)] = d_k * 0.125
+        dkv_own[:, lanes(1024 + pair * 128, 128)] = d_v
+        dkv_other[:, lanes(pair * 128, 128)] = (d_k_other * 0.125).astype(jnp.bfloat16)
+        dkv_other[:, lanes(1024 + pair * 128, 128)] = d_v_other.astype(jnp.bfloat16)
+
+    for onward in passed_on:
+        onward.wait()
+
+
+def backward(y_back, d_back, teacher, routes, lengths, layer, qkv, kv_other, attended, norm2, residual, lse, probs,
+             placing, vectors, g1, g2):
+    low, wide = jnp.bfloat16, jnp.float32
+    anywhere = pl.BlockSpec(memory_space=pl.ANY)
+    vmem = pl.BlockSpec(memory_space=pltpu.VMEM)
+    made = [
+        ((GROUP, WIDTH), low),
+        ((GROUP, WIDTH), wide),
+        ((GROUP, WIDTH), low),
+        ((GROUP, 2 * WIDTH), wide),
+        ((GROUP, 2 * WIDTH), low),
+        ((WIDTH, WIDTH), low),
+        ((WIDTH, 128), wide),
+        ((8, WIDTH), wide),
+        (g1.shape, wide),
+        (g2.shape, wide),
+    ]
+    return pl.pallas_call(
+        backward_kernel,
+        out_shape=tuple(jax.ShapeDtypeStruct(s, t) for s, t in made),
+        in_specs=[vmem, vmem, vmem, vmem, pl.BlockSpec(memory_space=pltpu.SMEM), anywhere] + [vmem] * 9 + [anywhere] * 2,
+        out_specs=(vmem,) * 8 + (anywhere,) * 2,
+        scratch_shapes=[
+            pltpu.VMEM((WIDTH, WIDTH), low),
+            pltpu.VMEM((WIDTH, 128), low),
+            pltpu.VMEM((GROUP, WIDTH), wide),
+            pltpu.VMEM((GROUP, WIDTH), wide),
+            pltpu.VMEM((3, 8, WIDTH), wide),
+            pltpu.VMEM((GROUP, WIDTH), low),
+            pltpu.VMEM((GROUP, WIDTH), low),
+            pltpu.VMEM((WIDTH, GROUP), low),
+            pltpu.VMEM((GROUP, 128), wide),
+            pltpu.VMEM((GROUP, 256), low),
+            pltpu.VMEM(g1.shape, wide),
+            pltpu.VMEM(g2.shape, wide),
+            pltpu.SemaphoreType.DMA((4,)),
+            pltpu.SemaphoreType.DMA((2,)),
+        ],
+        compiler_params=pltpu.CompilerParams(vmem_limit_bytes=56 * 1024 * 1024),
+        name="backward",
+    )(y_back, d_back, teacher, routes, lengths, layer, qkv, kv_other, attended, norm2, residual, lse, probs,
+      placing, vectors, g1, g2)
+
+
+def finish_kernel(
+    tokens, norm1, vectors, d_resid, dq, dkv_own, dkv_other, grad_out, grad_router, norm_grads, layer,
+    sum_qkv, sum_out, sum_side, grad_tokens,
+    weights, norm1_t, landed_kv, dqkv, acc, sums, grad_qkv, side, load_sem, kv_sems, *rest,
+):
+    pos = coords()
+    core = lax.axis_index("dp")
+    load = pltpu.make_async_copy(layer.at[:, pl.ds(0, 3072)], weights, load_sem)
+    load.start()
+    greet(pos, core)
+    passed = pltpu.make_async_remote_copy(
+        src_ref=dkv_other,
+        dst_ref=landed_kv,
+        send_sem=kv_sems.at[0],
+        recv_sem=kv_sems.at[1],
+        device_id={"dp": 1 - core},
+        device_id_type=MESH,
     )
+    passed.start()
+    norm1_t[...] = norm1[...].astype(jnp.float32).T.astype(jnp.bfloat16)
+    acc[...] = jnp.zeros_like(acc)
+    dqkv[:, pl.ds(0, WIDTH)] = dq[...]
+
+    def project(first):
+        @pl.loop(0, 2)
+        def _(i):
+            cols = lanes(first + i * 512, 512)
+            d = dqkv[:, cols]
+            for half in range(2):
+                part = dot_nn(norm1_t[half * 512 : (half + 1) * 512, :], d)
+                grad_qkv[half, :, :, :, :, cols] = part.reshape(SIDE, SIDE, SIDE, 8, 512).astype(jnp.bfloat16)
+            acc[...] += dot_nt(d, weights[:, cols])
+
+    load.wait()
+    project(0)
+    passed.wait_recv()
+
+    def join(rows, _):
+        dqkv[rows, pl.ds(WIDTH, 2 * WIDTH)] = (
+            dkv_own[rows, :] + landed_kv[rows, :].astype(jnp.float32)
+        ).astype(jnp.bfloat16)
+
+    row_blocks(join)
+    project(1024)
+    project(2048)
+    sums[...] = jnp.zeros_like(sums)
+
+    def norm_back(rows, _):
+        n, inverse = normed(tokens[rows, :].astype(jnp.float32))
+        u = acc[rows, :]
+        scaled = u * vectors[0:1, :]
+        average = jnp.mean(scaled, -1, keepdims=True)
+        project = jnp.mean(scaled * n, -1, keepdims=True)
+        grad_tokens[rows, :] = d_resid[rows, :] + inverse * (scaled - average - n * project)
+        sums[0] += jnp.sum((u * n).reshape(BLOCK // 8, 8, WIDTH), 0)
+        sums[1] += jnp.sum(u.reshape(BLOCK // 8, 8, WIDTH), 0)
+
+    row_blocks(norm_back)
+    ids = row_ids(8, WIDTH)
+    vector_grads = jnp.where(
+        ids == 0,
+        jnp.sum(sums[0], 0, keepdims=True),
+        jnp.where(ids == 1, jnp.sum(sums[1], 0, keepdims=True), norm_grads[...]),
+    )
+    for half in range(2):
+        rows = grad_router[half * 512 : (half + 1) * 512, :]
+        side[half, :, :, :, :, pl.ds(0, 128)] = rows.reshape(SIDE, SIDE, SIDE, 8, 128)
+        for x in range(SIDE):
+            block = vector_grads[:, (half * SIDE + x) * 128 : (half * SIDE + x + 1) * 128]
+            side[half, x, :, :, :, pl.ds(128, 128)] = jnp.broadcast_to(block[None, None], (SIDE, SIDE, 8, 128))
+    reduce_all(pos, core, (grad_qkv, grad_out, side), (sum_qkv, sum_out, sum_side), rest)
+    passed.wait_send()
+
+
+def finish(tokens, norm1, vectors, d_resid, dq, dkv_own, dkv_other, grad_out, grad_router, norm_grads, layer):
+    low, wide = jnp.bfloat16, jnp.float32
+    anywhere = pl.BlockSpec(memory_space=pl.ANY)
+    vmem = pl.BlockSpec(memory_space=pltpu.VMEM)
+    lead = (2, SIDE, SIDE, SIDE, 8)
+    scratch, copies = reduce_scratch()
+    return pl.pallas_call(
+        finish_kernel,
+        out_shape=tuple(jax.ShapeDtypeStruct((8, c), wide) for c in RS_COLS)
+        + (jax.ShapeDtypeStruct((GROUP, WIDTH), wide),),
+        in_specs=[vmem] * 10 + [anywhere],
+        out_specs=(vmem,) * 4,
+        scratch_shapes=[
+            pltpu.VMEM((WIDTH, 3 * WIDTH), low),
+            pltpu.VMEM((WIDTH, GROUP), low),
+            pltpu.VMEM((GROUP, 2 * WIDTH), low),
+            pltpu.VMEM((GROUP, 3 * WIDTH), low),
+            pltpu.VMEM((GROUP, WIDTH), wide),
+            pltpu.VMEM((2, 8, WIDTH), wide),
+            pltpu.VMEM(lead + (3 * WIDTH,), low),
+            pltpu.VMEM(lead + (256,), wide),
+            pltpu.SemaphoreType.DMA,
+            pltpu.SemaphoreType.DMA((2,)),
+            *scratch,
+            pltpu.SemaphoreType.DMA((copies,)),
+            pltpu.SemaphoreType.DMA((copies,)),
+        ],
+        compiler_params=pltpu.CompilerParams(
+            collective_id=1, has_side_effects=True, vmem_limit_bytes=60 * 1024 * 1024
+        ),
+        name="finish",
+    )(tokens, norm1, vectors, d_resid, dq, dkv_own, dkv_other, grad_out.reshape(lead + (WIDTH,)), grad_router,
+      norm_grads, layer)
 
 
 def per_device(
@@ -653,14 +1120,7 @@
     w_in,
     w_down,
 ):
-    group = tokens.shape[1]
-    width = tokens.shape[2]
-    head_dim = width // HEADS
-    sources = lax.axis_size("expert")
-    seq_len = group * lax.axis_size("dp")
-    capacity = max(2, 2 * group // sources)
-    core = lax.axis_index("dp")
-    device = core * sources + lax.axis_index("expert")
+    device = lax.axis_index("dp") * 64 + lax.axis_index("expert")
     vectors = jnp.tile(jnp.stack([ln1_gain, ln1_bias, ln2_gain, ln2_bias]), (1, 8))
     vectors = jnp.where(jnp.arange(64)[None, :] // 8 == device % 8, vectors, 0)
     vectors = jnp.concatenate([vectors, jnp.zeros_like(vectors)], 0)
@@ -669,136 +1129,21 @@
         w_in[0],
         w_down[0],
     )
-    w_qkv = layer[:, : 3 * width]
-    w_out = layer[:, 3 * width : 4 * width]
-    w_router = layer[:, 4 * width : 4 * width + sources]
-    vectors = layer[:, 4 * width + sources :].astype(jnp.float32)
-    vectors = jnp.sum(vectors.reshape(16, 8, 8, 64), 1)
-    gain_one, bias_one, gain_two, bias_two = [vectors[:, n].reshape(width) for n in range(4)]
-    inputs = tokens[0].astype(jnp.float32)
-    norm_full, normed_one, inverse_one = layer_norm(inputs, gain_one, bias_one)
-    first_norm = norm_full.astype(jnp.bfloat16)
-    query_key_value_rows = jnp.dot(
-        first_norm, w_qkv, preferred_element_type=jnp.float32
-    ).astype(jnp.bfloat16)
-    queries = query_key_value_rows[:, :width].reshape(group, HEADS, head_dim)
-    kv_whole = lax.all_gather(query_key_value_rows[:, width:], "dp", axis=0, tiled=True)
-    key_rows = kv_whole[:, :width].reshape(seq_len, HEADS, head_dim)
-    value_rows = kv_whole[:, width:].reshape(seq_len, HEADS, head_dim)
-    query_pos = lax.axis_index("dp") * group + jnp.arange(group)
-    key_pos = jnp.arange(seq_len)
-    allowed = (key_pos[None, :] <= query_pos[:, None]) & (key_pos[None, :] < lengths[0])
-
-    def score_block():
-        scaled_raw = (
-            jnp.einsum("qhd,khd->hqk", queries, key_rows, preferred_element_type=jnp.float32)
-            * 0.125
-        )
-        return jnp.where(allowed[None], scaled_raw, -1e30)
-
-    scores = score_block()
-    maximum = jnp.max(scores, -1, keepdims=True)
-    exponent = jnp.exp(scores - maximum)
-    denominator = jnp.sum(exponent, -1, keepdims=True)
-    log_total = maximum + jnp.log(denominator)
-    probs_low = (exponent / denominator).astype(jnp.bfloat16)
-    attention_result = jnp.einsum(
-        "hqk,khd->qhd", probs_low, value_rows, preferred_element_type=jnp.float32
+    x, parting, qkv, kv_other, attended, norm1, norm2, residual, lse, probs, placing, vectors = forward(
+        tokens[0], teacher[0], routes[0], lengths, layer
     )
-    attention_result = attention_result.reshape(group, width).astype(jnp.bfloat16)
-    residual_branch = jnp.dot(attention_result, w_out, preferred_element_type=jnp.float32)
-    residual = inputs + residual_branch
-    norm_two_full, normed_two, inverse_two = layer_norm(residual, gain_two, bias_two)
-    second_norm = norm_two_full.astype(jnp.bfloat16)
-    router_scores = jnp.dot(second_norm, w_router, preferred_element_type=jnp.float32)
-    router_probs = jax.nn.softmax(router_scores, -1)
-    route_ids = routes[0, :, 0]
-    chosen = route_ids[:, None] == jnp.arange(sources)[None, :]
-    gate_prob = jnp.sum(jnp.where(chosen, router_probs, 0.0), -1)
-    ranking = jnp.cumsum(chosen.astype(jnp.int32), 0) - 1
-    slot_ids = route_ids * capacity + jnp.sum(jnp.where(chosen, ranking, 0), -1)
-    placing = (jnp.arange(sources * capacity)[:, None] == slot_ids[None, :]).astype(jnp.bfloat16)
-    outgoing = jnp.dot(placing, second_norm, preferred_element_type=jnp.float32).astype(
-        jnp.bfloat16
+    y_back, d_back, g1, g2 = experts(x, parting, w_in[0], in_other, w_down[0], down_other)
+    mixed, d_resid, dq, dkv_own, dkv_other, grad_out, grad_router, norm_grads, g1, g2 = backward(
+        y_back, d_back, teacher[0], routes[0], lengths, layer, qkv, kv_other, attended, norm2, residual, lse, probs,
+        placing, vectors, g1, g2,
     )
-    outgoing = outgoing.reshape(sources, capacity, width)
-    valid_rows = (query_pos < lengths[0]).astype(jnp.float32)
-    taught = teacher[0].astype(jnp.float32)
-    gate_high = gate_prob.astype(jnp.bfloat16)
-    gate_low = (gate_prob - gate_high.astype(jnp.float32)).astype(jnp.bfloat16)
-    extras = jnp.stack([gate_high, gate_low, valid_rows.astype(jnp.bfloat16)], 1)
-    extras = jnp.pad(extras, ((0, 0), (0, 125)))
-    parting = jnp.concatenate([(residual - taught).astype(jnp.bfloat16), extras], 1)
-    parting = jnp.dot(placing, parting, preferred_element_type=jnp.float32).astype(jnp.bfloat16)
-    returned, d_back, grad_in_out, grad_down_out = experts(
-        outgoing,
-        parting.reshape(sources, capacity, width + 128),
-        w_in[0],
-        in_other,
-        w_down[0],
-        down_other,
+    grad_qkv, grad_out, side, grad_tokens = finish(
+        tokens[0], norm1, vectors, d_resid, dq, dkv_own, dkv_other, grad_out, grad_router, norm_grads, layer
     )
-    expert_out = transposed_times(placing, returned.reshape(-1, width))
-    mixed_out = (residual + gate_prob[:, None] * expert_out).astype(jnp.bfloat16)
-    errors = mixed_out.astype(jnp.float32) - taught
-    squares = jnp.sum(valid_rows[:, None] * errors * errors)
-    count = jnp.sum(valid_rows)
-    d_mixed = valid_rows[:, None] * errors
-    d_gate = jnp.sum(d_mixed * expert_out, -1)
-    d_norm_expert = transposed_times(placing, d_back.reshape(-1, width))
-    d_logits = (d_gate * gate_prob)[:, None] * (chosen.astype(jnp.float32) - router_probs)
-    router_full = w_router.astype(jnp.float32)
-    grad_router = jnp.dot(
-        second_norm.astype(jnp.float32).T, d_logits, precision=lax.Precision.HIGHEST
-    )
-    d_norm_two = d_norm_expert + jnp.dot(d_logits, router_full.T, precision=lax.Precision.HIGHEST)
-    d_resid_part, grad_gain_two, grad_bias_two = norm_back(
-        d_norm_two, normed_two, inverse_two, gain_two
-    )
-    d_resid = d_mixed + d_resid_part
-    d_branch = d_resid.astype(jnp.bfloat16)
-    grad_out = transposed_times(attention_result, d_branch)
-    d_attended = (
-        times_transposed(d_branch, w_out)
-        .astype(jnp.bfloat16)
-        .reshape(group, HEADS, head_dim)
-    )
-    probs_again = jnp.exp(score_block() - log_total)
-    d_probs = jnp.einsum("qhd,khd->hqk", d_attended, value_rows, preferred_element_type=jnp.float32)
-    delta_sum = jnp.sum(probs_again * d_probs, -1, keepdims=True)
-    d_scores = (probs_again * (d_probs - delta_sum)).astype(jnp.bfloat16)
-    d_queries = (
-        jnp.einsum("hqk,khd->qhd", d_scores, key_rows, preferred_element_type=jnp.float32) * 0.125
-    )
-    d_keys = (
-        jnp.einsum("hqk,qhd->khd", d_scores, queries, preferred_element_type=jnp.float32) * 0.125
-    )
-    d_values = jnp.einsum("hqk,qhd->khd", probs_low, d_attended, preferred_element_type=jnp.float32)
-    d_kv_whole = jnp.concatenate(
-        [d_keys.reshape(seq_len, width), d_values.reshape(seq_len, width)], 1
-    )
-    d_kv = lax.psum_scatter(d_kv_whole.astype(jnp.bfloat16), "dp", scatter_dimension=0, tiled=True)
-    d_qkv = jnp.concatenate([d_queries.reshape(group, width).astype(jnp.bfloat16), d_kv], 1)
-    grad_qkv = transposed_times(first_norm, d_qkv)
-    d_norm_one = times_transposed(d_qkv, w_qkv)
-    d_input_part, grad_gain_one, grad_bias_one = norm_back(
-        d_norm_one, normed_one, inverse_one, gain_one
-    )
-    grad_tokens = d_resid + d_input_part
-    vector_grads = jnp.stack(
-        [grad_gain_one, grad_bias_one, grad_gain_two, grad_bias_two]
-    ).reshape(4, 128, 8)
-    vector_grads = jnp.pad(vector_grads.transpose(1, 0, 2), ((0, 0), (0, 4), (0, 56)))
-    totals = jnp.zeros((8, 128), jnp.float32).at[0, 0].set(squares).at[1, 0].set(count)
-    side = jnp.concatenate(
-        [grad_router.reshape(128, 8, sources), vector_grads, jnp.broadcast_to(totals[None], (128, 8, 128))], 2
-    )
-    grad_qkv, grad_out, side = reduce_layer(grad_qkv, grad_out, side)
-    grad_router = side[:, :sources]
-    vector_grads = side[:4, sources : sources + 8]
-    loss_value = side[0, 128] / (side[1, 128] * width)
+    vector_grads = lax.dynamic_slice(side, (0, 128 + (device % 16) * 8), (4, 8))
+    loss_value = side[4, 128] / (side[5, 128] * WIDTH)
     return (
-        mixed_out[None],
+        mixed[None],
         loss_value,
         grad_tokens[None],
         vector_grads[0],
@@ -807,9 +1152,9 @@
         grad_out,
         vector_grads[2],
         vector_grads[3],
-        grad_router,
-        grad_in_out[None],
-        grad_down_out[None],
+        side[:, :64],
+        g1[None],
+        g2[None],
     )
 
 

time: 336 us -> 240 us (0.71)
  matrix products: 62 us -> 0 us
  Pallas kernels: 172 us -> 223 us
  local copies, waits for them, and re-layouts: 48 us -> 12.2 us
  other arithmetic: 25.7 us -> 0.73 us
  between operations: 17.7 us -> 3.81 us
  waiting for transfers between devices: 8.97 us -> 0 us
    dot_general x19 -> x0, matrix products: 62 us -> none  [the longest x4 14.4 us: transposed_times(): lax.dot_general(left_mat, right_mat, (((0,), (0,)), ((), ())), preferred_...]
    pallas_call x1 -> x3, Pallas kernels: 51.4 us -> 109 us  [the longest x1 61.4 us: finish(): pl.pallas_call(finish_kernel, out_shape=tuple((jax.ShapeDtypeStruct((8, c...]
    unnamed x41 -> x3, local copies, waits for them, and re-layouts: 22.1 us -> 5.22 us
    convert_element_type x8 -> x0, other arithmetic: 9.44 us -> none  [the longest x1 4.71 us: per_device(): d_scores = (probs_again * (d_probs - delta_sum)).astype(jnp.bfloat16)]
    all_gather x1 -> x0, waiting for transfers between devices: 8.94 us -> none  [per_device(): lax.all_gather(query_key_value_rows[:, width:], 'dp', axis=0, tiled=True)]
    slice x10 -> x2, local copies, waits for them, and re-layouts: 10.1 us -> 2.54 us  [the longest x1 1.27 us: per_device(): loss_value = side[4, 128] / (side[5, 128] * WIDTH)]
    pallas_call x1, Pallas kernels: 78.8 us -> 71.9 us  [experts(): pl.pallas_call(expert_kernel, out_shape=(jax.ShapeDtypeStruct((64, 8, WID...]
    reduce_sum x9 -> x0, other arithmetic: 5.88 us -> none  [the longest x1 2.24 us: per_device(): denominator = jnp.sum(exponent, -1, keepdims=True)]
  transfers between devices with their start and end apart: 2 -> 0, of which waited for: 1 -> 0; matrix products, arithmetic and copies ran while one was open for 4% -> 0% of each run, Pallas kernels for 0% -> 0%
where the time goes in v1:
time: 240 us
  Pallas kernels  223 us (93%)
  local copies, waits for them, and re-layouts  12.2 us (5%)
  between operations  3.81 us (2%)
    pallas_call x1, Pallas kernels, experts(): pl.pallas_call(expert_kernel, out_shape=(jax.ShapeDtypeStruct((64, 8, WID...  71.9 us
    pallas_call x1, Pallas kernels, finish(): pl.pallas_call(finish_kernel, out_shape=tuple((jax.ShapeDtypeStruct((8, c...  61.4 us
    pallas_call x1, Pallas kernels, gather_layer(): pl.pallas_call(gather_kernel, out_shape=(jax.ShapeDtypeStruct((2, SIDE, S...  42.3 us
    pallas_call x1, Pallas kernels, backward(): pl.pallas_call(backward_kernel, out_shape=tuple((jax.ShapeDtypeStruct(s,...  26 us
    pallas_call x1, Pallas kernels, forward(): pl.pallas_call(forward_kernel, out_shape=tuple((jax.ShapeDtypeStruct(s, t...  21.7 us
    unnamed x3, local copies, waits for them, and re-layouts  5.22 us

profile of v1, /device:TPU:0, one launch (start us, length us, event | category | flops | bytes accessed | tf_op | source)
XLA Modules:
  0.0 240.0 jit_solution(7592603018088515297)
XLA Ops:
  1.3 0.7 pad_maximum_fusion
  2.1 0.1 tile.10
  2.2 1.5 concatenate.7.shard
  3.7 1.5 copy.25.routes
  5.2 42.3 %gather_layer.1 = (bf16[2,4,4,4,8,4224]{5,4,3,2,1,0:T(8,128)(2,1)}, bf16[512,4096]{1,0:T(8,128)(2,1)}, bf16[2048,1024]{1,0:T(8,128)(2,1)}) custom-call(bf16[8,4224]{1,0:T(8,128)(2,1)} %concatenate.7.shard, bf16[512,4096]{1,0:T(8,128)(2,1)} %bitcast.27, bf16[2048,1024]{1,0:T(8,128)(2,1)} %bitcast.29), custom_call_target="tpu_custom_call" | custom-call | tf_op jit(solution)/shard_map/gather_layer/pallas_call | solution.py:120
  47.5 21.7 %forward.1 = (bf16[64,8,1024]{2,1,0:T(8,128)(2,1)}, bf16[64,8,1152]{2,1,0:T(8,128)(2,1)}, bf16[256,3072]{1,0:T(8,128)(2,1)}, bf16[256,2048]{1,0:T(8,128)(2,1)}, ...) custom-call(bf16[256,1024]{1,0:T(8,128)(2,1)} %bitcast.31, ...), custom_call_target="tpu_custom_call" | custom-call | tf_op jit(solution)/shard_map/forward/pallas_call | solution.py:793
  69.1 71.9 %experts.1 = (bf16[64,8,1024]{2,1,0:T(8,128)(2,1)}, bf16[64,8,1024]{2,1,0:T(8,128)(2,1)}, f32[512,4096]{1,0:T(8,128)}, f32[2048,1024]{1,0:T(8,128)}) custom-call(bf16[64,8,1024]{2,1,0:T(8,128)(2,1)} %get-tuple-element.46.x, bf16[64,8,1152]{2,1,0:T(8,128)(2,1)} %get-tuple-element.47.r, bf16[512,4096]{1,0:T(8,128)(2,1)} %bitcast.28, ...), custom_call_target="tpu_custom_call" | custom-call | tf_op jit(solution)/shard_map/experts/pallas_call | solution.py:545
  141.1 26.0 %backward.1 = (bf16[256,1024]{1,0:T(8,128)(2,1)}, f32[256,1024]{1,0:T(8,128)}, bf16[256,1024]{1,0:T(8,128)(2,1)}, f32[256,2048]{1,0:T(8,128)}, bf16[256,2048]{1,...) custom-call(bf16[64,8,1024]{2,1,0:T(8,128)(2,1)} %get-tuple-element., ...), custom_call_target="tpu_custom_call" | custom-call | tf_op jit(solution)/shard_map/backward/pallas_call | solution.py:972
  167.1 61.4 %finish.1 = (f32[8,3072]{1,0:T(8,128)}, f32[8,1024]{1,0:T(8,128)}, f32[8,256]{1,0:T(8,128)}, f32[256,1024]{1,0:T(8,128)}) custom-call(bf16[256,1024]{1,0:T(8,128)(2,1)} %bitcast.32, bf16[256,1024]{1,0:T(8,128)(2,1)} %get-tuple-element.64.norm1, f32[8,1024]{1,0:T(8,128)} %get-tuple-element.60.vectors, f32[256,1024]{1,0:T(8,128)} %get-tuple-element.65.d_resid, ...), custom_call_target="tpu_custom_call" | custom-call | tf_op jit(solution)/shard_map/finish/pallas_call | solution.py:1079
  228.5 1.3 fusion.1
  231.1 0.8 constant_dynamic-slice_fusion
  231.8 1.3 slice.27
  233.1 0.5 slice_bitcast_fusion
  233.6 2.3 copy.31
  235.9 1.5 copy.32
  237.4 1.4 copy.33
  (4 shorter events, 0.0 us)

commit v2 on v1

--- a/solution.py
+++ b/solution.py
@@ -13,10 +13,6 @@
 AG_PIECES = ((0, 768, 1408), (1408, 2176, 2816), (2816, 3584, 4224))
 
 
-def place(region, c0, c1):
-    return tuple(region) + (FULL, pl.ds(c0, c1 - c0))
-
-
 def coords():
     e = lax.axis_index("expert")
     return [e // 16, (e // 4) % 4, e % 4]
@@ -32,15 +28,13 @@
     return {"expert": pos[0] * 16 + pos[1] * 4 + pos[2]}
 
 
-def neighbours(pos):
-    return [chip(shifted(pos, axis, by)) for axis in range(3) for by in (1, 3)]
-
-
 def greet(pos, core):
     barrier = pltpu.get_barrier_semaphore()
-    for other in neighbours(pos) + [{"dp": 1 - core}]:
-        pl.semaphore_signal(barrier, inc=1, device_id=other, device_id_type=MESH)
-    pl.semaphore_wait(barrier, 7)
+    for axis in range(3):
+        for by in range(1, SIDE):
+            pl.semaphore_signal(barrier, inc=1, device_id=chip(shifted(pos, axis, by)), device_id_type=MESH)
+    pl.semaphore_signal(barrier, inc=1, device_id={"dp": 1 - core}, device_id_type=MESH)
+    pl.semaphore_wait(barrier, 10)
 
 
 class Sender:
@@ -61,62 +55,105 @@
         self.sent.append(copy)
         return copy
 
-
-def gather_kernel(shard, w_in, w_down, whole, in_other, down_other, own_sem, send_sems, recv_sems):
+    def close(self):
+        for copy in self.sent:
+            copy.wait_send()
+
+
+def gather_kernel(
+    q, o, r, vectors, w_in, w_down, whole, in_other, down_other, shard, own_sem, send_sems, recv_sems
+):
     pos = coords()
     core = lax.axis_index("dp")
     partner = {"dp": 1 - core}
+    shard[:, :3072] = q[...]
+    shard[:, 3072:4096] = o[...]
+    shard[:, 4096:] = jnp.concatenate([r[...].astype(jnp.float32), vectors[...]], 1).astype(jnp.bfloat16)
     own = pltpu.make_async_copy(shard, whole.at[(core, *pos)], own_sem)
     own.start()
     greet(pos, core)
     send = Sender(send_sems, recv_sems)
+
+    def share(region, c0, c1, device):
+        spot = whole.at[(core, *region, FULL, pl.ds(c0, c1 - c0))]
+        return send(spot, spot, device)
+
+    plans = []
+    for piece, (c0, mid, c1) in enumerate(AG_PIECES):
+        axes = [(piece + step) % 3 for step in range(3)]
+        spot = whole.at[(core, *pos, FULL, pl.ds(c0, c1 - c0))]
+        first = [send(shard.at[:, pl.ds(c0, c1 - c0)], spot, chip(shifted(pos, axes[0], by))) for by in (1, 3, 2)]
+        plans.append((axes, c0, mid, c1, first))
     across = [send(w_in, in_other, partner), send(w_down, down_other, partner)]
     own.wait()
 
-    def share(region, c0, c1, device):
-        spot = whole.at[place([core] + region, c0, c1)]
-        return send(spot, spot, device)
-
-    for stage in range(3):
-        first = []
-        for piece, (c0, mid, c1) in enumerate(AG_PIECES):
-            order = [(piece + step) % 3 for step in range(3)]
-            axis = order[stage]
-            done = order[:stage]
-            region = [FULL if a in done else pos[a] for a in range(3)]
-            up, down = chip(shifted(pos, axis, 1)), chip(shifted(pos, axis, 3))
-            first.append((axis, region, up, down, share(region, c0, c1, up), share(region, c0, c1, down)))
-        if stage == 2:
-            for (c0, mid, c1), (axis, region, up, down, _, _) in zip(AG_PIECES, first):
-                across.append(share(region, c0, c1, partner))
-        second = []
-        for (c0, mid, c1), (axis, region, up, down, to_up, to_down) in zip(AG_PIECES, first):
-            below, above = list(region), list(region)
-            below[axis], above[axis] = (pos[axis] + 3) % SIDE, (pos[axis] + 1) % SIDE
-            to_up.wait_recv()
-            on_up = share(below, c0, mid, up)
-            to_down.wait_recv()
-            on_down = share(above, mid, c1, down)
-            second.append((on_up, on_down))
-            if stage == 2:
-                across.append(share(below, c0, c1, partner))
-                across.append(share(above, c0, c1, partner))
-        for (c0, mid, c1), (axis, region, up, down, _, _), (on_up, on_down) in zip(AG_PIECES, first, second):
-            on_up.wait_recv()
-            on_down.wait_recv()
-            if stage == 2:
-                far = list(region)
-                far[axis] = (pos[axis] + 2) % SIDE
-                across.append(share(far, c0, c1, partner))
+    def line(axes, second, third):
+        region = [None] * 3
+        region[axes[0]], region[axes[1]], region[axes[2]] = FULL, second, third
+        return region
+
+    def at(axis, by):
+        return (pos[axis] + by) % SIDE
+
+    seconds, lines = [], [{} for _ in plans]
+
+    def onward(piece, by):
+        axes, c0, mid, c1, _ = plans[piece]
+        region = line(axes, at(axes[1], by), pos[axes[2]])
+        lines[piece][by] = (
+            share(region, c0, c1, chip(shifted(pos, axes[2], 1))),
+            share(region, c0, c1, chip(shifted(pos, axes[2], 3))),
+        )
+        across.append(share(region, c0, c1, partner))
+
+    def relay(piece, by):
+        axes, c0, mid, c1, _ = plans[piece]
+        up, down = lines[piece][by]
+        up.wait_recv()
+        below = line(axes, at(axes[1], by), at(axes[2], 3))
+        on_up = share(below, c0, mid, chip(shifted(pos, axes[2], 1)))
+        down.wait_recv()
+        above = line(axes, at(axes[1], by), at(axes[2], 1))
+        on_down = share(above, mid, c1, chip(shifted(pos, axes[2], 3)))
+        across.append(share(below, c0, c1, partner))
+        across.append(share(above, c0, c1, partner))
+        lines[piece][by] = (on_up, on_down)
+
+    def end(piece, by):
+        axes, c0, mid, c1, _ = plans[piece]
+        for copy in lines[piece][by]:
+            copy.wait_recv()
+        across.append(share(line(axes, at(axes[1], by), at(axes[2], 2)), c0, c1, partner))
+
+    for piece, (axes, c0, mid, c1, first) in enumerate(plans):
+        for copy in first:
+            copy.wait_recv()
+        region = line(axes, pos[axes[1]], pos[axes[2]])
+        seconds.append([share(region, c0, c1, chip(shifted(pos, axes[1], by))) for by in (1, 3, 2)])
+        onward(piece, 0)
+    for n, by in enumerate((3, 1)):
+        for piece in range(3):
+            seconds[piece][n].wait_recv()
+            onward(piece, by)
+    for piece in range(3):
+        relay(piece, 0)
+    for piece in range(3):
+        seconds[piece][2].wait_recv()
+        onward(piece, 2)
+    for by in (3, 1, 2):
+        for piece in range(3):
+            relay(piece, by)
+    for by in (0, 3, 1, 2):
+        for piece in range(3):
+            end(piece, by)
     for copy in across:
         copy.wait_recv()
-    for copy in send.sent:
-        copy.wait_send()
-
-
-def gather_layer(shard, w_in, w_down):
-    copies = 3 * 3 * 4 + 3 * 4 + 2
-    anywhere = pl.BlockSpec(memory_space=pl.ANY)
+    send.close()
+
+
+def gather_layer(q, o, r, vectors, w_in, w_down):
+    copies = 3 * (3 + 3 + 4 * 4 + 4 * 4) + 2
+    anywhere, vmem = pl.BlockSpec(memory_space=pl.ANY), pl.BlockSpec(memory_space=pltpu.VMEM)
     whole, in_other, down_other = pl.pallas_call(
         gather_kernel,
         out_shape=(
@@ -124,191 +161,193 @@
             jax.ShapeDtypeStruct(w_in.shape, w_in.dtype),
             jax.ShapeDtypeStruct(w_down.shape, w_down.dtype),
         ),
-        in_specs=[anywhere] * 3,
+        in_specs=[vmem] * 4 + [anywhere] * 2,
         out_specs=(anywhere,) * 3,
         scratch_shapes=[
+            pltpu.VMEM((8, AG_COLS), jnp.bfloat16),
             pltpu.SemaphoreType.DMA,
             pltpu.SemaphoreType.DMA((copies,)),
             pltpu.SemaphoreType.DMA((copies,)),
         ],
         compiler_params=pltpu.CompilerParams(collective_id=0, has_side_effects=True),
         name="gather_layer",
-    )(shard, w_in, w_down)
+    )(q, o, r, vectors, w_in, w_down)
     return whole.reshape(1024, AG_COLS), in_other, down_other
 
 
 RS_COLS = (3072, 1024, 256)
-RS_KINDS = (jnp.bfloat16, jnp.bfloat16, jnp.float32)
-RS_HALVES = (
-    (((0, 0, 768),), ((0, 768, 1536),)),
-    (((0, 1536, 2304),), ((0, 2304, 3072),)),
-    (((1, 0, 768),), ((1, 768, 1024), (2, 0, 256))),
-)
-RS_PIECES = tuple(h0 + h1 for h0, h1 in RS_HALVES)
-
-
-def reduce_all(pos, core, source, outs, rest):
-    refs, (send_sems, recv_sems) = list(rest[:-2]), rest[-2:]
-    take = iter(refs)
-    partner = {"dp": 1 - core}
-    send = Sender(send_sems, recv_sems)
-    landed = (next(take), next(take), next(take))
-
-    opening = []
-    for piece in range(3):
+RS_PIECES = ((0, 0, 768, 1536, 0), (0, 1536, 2304, 3072, 1), (1, 0, 512, 1024, 2))
+ORDER = (2, 1, 3, 0)
+
+
+class Reduction:
+    low = jnp.bfloat16
+    COPIES = 8 + 8 + 3 + 3
+
+    def __init__(self, piece, pos, send, source, out, bufs):
+        _, self.c0, self.mid, self.c1, first = piece
+        self.axes = [(first + step) % 3 for step in range(3)]
+        self.pos, self.send, self.source, self.out = pos, send, source, out
+        (self.total, self.send_2, self.recv_2, self.mine, self.send_3, self.recv_3) = bufs[:6]
+        self.take(bufs[6:])
+
+    def take(self, bufs):
+        self.send_a, self.recv_a, self.send_b, self.recv_b = bufs
+
+    @classmethod
+    def scratch(cls, piece):
+        _, c0, mid, c1, _ = piece
+        width, low, wide = c1 - c0, cls.low, jnp.float32
+        return [
+            pltpu.VMEM((SIDE, 8, width), wide),
+            pltpu.VMEM((3, SIDE, 8, width), low),
+            pltpu.VMEM((3, SIDE, 8, width), low),
+            pltpu.VMEM((8, width), wide),
+            pltpu.VMEM((3, 8, width), low),
+            pltpu.VMEM((3, 8, width), low),
+        ] + cls.more(mid - c0, width)
+
+    @classmethod
+    def more(cls, half, width):
+        return [pltpu.VMEM((2, SIDE, SIDE, 8, half), cls.low)] * 2 + [pltpu.VMEM((2, SIDE, SIDE, 8, width), cls.low)] * 2
+
+    def to(self, step, by):
+        return chip(shifted(self.pos, self.axes[step], by))
+
+    def term(self, first, second, third, c0, c1):
+        spot = [None] * 3
+        spot[self.axes[0]] = (self.pos[self.axes[0]] + first) % SIDE
+        spot[self.axes[1]] = (self.pos[self.axes[1]] + second) % SIDE
+        spot[self.axes[2]] = third
+        return self.source[(*spot, FULL, pl.ds(c0, c1 - c0))]
+
+    def first(self):
+        self.firsts = []
+        for group in ORDER:
+            @pl.loop(0, SIDE)
+            def _(s):
+                self.send_a[0, group, s] = self.term(2, group, s, self.c0, self.mid).astype(self.low)
+                self.send_a[1, group, s] = self.term(2, group, s, self.mid, self.c1).astype(self.low)
+
+            self.firsts.append([
+                self.send(self.send_a.at[way, group], self.recv_a.at[way, group], self.to(0, (1, 3)[way]))
+                for way in range(2)
+            ])
+
+    def second(self):
+        self.seconds = []
+        half = self.mid - self.c0
+        for n, group in enumerate(ORDER):
+            for copy in self.firsts[n]:
+                copy.wait_recv()
+
+            @pl.loop(0, SIDE)
+            def _(s):
+                for way, by in enumerate((1, 3)):
+                    for part, (c0, c1) in enumerate(((self.c0, self.mid), (self.mid, self.c1))):
+                        block = self.term(by, group, s, c0, c1)
+                        if part == way:
+                            block = block + self.recv_a[way, group, s].astype(jnp.float32)
+                        self.send_b[way, group, s, :, pl.ds(part * half, half)] = block.astype(self.low)
+
+            self.seconds.append([
+                self.send(self.send_b.at[way, group], self.recv_b.at[way, group], self.to(0, (1, 3)[way]))
+                for way in range(2)
+            ])
+
+    def arrived(self, n, group, s):
+        block = self.term(0, group, s, self.c0, self.c1)
+        for way in range(2):
+            block = block + self.recv_b[way, group, s].astype(jnp.float32)
+        return block
+
+    def third(self):
+        self.thirds = []
+        for n, group in enumerate(ORDER):
+            for copy in self.seconds[n]:
+                copy.wait_recv()
+
+            @pl.loop(0, SIDE)
+            def _(s):
+                block = self.arrived(n, group, s)
+                if group:
+                    self.send_2[group - 1, s] = block.astype(self.low)
+                else:
+                    self.total[s] = block
+
+            if group:
+                self.thirds.append(self.send(self.send_2.at[group - 1], self.recv_2.at[group - 1], self.to(1, group)))
+
+    def fourth(self):
+        for copy in self.thirds:
+            copy.wait_recv()
+        self.fourths = []
+        for by in ORDER:
+            s = (self.pos[self.axes[2]] + by) % SIDE
+            block = self.total[s]
+            for n in range(3):
+                block = block + self.recv_2[n, s].astype(jnp.float32)
+            if by:
+                self.send_3[by - 1] = block.astype(self.low)
+                self.fourths.append(self.send(self.send_3.at[by - 1], self.recv_3.at[by - 1], self.to(2, by)))
+            else:
+                self.mine[...] = block
+
+    def last(self):
+        for copy in self.fourths:
+            copy.wait_recv()
+        block = self.mine[...]
+        for n in range(3):
+            block = block + self.recv_3[n].astype(jnp.float32)
+        self.out[:, pl.ds(self.c0, self.c1 - self.c0)] = block
+
+
+class SmallReduction(Reduction):
+    low = jnp.float32
+    COPIES = 1 + 3 + 3 + 3
+
+    def take(self, bufs):
+        self.landed, self.send_1, self.recv_1 = bufs
+
+    @classmethod
+    def more(cls, half, width):
+        return [pltpu.VMEM((SIDE, SIDE, SIDE, 8, width), cls.low)] + [
+            pltpu.VMEM((3, SIDE, SIDE, 8, width), cls.low)
+        ] * 2
+
+    def open(self, core, both):
+        self.source = both.at[core]
+        self.opening = self.send(both.at[1 - core], self.landed, {"dp": 1 - core})
+
+    def term(self, *spot):
+        kept = self.source
+        mine = super().term(*spot)
+        self.source = self.landed
+        theirs = super().term(*spot)
+        self.source = kept
+        return mine + theirs
+
+    def first(self):
+        self.opening.wait_recv()
+        self.seconds = [[]] * SIDE
         copies = []
-        for kind, c0, c1 in RS_PIECES[piece]:
-            copies.append(
-                send(
-                    source[kind].at[place([1 - core, FULL, FULL, FULL], c0, c1)],
-                    landed[kind].at[place([FULL, FULL, FULL], c0, c1)],
-                    partner,
-                )
-            )
-        opening.append(copies)
-
-    def whole_sum(kind, index, c0, c1):
-        spot = index + (FULL, pl.ds(c0, c1 - c0))
-        mine = source[kind][(core,) + spot].astype(jnp.float32)
-        return mine + landed[kind][spot].astype(jnp.float32)
-
-    sums = []
-    for piece in range(3):
-        sums.append(whole_sum)
-
-    for stage in range(3):
-        plans = []
-        for piece in range(3):
-            order = [(piece + step) % 3 for step in range(3)]
-            axis = order[stage]
-            free = sorted(order[stage + 1:])
-            fixed = order[:stage]
-            bufs = {}
-            for half in range(2):
-                for n, (kind, c0, c1) in enumerate(RS_HALVES[piece][half]):
-                    for what in ("sendA", "recvA"):
-                        bufs[what, half, n] = next(take)
-            for way in range(2):
-                for n, (kind, c0, c1) in enumerate(RS_PIECES[piece]):
-                    for what in ("sendB", "recvB"):
-                        bufs[what, way, n] = next(take)
-            up, down = chip(shifted(pos, axis, 1)), chip(shifted(pos, axis, 3))
-            plans.append((axis, free, fixed, bufs, (up, down)))
-
-        def each(free, body):
-            total = SIDE ** len(free)
-
-            @pl.loop(0, total)
-            def _(i):
-                if len(free) == 2:
-                    body((i // SIDE, i % SIDE))
-                elif len(free) == 1:
-                    body((i,))
-                else:
-                    body(())
-
-        def index_of(axis, free, fixed, at, spots):
-            index = [None] * 3
-            for a in fixed:
-                index[a] = pos[a]
-            index[axis] = at
-            for a, s in zip(free, spots):
-                index[a] = s
-            return tuple(index)
-
-        firsts = []
-        for piece, (axis, free, fixed, bufs, ways) in enumerate(plans):
-            if stage == 0:
-                for copy in opening[piece]:
-                    copy.wait_recv()
-            far = (pos[axis] + 2) % SIDE
-            copies = []
-            for half in range(2):
-                def fill(spots, half=half, axis=axis, free=free, fixed=fixed, bufs=bufs, piece=piece, far=far):
-                    for n, (kind, c0, c1) in enumerate(RS_HALVES[piece][half]):
-                        block = sums[piece](kind, index_of(axis, free, fixed, far, spots), c0, c1)
-                        buf = bufs["sendA", half, n]
-                        buf[spots + (FULL, FULL)] = block.astype(buf.dtype)
-
-                each(free, fill)
-                for n in range(len(RS_HALVES[piece][half])):
-                    copies.append(send(bufs["sendA", half, n], bufs["recvA", half, n], ways[half]))
-            firsts.append(copies)
-        seconds = []
-        for piece, (axis, free, fixed, bufs, ways) in enumerate(plans):
-            for copy in firsts[piece]:
-                copy.wait_recv()
-            copies = []
-            for way in range(2):
-                at = (pos[axis] + (1, 3)[way]) % SIDE
-
-                def fill(spots, way=way, axis=axis, free=free, fixed=fixed, bufs=bufs, piece=piece, at=at):
-                    index = index_of(axis, free, fixed, at, spots)
-                    n = 0
-                    for half in range(2):
-                        for m, (kind, c0, c1) in enumerate(RS_HALVES[piece][half]):
-                            block = sums[piece](kind, index, c0, c1)
-                            if half == way:
-                                block = block + bufs["recvA", half, m][spots + (FULL, FULL)].astype(jnp.float32)
-                            buf = bufs["sendB", way, n]
-                            buf[spots + (FULL, FULL)] = block.astype(buf.dtype)
-                            n += 1
-
-                each(free, fill)
-                for n in range(len(RS_PIECES[piece])):
-                    copies.append(send(bufs["sendB", way, n], bufs["recvB", way, n], ways[way]))
-            seconds.append(copies)
-        for piece, (axis, free, fixed, bufs, ways) in enumerate(plans):
-            for copy in seconds[piece]:
-                copy.wait_recv()
-            if stage < 2:
-                total = {n: next(take) for n in range(len(RS_PIECES[piece]))}
-            else:
-                total = None
-
-            def fill(spots, axis=axis, free=free, fixed=fixed, bufs=bufs, piece=piece, total=total):
-                index = index_of(axis, free, fixed, pos[axis], spots)
-                for n, (kind, c0, c1) in enumerate(RS_PIECES[piece]):
-                    block = sums[piece](kind, index, c0, c1)
-                    for way in range(2):
-                        block = block + bufs["recvB", way, n][spots + (FULL, FULL)].astype(jnp.float32)
-                    if total is None:
-                        outs[kind][:, c0:c1] = block
-                    else:
-                        total[n][spots + (FULL, FULL)] = block
-
-            each(free, fill)
-            if total is not None:
-                def partial(kind, index, c0, c1, total=total, piece=piece, free=free):
-                    spots = tuple(index[a] for a in free)
-                    for n, (k, s0, s1) in enumerate(RS_PIECES[piece]):
-                        if k == kind and s0 <= c0 and c1 <= s1:
-                            return total[n][spots + (FULL, pl.ds(c0 - s0, c1 - c0))]
-
-                sums[piece] = partial
-    for copy in send.sent:
-        copy.wait_send()
-
-
-def reduce_scratch():
-    scratch = [pltpu.VMEM((SIDE, SIDE, SIDE, 8, c), k) for c, k in zip(RS_COLS, RS_KINDS)]
-    copies = sum(len(p) for p in RS_PIECES)
-    for stage in range(3):
-        lead = (SIDE,) * (2 - stage)
-        for piece in range(3):
-            for half in range(2):
-                for kind, c0, c1 in RS_HALVES[piece][half]:
-                    scratch += [pltpu.VMEM(lead + (8, c1 - c0), RS_KINDS[kind])] * 2
-                    copies += 1
-            for way in range(2):
-                for kind, c0, c1 in RS_PIECES[piece]:
-                    scratch += [pltpu.VMEM(lead + (8, c1 - c0), RS_KINDS[kind])] * 2
-                    copies += 1
-        if stage < 2:
-            for piece in range(3):
-                for kind, c0, c1 in RS_PIECES[piece]:
-                    scratch += [pltpu.VMEM(lead + (8, c1 - c0), jnp.float32)]
-    return scratch, copies
+        for by in (2, 1, 3):
+            @pl.loop(0, SIDE)
+            def _(s):
+                for group in range(SIDE):
+                    self.send_1[by - 1, group, s] = self.term(by, group, s, self.c0, self.c1)
+
+            copies.append(self.send(self.send_1.at[by - 1], self.recv_1.at[by - 1], self.to(0, by)))
+        self.seconds = [copies] + [[]] * 3
+
+    def arrived(self, n, group, s):
+        block = self.term(0, group, s, self.c0, self.c1)
+        for way in range(3):
+            block = block + self.recv_1[way, group, s]
+        return block
+
+
+SMALL = (2, 0, 128, 256, 2)
 
 
 ROWS = 512
@@ -634,7 +673,7 @@
 
 
 def forward_kernel(
-    tokens, teacher, routes, lengths, layer,
+    tokens, teacher, routes_row, lengths, layer,
     x_out, parting_out, qkv_out, kv_other_out, attended_out, norm1_out, norm2_out, residual_out,
     lse_out, probs_out, placing_out, vectors_out,
     weights, norm1, qkv, kv_other, attended, norm2, residual, lse, probs, placing, vectors, parted, packed_x, packed_r,
@@ -665,6 +704,9 @@
         part = jnp.sum(part.reshape(8, 8, 128), 0)
         vectors[:, g * 64 : (g + 1) * 64] = part[:, 64:]
     save(vectors, vectors_out)
+
+    routes = jnp.where(row_ids(GROUP, GROUP) == lane_ids(GROUP, GROUP), routes_row[...], 0)
+    route = jnp.sum(routes.astype(jnp.float32), -1, keepdims=True)
 
     def first_norm(rows, _):
         n, _ = normed(tokens[rows, :].astype(jnp.float32))
@@ -745,10 +787,10 @@
     logits = jnp.where(ids < 64, logits, MASKED)
     e = jnp.exp(logits - jnp.max(logits, -1, keepdims=True))
     share = e / jnp.sum(e, -1, keepdims=True)
-    probs[...] = share
+    chosen = ids.astype(jnp.float32) == route
+    gate = jnp.sum(jnp.where(chosen, share, 0.0), -1, keepdims=True)
+    probs[...] = jnp.where(ids == 64, gate, jnp.where(ids == 65, route, share))
     save(probs, probs_out)
-    chosen = ids == routes[...]
-    gate = jnp.sum(jnp.where(chosen, share, 0.0), -1, keepdims=True)
     low_gate = gate.astype(jnp.bfloat16).astype(jnp.float32)
     valid = (row_ids(GROUP, 128) + core * GROUP < length).astype(jnp.float32)
     extras = jnp.where(ids == 0, low_gate, jnp.where(ids == 1, gate - low_gate, jnp.where(ids == 2, valid, 0.0)))
@@ -756,7 +798,7 @@
     marks = chosen.astype(jnp.float32).astype(jnp.bfloat16)
     before = (lane_ids(GROUP, GROUP) < row_ids(GROUP, GROUP)).astype(jnp.float32).astype(jnp.bfloat16)
     rank = jnp.sum(jnp.where(chosen, dot_nn(before, marks), 0.0), -1, keepdims=True)
-    slot = routes[...].astype(jnp.float32) * 8.0 + rank
+    slot = route * 8.0 + rank
     placing[...] = (lane_ids(GROUP, SLOTS).astype(jnp.float32) == slot).astype(jnp.float32).astype(jnp.bfloat16)
     save(placing, placing_out)
     for half in range(2):
@@ -822,10 +864,10 @@
 
 
 def backward_kernel(
-    y_back, d_back, teacher, routes, lengths, layer, qkv, kv_other, attended, norm2, residual, lse, probs,
+    y_back, d_back, teacher, lengths, layer, qkv, kv_other, norm2, residual, lse, probs,
     placing, vectors, g1, g2,
-    mixed_out, d_resid, dq, dkv_own, dkv_other, grad_out, grad_router, norm_grads, g1_out, g2_out,
-    w_out, w_router, eo, dn, sums, d_branch, d_attended, attended_t, delta, logit_parts,
+    mixed_out, d_resid, dq, dkv_own, dkv_other, d_branch, grad_router, norm_grads, g1_out, g2_out,
+    w_out, w_router, eo, dn, sums, d_attended, logit_parts,
     held1, held2, pass_sems, load_sems,
 ):
     core = lax.axis_index("dp")
@@ -853,8 +895,9 @@
     def loss(rows, first):
         ids = lane_ids(BLOCK, 128)
         share = probs[rows, :]
-        chosen = ids == routes[rows, :]
-        gate = jnp.sum(jnp.where(chosen, share, 0.0), -1, keepdims=True)
+        gate = share[:, 64:65]
+        chosen = ids.astype(jnp.float32) == share[:, 65:66]
+        share = jnp.where(ids < 64, share, 0.0)
         out = eo[rows, :]
         mixed = (residual[rows, :] + gate * out).astype(jnp.bfloat16)
         mixed_out[rows, :] = mixed
@@ -901,12 +944,10 @@
             jnp.where(ids == 4, square, jnp.where(ids == 5, valid_all, 0.0)),
         ),
     )
-    attended_t[...] = attended[...].astype(jnp.float32).T.astype(jnp.bfloat16)
 
     @pl.loop(0, 2)
     def _(i):
         cols = lanes(i * 512, 512)
-        grad_out[:, cols] = dot_nn(attended_t[...], d_branch[:, cols]).astype(jnp.bfloat16)
         rows = pl.ds(pl.multiple_of(i * 512, 512), 512)
         d_attended[:, cols] = dot_nt(d_branch[...], w_out[rows, :]).astype(jnp.bfloat16)
 
@@ -943,8 +984,8 @@
             ))
         d_q, d_k, d_k_other, d_v, d_v_other = [jnp.where(left, a, b) for a, b in zip(*parts)]
         dq[:, lanes(pair * 128, 128)] = (d_q * 0.125).astype(jnp.bfloat16)
-        dkv_own[:, lanes(pair * 128, 128)] = d_k * 0.125
-        dkv_own[:, lanes(1024 + pair * 128, 128)] = d_v
+        dkv_own[:, lanes(pair * 128, 128)] = (d_k * 0.125).astype(jnp.bfloat16)
+        dkv_own[:, lanes(1024 + pair * 128, 128)] = d_v.astype(jnp.bfloat16)
         dkv_other[:, lanes(pair * 128, 128)] = (d_k_other * 0.125).astype(jnp.bfloat16)
         dkv_other[:, lanes(1024 + pair * 128, 128)] = d_v_other.astype(jnp.bfloat16)
 
@@ -952,7 +993,7 @@
         onward.wait()
 
 
-def backward(y_back, d_back, teacher, routes, lengths, layer, qkv, kv_other, attended, norm2, residual, lse, probs,
+def backward(y_back, d_back, teacher, lengths, layer, qkv, kv_other, norm2, residual, lse, probs,
              placing, vectors, g1, g2):
     low, wide = jnp.bfloat16, jnp.float32
     anywhere = pl.BlockSpec(memory_space=pl.ANY)
@@ -961,9 +1002,9 @@
         ((GROUP, WIDTH), low),
         ((GROUP, WIDTH), wide),
         ((GROUP, WIDTH), low),
-        ((GROUP, 2 * WIDTH), wide),
         ((GROUP, 2 * WIDTH), low),
-        ((WIDTH, WIDTH), low),
+        ((GROUP, 2 * WIDTH), low),
+        ((GROUP, WIDTH), low),
         ((WIDTH, 128), wide),
         ((8, WIDTH), wide),
         (g1.shape, wide),
@@ -972,7 +1013,7 @@
     return pl.pallas_call(
         backward_kernel,
         out_shape=tuple(jax.ShapeDtypeStruct(s, t) for s, t in made),
-        in_specs=[vmem, vmem, vmem, vmem, pl.BlockSpec(memory_space=pltpu.SMEM), anywhere] + [vmem] * 9 + [anywhere] * 2,
+        in_specs=[vmem, vmem, vmem, pl.BlockSpec(memory_space=pltpu.SMEM), anywhere] + [vmem] * 8 + [anywhere] * 2,
         out_specs=(vmem,) * 8 + (anywhere,) * 2,
         scratch_shapes=[
             pltpu.VMEM((WIDTH, WIDTH), low),
@@ -981,9 +1022,6 @@
             pltpu.VMEM((GROUP, WIDTH), wide),
             pltpu.VMEM((3, 8, WIDTH), wide),
             pltpu.VMEM((GROUP, WIDTH), low),
-            pltpu.VMEM((GROUP, WIDTH), low),
-            pltpu.VMEM((WIDTH, GROUP), low),
-            pltpu.VMEM((GROUP, 128), wide),
             pltpu.VMEM((GROUP, 256), low),
             pltpu.VMEM(g1.shape, wide),
             pltpu.VMEM(g2.shape, wide),
@@ -992,64 +1030,131 @@
         ],
         compiler_params=pltpu.CompilerParams(vmem_limit_bytes=56 * 1024 * 1024),
         name="backward",
-    )(y_back, d_back, teacher, routes, lengths, layer, qkv, kv_other, attended, norm2, residual, lse, probs,
+    )(y_back, d_back, teacher, lengths, layer, qkv, kv_other, norm2, residual, lse, probs,
       placing, vectors, g1, g2)
 
 
+HALF = WIDTH // 2
+
+
+def transposed(block):
+    return block.astype(jnp.float32).T.astype(jnp.bfloat16)
+
+
 def finish_kernel(
-    tokens, norm1, vectors, d_resid, dq, dkv_own, dkv_other, grad_out, grad_router, norm_grads, layer,
+    tokens, norm1, attended, vectors, d_resid, dq, dkv_own, dkv_other, d_branch, grad_router, norm_grads, layer,
     sum_qkv, sum_out, sum_side, grad_tokens,
-    weights, norm1_t, landed_kv, dqkv, acc, sums, grad_qkv, side, load_sem, kv_sems, *rest,
+    weights, x, d_res, left, left_t, mine, theirs, got_left, dqkv, d_both, acc, sums, grad_qkv, grad_out,
+    router, vec, norms, side, load_sems, *rest,
 ):
     pos = coords()
     core = lax.axis_index("dp")
-    load = pltpu.make_async_copy(layer.at[:, pl.ds(0, 3072)], weights, load_sem)
-    load.start()
+    partner = {"dp": 1 - core}
+    keep, give = pl.ds(core * HALF, HALF), pl.ds((1 - core) * HALF, HALF)
+    own, other = pl.ds(0, GROUP), pl.ds(GROUP, GROUP)
+    spans = (
+        (norm1.at[:, keep], left.at[0]),
+        (attended.at[:, keep], left.at[1]),
+        (d_branch, d_both.at[own, :]),
+        (layer.at[:, pl.ds(0, 3072)], weights),
+        (dq, dqkv.at[own, pl.ds(0, WIDTH)]),
+        (dkv_own, mine.at[0]),
+        (dkv_other, mine.at[1]),
+        (tokens, x),
+        (vectors, vec),
+        (d_resid, d_res),
+        (grad_router, router),
+        (norm_grads, norms),
+    )
+    loads = [pltpu.make_async_copy(src, dst, load_sems.at[n]) for n, (src, dst) in enumerate(spans)]
+    for load in loads:
+        load.start()
     greet(pos, core)
-    passed = pltpu.make_async_remote_copy(
-        src_ref=dkv_other,
-        dst_ref=landed_kv,
-        send_sem=kv_sems.at[0],
-        recv_sem=kv_sems.at[1],
-        device_id={"dp": 1 - core},
-        device_id_type=MESH,
-    )
-    passed.start()
-    norm1_t[...] = norm1[...].astype(jnp.float32).T.astype(jnp.bfloat16)
+    send = Sender(*rest[-2:])
+    to_left = send(attended.at[:, give], got_left.at[1], partner)
+    to_branch = send(d_branch, d_both.at[other, :], partner)
+    to_other = send(dkv_other, theirs.at[1], partner)
+    to_norm = send(norm1.at[:, give], got_left.at[0], partner)
+    to_query = send(dq, dqkv.at[other, pl.ds(0, WIDTH)], partner)
+    to_own = send(dkv_own, theirs.at[0], partner)
+    bufs, groups = list(rest[:-2]), []
+    for piece in RS_PIECES + (SMALL,):
+        kind = Reduction if piece is not SMALL else SmallReduction
+        count = len(kind.scratch(piece))
+        source, out = ((grad_qkv, sum_qkv), (grad_out, sum_out), (side, sum_side))[piece[0]]
+        groups.append(kind(piece, pos, send, source, out, bufs[:count]))
+        bufs = bufs[count:]
+    query, value, branch, small = groups
+
+    loads[0].wait()
+    left_t[0, :, own] = transposed(left[0])
+    loads[1].wait()
+    left_t[1, :, own] = transposed(left[1])
+    loads[2].wait()
+    to_left.wait_recv()
+    left_t[1, :, other] = transposed(got_left[1])
+    to_branch.wait_recv()
+
+    @pl.loop(0, 2)
+    def _(i):
+        cols = lanes(i * 512, 512)
+        grad_out[:, :, :, :, cols] = dot_nn(left_t[1], d_both[:, cols]).reshape(SIDE, SIDE, SIDE, 8, 512)
+
+    branch.first()
+    loads[3].wait()
+    loads[4].wait()
     acc[...] = jnp.zeros_like(acc)
-    dqkv[:, pl.ds(0, WIDTH)] = dq[...]
-
-    def project(first):
-        @pl.loop(0, 2)
+
+    def back(first, count):
+        @pl.loop(0, count)
         def _(i):
             cols = lanes(first + i * 512, 512)
-            d = dqkv[:, cols]
-            for half in range(2):
-                part = dot_nn(norm1_t[half * 512 : (half + 1) * 512, :], d)
-                grad_qkv[half, :, :, :, :, cols] = part.reshape(SIDE, SIDE, SIDE, 8, 512).astype(jnp.bfloat16)
-            acc[...] += dot_nt(d, weights[:, cols])
-
-    load.wait()
-    project(0)
-    passed.wait_recv()
-
-    def join(rows, _):
-        dqkv[rows, pl.ds(WIDTH, 2 * WIDTH)] = (
-            dkv_own[rows, :] + landed_kv[rows, :].astype(jnp.float32)
-        ).astype(jnp.bfloat16)
-
-    row_blocks(join)
-    project(1024)
-    project(2048)
+            acc[...] += dot_nt(dqkv[own, cols], weights[:, cols])
+
+    def grads(first, count):
+        @pl.loop(0, count)
+        def _(i):
+            cols = lanes(first + i * 512, 512)
+            grad_qkv[:, :, :, :, cols] = dot_nn(left_t[0], dqkv[:, cols]).reshape(SIDE, SIDE, SIDE, 8, 512)
+
+    back(0, 2)
+    loads[5].wait()
+    loads[6].wait()
+    to_other.wait_recv()
+
+    def join(first, a, b):
+        def add(rows, start):
+            spot = pl.ds(pl.multiple_of(first + start, BLOCK), BLOCK)
+            dqkv[spot, pl.ds(WIDTH, 2 * WIDTH)] = (
+                a[rows, :].astype(jnp.float32) + b[rows, :].astype(jnp.float32)
+            ).astype(jnp.bfloat16)
+
+        row_blocks(add)
+
+    join(0, mine.at[0], theirs.at[1])
+    to_norm.wait_recv()
+    left_t[0, :, other] = transposed(got_left[0])
+    to_query.wait_recv()
+    to_own.wait_recv()
+    join(GROUP, theirs.at[0], mine.at[1])
+    grads(0, 3)
+    query.first()
+    branch.second()
+    grads(1536, 3)
+    value.first()
+    back(1024, 4)
+    query.second()
+    for load in loads[7:]:
+        load.wait()
     sums[...] = jnp.zeros_like(sums)
 
     def norm_back(rows, _):
-        n, inverse = normed(tokens[rows, :].astype(jnp.float32))
+        n, inverse = normed(x[rows, :].astype(jnp.float32))
         u = acc[rows, :]
-        scaled = u * vectors[0:1, :]
+        scaled = u * vec[0:1, :]
         average = jnp.mean(scaled, -1, keepdims=True)
         project = jnp.mean(scaled * n, -1, keepdims=True)
-        grad_tokens[rows, :] = d_resid[rows, :] + inverse * (scaled - average - n * project)
+        grad_tokens[rows, :] = d_res[rows, :] + inverse * (scaled - average - n * project)
         sums[0] += jnp.sum((u * n).reshape(BLOCK // 8, 8, WIDTH), 0)
         sums[1] += jnp.sum(u.reshape(BLOCK // 8, 8, WIDTH), 0)
 
@@ -1058,41 +1163,67 @@
     vector_grads = jnp.where(
         ids == 0,
         jnp.sum(sums[0], 0, keepdims=True),
-        jnp.where(ids == 1, jnp.sum(sums[1], 0, keepdims=True), norm_grads[...]),
+        jnp.where(ids == 1, jnp.sum(sums[1], 0, keepdims=True), norms[...]),
     )
     for half in range(2):
-        rows = grad_router[half * 512 : (half + 1) * 512, :]
+        rows = router[half * 512 : (half + 1) * 512, :]
         side[half, :, :, :, :, pl.ds(0, 128)] = rows.reshape(SIDE, SIDE, SIDE, 8, 128)
-        for x in range(SIDE):
-            block = vector_grads[:, (half * SIDE + x) * 128 : (half * SIDE + x + 1) * 128]
-            side[half, x, :, :, :, pl.ds(128, 128)] = jnp.broadcast_to(block[None, None], (SIDE, SIDE, 8, 128))
-    reduce_all(pos, core, (grad_qkv, grad_out, side), (sum_qkv, sum_out, sum_side), rest)
-    passed.wait_send()
-
-
-def finish(tokens, norm1, vectors, d_resid, dq, dkv_own, dkv_other, grad_out, grad_router, norm_grads, layer):
+        for at in range(SIDE):
+            block = vector_grads[:, (half * SIDE + at) * 128 : (half * SIDE + at + 1) * 128]
+            side[half, at, :, :, :, pl.ds(128, 128)] = jnp.broadcast_to(block[None, None], (SIDE, SIDE, 8, 128))
+    small.open(core, side)
+    value.second()
+    branch.third()
+    small.first()
+    query.third()
+    value.third()
+    small.third()
+    branch.fourth()
+    query.fourth()
+    value.fourth()
+    small.fourth()
+    branch.last()
+    query.last()
+    value.last()
+    small.last()
+    send.close()
+
+
+def finish(tokens, norm1, attended, vectors, d_resid, dq, dkv_own, dkv_other, d_branch, grad_router, norm_grads,
+           layer):
     low, wide = jnp.bfloat16, jnp.float32
     anywhere = pl.BlockSpec(memory_space=pl.ANY)
     vmem = pl.BlockSpec(memory_space=pltpu.VMEM)
-    lead = (2, SIDE, SIDE, SIDE, 8)
-    scratch, copies = reduce_scratch()
+    lead = (SIDE, SIDE, SIDE, 8)
+    scratch, copies = SmallReduction.scratch(SMALL), 6 + SmallReduction.COPIES
+    for piece in RS_PIECES[::-1]:
+        scratch, copies = Reduction.scratch(piece) + scratch, copies + Reduction.COPIES
     return pl.pallas_call(
         finish_kernel,
         out_shape=tuple(jax.ShapeDtypeStruct((8, c), wide) for c in RS_COLS)
         + (jax.ShapeDtypeStruct((GROUP, WIDTH), wide),),
-        in_specs=[vmem] * 10 + [anywhere],
+        in_specs=[anywhere] * 12,
         out_specs=(vmem,) * 4,
         scratch_shapes=[
             pltpu.VMEM((WIDTH, 3 * WIDTH), low),
-            pltpu.VMEM((WIDTH, GROUP), low),
-            pltpu.VMEM((GROUP, 2 * WIDTH), low),
-            pltpu.VMEM((GROUP, 3 * WIDTH), low),
+            pltpu.VMEM((GROUP, WIDTH), low),
+            pltpu.VMEM((GROUP, WIDTH), wide),
+            pltpu.VMEM((2, GROUP, HALF), low),
+            pltpu.VMEM((2, HALF, 2 * GROUP), low),
+            pltpu.VMEM((2, GROUP, 2 * WIDTH), low),
+            pltpu.VMEM((2, GROUP, 2 * WIDTH), low),
+            pltpu.VMEM((2, GROUP, HALF), low),
+            pltpu.VMEM((2 * GROUP, 3 * WIDTH), low),
+            pltpu.VMEM((2 * GROUP, WIDTH), low),
             pltpu.VMEM((GROUP, WIDTH), wide),
             pltpu.VMEM((2, 8, WIDTH), wide),
-            pltpu.VMEM(lead + (3 * WIDTH,), low),
-            pltpu.VMEM(lead + (256,), wide),
-            pltpu.SemaphoreType.DMA,
-            pltpu.SemaphoreType.DMA((2,)),
+            pltpu.VMEM(lead + (3 * WIDTH,), wide),
+            pltpu.VMEM(lead + (WIDTH,), wide),
+            pltpu.VMEM((WIDTH, 128), wide),
+            pltpu.VMEM((8, WIDTH), wide),
+            pltpu.VMEM((8, WIDTH), wide),
+            pltpu.VMEM((2,) + lead + (256,), wide),
+            pltpu.SemaphoreType.DMA((12,)),
             *scratch,
             pltpu.SemaphoreType.DMA((copies,)),
             pltpu.SemaphoreType.DMA((copies,)),
@@ -1101,8 +1232,31 @@
             collective_id=1, has_side_effects=True, vmem_limit_bytes=60 * 1024 * 1024
         ),
         name="finish",
-    )(tokens, norm1, vectors, d_resid, dq, dkv_own, dkv_other, grad_out.reshape(lead + (WIDTH,)), grad_router,
-      norm_grads, layer)
+    )(tokens, norm1, attended, vectors, d_resid, dq, dkv_own, dkv_other, d_branch, grad_router, norm_grads, layer)
+
+
+def results_kernel(sum_qkv, sum_out, side, given_tokens, qkv, out, router, vectors, loss, tokens):
+    place = (lax.axis_index("dp") * 64 + lax.axis_index("expert")) % 16
+    qkv[...] = sum_qkv[...]
+    out[...] = sum_out[...]
+    tokens[...] = given_tokens[...]
+    router[...] = side[:, :64]
+    sums = side[:, 128:256]
+    vectors[...] = pltpu.roll(sums, (16 - place) * 8 % 128, 1)
+    loss[...] = sums[4:5, 0:1] / (sums[5:6, 0:1] * WIDTH)
+
+
+def results(*sums):
+    wide = jnp.float32
+    shapes = ((8, 3072), (8, 1024), (8, 64), (8, 128), (1, 1), (GROUP, WIDTH))
+    vmem = pl.BlockSpec(memory_space=pltpu.VMEM)
+    return pl.pallas_call(
+        results_kernel,
+        out_shape=tuple(jax.ShapeDtypeStruct(s, wide) for s in shapes),
+        in_specs=[vmem] * 4,
+        out_specs=(vmem,) * 6,
+        name="results",
+    )(*sums)
 
 
 def per_device(
@@ -1121,38 +1275,35 @@
     w_down,
 ):
     device = lax.axis_index("dp") * 64 + lax.axis_index("expert")
-    vectors = jnp.tile(jnp.stack([ln1_gain, ln1_bias, ln2_gain, ln2_bias]), (1, 8))
+    vectors = jnp.tile(jnp.stack([ln1_gain, ln1_bias, ln2_gain, ln2_bias] * 2).astype(jnp.float32), (1, 8))
     vectors = jnp.where(jnp.arange(64)[None, :] // 8 == device % 8, vectors, 0)
-    vectors = jnp.concatenate([vectors, jnp.zeros_like(vectors)], 0)
     layer, in_other, down_other = gather_layer(
-        jnp.concatenate([query_key_value_weight, output_weight, router_weight, vectors], 1),
-        w_in[0],
-        w_down[0],
+        query_key_value_weight, output_weight, router_weight, vectors, w_in[0], w_down[0]
     )
     x, parting, qkv, kv_other, attended, norm1, norm2, residual, lse, probs, placing, vectors = forward(
-        tokens[0], teacher[0], routes[0], lengths, layer
+        tokens[0], teacher[0], routes.reshape(1, GROUP), lengths, layer
     )
     y_back, d_back, g1, g2 = experts(x, parting, w_in[0], in_other, w_down[0], down_other)
-    mixed, d_resid, dq, dkv_own, dkv_other, grad_out, grad_router, norm_grads, g1, g2 = backward(
-        y_back, d_back, teacher[0], routes[0], lengths, layer, qkv, kv_other, attended, norm2, residual, lse, probs,
-        placing, vectors, g1, g2,
+    mixed, d_resid, dq, dkv_own, dkv_other, d_branch, grad_router, norm_grads, g1, g2 = backward(
+        y_back, d_back, teacher[0], lengths, layer, qkv, kv_other, norm2, residual, lse, probs, placing, vectors,
+        g1, g2,
     )
-    grad_qkv, grad_out, side, grad_tokens = finish(
-        tokens[0], norm1, vectors, d_resid, dq, dkv_own, dkv_other, grad_out, grad_router, norm_grads, layer
+    sums = finish(
+        tokens[0], norm1, attended, vectors, d_resid, dq, dkv_own, dkv_other, d_branch, grad_router, norm_grads,
+        layer,
     )
-    vector_grads = lax.dynamic_slice(side, (0, 128 + (device % 16) * 8), (4, 8))
-    loss_value = side[4, 128] / (side[5, 128] * WIDTH)
+    grad_qkv, grad_out, grad_router, vector_grads, loss_value, grad_tokens = results(*sums)
     return (
         mixed[None],
-        loss_value,
+        loss_value[0, 0],
         grad_tokens[None],
-        vector_grads[0],
-        vector_grads[1],
+        vector_grads[0, :8],
+        vector_grads[1, :8],
         grad_qkv,
         grad_out,
-        vector_grads[2],
-        vector_grads[3],
-        side[:, :64],
+        vector_grads[2, :8],
+        vector_grads[3, :8],
+        grad_router,
         g1[None],
         g2[None],
     )

time: 240 us -> 207 us (0.86)
  Pallas kernels: 223 us -> 202 us
  local copies, waits for them, and re-layouts: 12.2 us -> 2.25 us
  between operations: 3.81 us -> 1.35 us
    pallas_call x1, Pallas kernels: 61.4 us -> 47 us  [finish(): pl.pallas_call(finish_kernel, out_shape=tuple((jax.ShapeDtypeStruct((8, c...]
    pallas_call x1, Pallas kernels: 42.3 us -> 35.8 us  [gather_layer(): pl.pallas_call(gather_kernel, out_shape=(jax.ShapeDtypeStruct((2, SIDE, S...]
    unnamed x3 -> x0, local copies, waits for them, and re-layouts: 5.22 us -> none
    slice x2 -> x0, local copies, waits for them, and re-layouts: 2.54 us -> none  [the longest x1 1.27 us: per_device(): loss_value = side[4, 128] / (side[5, 128] * WIDTH)]
where the time goes in v2:
time: 207 us
  Pallas kernels  202 us (98%)
  local copies, waits for them, and re-layouts  2.25 us (1%)
    pallas_call x1, Pallas kernels, experts(): pl.pallas_call(expert_kernel, out_shape=(jax.ShapeDtypeStruct((64, 8, WID...  70.8 us
    pallas_call x1, Pallas kernels, finish(): pl.pallas_call(finish_kernel, out_shape=tuple((jax.ShapeDtypeStruct((8, c...  47 us
    pallas_call x1, Pallas kernels, gather_layer(): pl.pallas_call(gather_kernel, out_shape=(jax.ShapeDtypeStruct((2, SIDE, S...  35.8 us
    pallas_call x1, Pallas kernels, backward(): pl.pallas_call(backward_kernel, out_shape=tuple((jax.ShapeDtypeStruct(s,...  24.6 us
    pallas_call x1, Pallas kernels, forward(): pl.pallas_call(forward_kernel, out_shape=tuple((jax.ShapeDtypeStruct(s, t...  21.9 us

profile of v2, /device:TPU:0, one launch (start us, length us, event | category | flops | bytes accessed | tf_op | source)
XLA Modules:
  0.0 206.6 jit_solution(8789816311208070612)
XLA Ops:
  1.3 0.8 stack.23
  2.1 0.1 tile.10
  2.2 0.6 broadcast_select_fusion.vectors
  2.8 35.8 %gather_layer.1 = (bf16[2,4,4,4,8,4224]{5,4,3,2,1,0:T(8,128)(2,1)}, bf16[512,4096]{1,0:T(8,128)(2,1)}, bf16[2048,1024]{1,0:T(8,128)(2,1)}) custom-call(bf16[8,3072]{1,0:T(8,128)(2,1)} %q.1, bf16[8,1024]{1,0:T(8,128)(2,1)} %o.1, bf16[8,64]{1,0:T(8,128)(2,1)} %r.1, f32[8,64]{1,0:T(8,128)} %broadcast_select_fusion.vectors, bf16[512,4096]{1,0:T(8,128)(2,1)} %bitcast.26, ...), custom_call_target="tpu_custom_call" | custom-call | tf_op jit(solution)/shard_map/gather_layer/pallas_call | solution.py:157
  38.6 21.9 %forward.1 = (bf16[64,8,1024]{2,1,0:T(8,128)(2,1)}, bf16[64,8,1152]{2,1,0:T(8,128)(2,1)}, bf16[256,3072]{1,0:T(8,128)(2,1)}, bf16[256,2048]{1,0:T(8,128)(2,1)}, ...) custom-call(bf16[256,1024]{1,0:T(8,128)(2,1)} %bitcast.32, ...), custom_call_target="tpu_custom_call" | custom-call | tf_op jit(solution)/shard_map/forward/pallas_call | solution.py:835
  60.5 70.8 %experts.1 = (bf16[64,8,1024]{2,1,0:T(8,128)(2,1)}, bf16[64,8,1024]{2,1,0:T(8,128)(2,1)}, f32[512,4096]{1,0:T(8,128)}, f32[2048,1024]{1,0:T(8,128)}) custom-call(bf16[64,8,1024]{2,1,0:T(8,128)(2,1)} %get-tuple-element.52.x, bf16[64,8,1152]{2,1,0:T(8,128)(2,1)} %get-tuple-element.53.r, bf16[512,4096]{1,0:T(8,128)(2,1)} %bitcast.27, ...), custom_call_target="tpu_custom_call" | custom-call | tf_op jit(solution)/shard_map/experts/pallas_call | solution.py:584
  131.3 24.6 %backward.1 = (bf16[256,1024]{1,0:T(8,128)(2,1)}, f32[256,1024]{1,0:T(8,128)}, bf16[256,1024]{1,0:T(8,128)(2,1)}, bf16[256,2048]{1,0:T(8,128)(2,1)}, bf16[256,20...) custom-call(bf16[64,8,1024]{2,1,0:T(8,128)(2,1)} %get-tuple-element., ...), custom_call_target="tpu_custom_call" | custom-call | tf_op jit(solution)/shard_map/backward/pallas_call | solution.py:1013
  155.9 47.0 %finish.1 = (f32[8,3072]{1,0:T(8,128)}, f32[8,1024]{1,0:T(8,128)}, f32[8,256]{1,0:T(8,128)}, f32[256,1024]{1,0:T(8,128)}) custom-call(bf16[256,1024]{1,0:T(8,128)(2,1)} %bitcast.33, bf16[256,1024]{1,0:T(8,128)(2,1)} %get-tuple-element.69.norm1, bf16[256,1024]{1,0:T(8,128)(2,1)} %get-tuple-element.70.attended, f32[8,1024]{1,0:T(8,128)} %get-tuple-element.65.vectors, ...), custom_call_target="tpu_custom_call" | custom-call | tf_op jit(solution)/shard_map/finish/pallas_call | solution.py:1201
  202.9 2.4 %results.1 = (f32[8,3072]{1,0:T(8,128)}, f32[8,1024]{1,0:T(8,128)}, f32[8,64]{1,0:T(8,128)}, f32[8,128]{1,0:T(8,128)}, f32[1,1]{1,0:T(1,128)}, /*index=5*/f32[256,1024]{1,0:T(8,128)}) custom-call(f32[8,3072]{1,0:T(8,128)} %get-tuple-element.78.sum_qkv, f32[8,1024]{1,0:T(8,128)} %get-tuple-element.79.sum_out, f32[8,256]{1,0:T(8,128)} %get-tuple-element.80.side, ...), custom_call_target="tpu_custom_call" | custom-call | tf_op jit(solution)/shard_map/results/pallas_call | solution.py:1253
  205.2 1.4 slice_bitcast_fusion
  (2 shorter events, 0.0 us)

commit v3 on v2

--- a/solution.py
+++ b/solution.py
@@ -374,26 +374,67 @@
     return lax.dot_general(a, b, (((0,), (0,)), ((), ())), preferred_element_type=jnp.float32)
 
 
-def to_chips(pos, me, source, target, send_sem, recv_sem):
-    @pl.loop(0, 64)
-    def _(n):
-        there = [(pos[0] + 2 + n // 16) % 4, (pos[1] + 2 + (n // 4) % 4) % 4, (pos[2] + 2 + n % 4) % 4]
-        d = there[0] * 16 + there[1] * 4 + there[2]
-
-        @pl.when(n != 42)
-        def _():
+ALL_STEPS = [((2 + n // 16) % 4, (2 + n // 4 % 4) % 4, (2 + n % 4) % 4) for n in range(64)]
+STEPS = [steps for steps in ALL_STEPS if sum(steps) % 2] + [steps for steps in ALL_STEPS if sum(steps) % 2 == 0]
+OWN = STEPS.index((0, 0, 0))
+
+
+def ring_places(pos):
+    return [[(pos[axis] + step) % 4 * scale for step in range(4)] for axis, scale in enumerate((16, 4, 1))]
+
+
+def away(places, n, sign):
+    return sum(places[axis][sign * step % 4] for axis, step in enumerate(STEPS[n]))
+
+
+def spread(places, source, target, send_sem, recv_sems):
+    for n in range(64):
+        if n != OWN:
+            d = away(places, n, 1)
             pltpu.make_async_remote_copy(
                 src_ref=source.at[d],
+                dst_ref=target.at[n],
+                send_sem=send_sem,
+                recv_sem=recv_sems.at[n // 32],
+                device_id={"expert": d},
+                device_id_type=MESH,
+            ).start()
+
+
+def bring_back(places, me, source, target, send_sem, recv_sem):
+    for n in range(64):
+        if n != OWN:
+            pltpu.make_async_remote_copy(
+                src_ref=source.at[n],
                 dst_ref=target.at[me],
                 send_sem=send_sem,
                 recv_sem=recv_sem,
-                device_id={"expert": d},
+                device_id={"expert": away(places, n, -1)},
                 device_id_type=MESH,
             ).start()
 
 
+def blocks(ref, count, sem):
+    pltpu.make_async_copy(ref.at[pl.ds(0, count)], ref.at[pl.ds(0, count)], sem).wait()
+
+
 def all_but_one(ref, sem):
-    pltpu.make_async_copy(ref.at[pl.ds(0, 63)], ref.at[pl.ds(0, 63)], sem).wait()
+    blocks(ref, 63, sem)
+
+
+def in_turn(count, make, use, first, second):
+    make(0, first)
+
+    @pl.loop(0, count // 2 - 1)
+    def _(i):
+        make(2 * i + 1, second)
+        use(2 * i, first)
+        make(2 * i + 2, first)
+        use(2 * i + 1, second)
+
+    make(count - 1, second)
+    use(count - 2, first)
+    use(count - 1, second)
 
 
 def expert_kernel(
@@ -414,47 +455,64 @@
     ]
     barrier = pltpu.get_barrier_semaphore()
 
-    @pl.loop(1, 64)
-    def _(n):
-        pl.semaphore_signal(barrier, inc=1, device_id={"expert": (me + n) % 64}, device_id_type=MESH)
+    places = ring_places(pos)
+    for n in range(64):
+        if n != OWN:
+            pl.semaphore_signal(barrier, inc=1, device_id={"expert": away(places, n, 1)}, device_id_type=MESH)
 
     pl.semaphore_signal(barrier, inc=1, device_id={"dp": 1 - core}, device_id_type=MESH)
-    own_x = pltpu.make_async_copy(x.at[me], x_in.at[me], own_sems.at[0])
-    own_r = pltpu.make_async_copy(r.at[me], r_in.at[me], own_sems.at[1])
+    own_x = pltpu.make_async_copy(x.at[me], x_in.at[OWN], own_sems.at[0])
+    own_r = pltpu.make_async_copy(r.at[me], r_in.at[OWN], own_sems.at[1])
     own_x.start()
     own_r.start()
     for load in loads:
         load.start()
     pl.semaphore_wait(barrier, 64)
-    to_chips(pos, me, x, x_in, x_sems.at[0], x_sems.at[1])
-    to_chips(pos, me, r, r_in, r_sems.at[0], r_sems.at[1])
-    own_x.wait()
-    all_but_one(x_in, x_sems.at[1])
-    for load in loads:
-        load.wait()
-
-    @pl.loop(0, 8)
-    def _(i):
-        rows = x_in[pl.ds(i * 8, 8)].astype(jnp.float32).reshape(64, WIDTH)
-        xb[pl.ds(pl.multiple_of(i * 64, 64), 64), :] = rows.astype(jnp.bfloat16)
-
+    spread(places, x, x_in, x_sems.at[0], x_sems.at[pl.ds(1, 2)])
+    spread(places, r, r_in, r_sems.at[0], r_sems.at[pl.ds(1, 2)])
     acc[...] = jnp.zeros_like(acc)
-
-    @pl.loop(0, N_TILES)
-    def _(c):
-        cols = pl.ds(pl.multiple_of(c * TILE, TILE), TILE)
-        pre = dot_nn(xb[:, :HALF_IN], w1[0, :, cols]) + dot_nn(xb[:, HALF_IN:], w1[1, :, cols])
-        square = pre * pre
-        t = jnp.tanh(CURVE * pre * (1.0 + 0.044715 * square))
-        low = (0.5 * pre * (1.0 + t)).astype(jnp.bfloat16)
-        act[:, cols] = low
-        slope[:, cols] = 0.5 * (1.0 + t) + (0.5 * CURVE) * pre * (1.0 - t * t) * (1.0 + (3 * 0.044715) * square)
-        half = c // HALF_TILES
-        ff = pl.ds(pl.multiple_of((c % HALF_TILES) * TILE, TILE), TILE)
-        acc[...] += dot_nn(low, w2[half, ff, :])
+    spare = [stage.at[n] for n in range(2)]
+    for part in range(2):
+        rows = pl.ds(part * 256, 256)
+        if part == 0:
+            blocks(x_in, 32, x_sems.at[1])
+        else:
+            own_x.wait()
+            blocks(x_in, 31, x_sems.at[2])
+
+        @pl.loop(0, 4)
+        def _(i):
+            block = x_in[pl.ds(part * 32 + i * 8, 8)].astype(jnp.float32).reshape(64, WIDTH)
+            xb[pl.ds(pl.multiple_of(part * 256 + i * 64, 64), 64), :] = block.astype(jnp.bfloat16)
+
+        if part == 0:
+            loads[0].wait()
+            loads[1].wait()
+
+        def make(c, to):
+            cols = pl.ds(pl.multiple_of(c * TILE, TILE), TILE)
+            to[:256, :] = dot_nn(xb[rows, :HALF_IN], w1[0, :, cols]) + dot_nn(xb[rows, HALF_IN:], w1[1, :, cols])
+
+        def use(c, pre_ref):
+            cols = pl.ds(pl.multiple_of(c * TILE, TILE), TILE)
+            pre = pre_ref[:256, :]
+            square = pre * pre
+            t = jnp.tanh(CURVE * pre * (1.0 + 0.044715 * square))
+            low = (0.5 * pre * (1.0 + t)).astype(jnp.bfloat16)
+            act[rows, cols] = low
+            slope[rows, cols] = 0.5 * (1.0 + t) + (0.5 * CURVE) * pre * (1.0 - t * t) * (1.0 + (3 * 0.044715) * square)
+            half = c // HALF_TILES
+            ff = pl.ds(pl.multiple_of((c % HALF_TILES) * TILE, TILE), TILE)
+            acc[rows, :] += dot_nn(low, w2[half, ff, :])
+
+        if part == 0:
+            loads[2].wait()
+            loads[3].wait()
+        in_turn(N_TILES, make, use, *spare)
 
     own_r.wait()
-    all_but_one(r_in, r_sems.at[1])
+    blocks(r_in, 32, r_sems.at[1])
+    blocks(r_in, 31, r_sems.at[2])
 
     @pl.loop(0, 8)
     def _(i):
@@ -467,21 +525,23 @@
         valid = parted[:, WIDTH + 2 : WIDTH + 3]
         d_exp[rows, :] = (gate * valid * (parted[:, :WIDTH] + gate * out)).astype(jnp.bfloat16)
 
-    own_y = pltpu.make_async_copy(out_rows.at[me], y_back.at[me], own_sems.at[2])
+    own_y = pltpu.make_async_copy(out_rows.at[OWN], y_back.at[me], own_sems.at[2])
     own_y.start()
-    to_chips(pos, me, out_rows, y_back, y_sems.at[0], y_sems.at[1])
+    bring_back(places, me, out_rows, y_back, y_sems.at[0], y_sems.at[1])
     acc[...] = jnp.zeros_like(acc)
 
-    @pl.loop(0, N_TILES)
-    def _(c):
+    def make_back(c, to):
+        ff = pl.ds(pl.multiple_of((c % HALF_TILES) * TILE, TILE), TILE)
+        to[...] = dot_nt(d_exp[...], w2[c // HALF_TILES, ff, :])
+
+    def use_back(c, d_act):
         cols = pl.ds(pl.multiple_of(c * TILE, TILE), TILE)
-        half = c // HALF_TILES
-        ff = pl.ds(pl.multiple_of((c % HALF_TILES) * TILE, TILE), TILE)
-        d_act = dot_nt(d_exp[...], w2[half, ff, :])
-        low = (slope[:, cols] * d_act).astype(jnp.bfloat16)
+        low = (slope[:, cols] * d_act[...]).astype(jnp.bfloat16)
         d_pre[:, cols] = low
         acc[:, :HALF_IN] += dot_nt(low, w1[0, :, cols])
         acc[:, HALF_IN:] += dot_nt(low, w1[1, :, cols])
+
+    in_turn(N_TILES, make_back, use_back, *spare)
 
     own_y.wait()
     all_but_one(out_rows, y_sems.at[0])
@@ -491,9 +551,9 @@
         rows = pl.ds(pl.multiple_of(i * 64, 64), 64)
         out_rows[pl.ds(i * 8, 8)] = acc[rows, :].reshape(8, 8, WIDTH).astype(jnp.bfloat16)
 
-    own_d = pltpu.make_async_copy(out_rows.at[me], d_back.at[me], own_sems.at[3])
+    own_d = pltpu.make_async_copy(out_rows.at[OWN], d_back.at[me], own_sems.at[3])
     own_d.start()
-    to_chips(pos, me, out_rows, d_back, d_sems.at[0], d_sems.at[1])
+    bring_back(places, me, out_rows, d_back, d_sems.at[0], d_sems.at[1])
 
     xt[...] = xb[...].astype(jnp.float32).T.astype(jnp.bfloat16)
 
@@ -522,13 +582,16 @@
         sent2[c] = dot_tn(act[:, cols], d_exp[...]).astype(jnp.bfloat16)
         passed(sent2, got2, c, N_TILES).start()
 
+    def made(slot, columns):
+        return slope.at[:, pl.ds(pl.multiple_of(slot * WIDTH, WIDTH), columns)]
+
     def out1(c, slot):
         cols = pl.ds(pl.multiple_of(c * TILE, TILE), TILE)
-        return pltpu.make_async_copy(stage.at[slot, :, pl.ds(0, TILE)], g1.at[:, cols], out_sems.at[slot])
+        return pltpu.make_async_copy(made(slot, TILE), g1.at[:, cols], out_sems.at[slot])
 
     def out2(c, slot):
         rows = pl.ds(pl.multiple_of(c * TILE, TILE), TILE)
-        return pltpu.make_async_copy(stage.at[slot], g2.at[rows, :], out_sems.at[slot])
+        return pltpu.make_async_copy(made(slot, WIDTH), g2.at[rows, :], out_sems.at[slot])
 
     @pl.loop(0, N_TILES)
     def _(c):
@@ -540,7 +603,7 @@
             out1(c - 2, slot).wait()
 
         passed(sent1, got1, c, 0).wait_recv()
-        stage[slot, :, pl.ds(0, TILE)] = dot_nn(in_rows(core), d_pre[:, cols]) + got1[c].astype(jnp.float32)
+        made(slot, TILE)[...] = dot_nn(in_rows(core), d_pre[:, cols]) + got1[c].astype(jnp.float32)
         out1(c, slot).start()
 
     out1(N_TILES - 2, 0).wait()
@@ -556,7 +619,7 @@
             out2(c - 2, slot).wait()
 
         passed(sent2, got2, c, N_TILES).wait_recv()
-        stage[slot] = dot_tn(act[:, cols], d_exp[...]) + got2[c].astype(jnp.float32)
+        made(slot, WIDTH)[...] = dot_tn(act[:, cols], d_exp[...]) + got2[c].astype(jnp.float32)
         out2(c, slot).start()
 
     out2(HALF_TILES - 2, 0).wait()
@@ -608,10 +671,10 @@
             pltpu.VMEM((HALF_TILES, TILE, WIDTH), low),
             pltpu.VMEM((N_TILES, HALF_IN, TILE), low),
             pltpu.VMEM((HALF_TILES, TILE, WIDTH), low),
-            pltpu.VMEM((2, HALF_IN, WIDTH), wide),
+            pltpu.VMEM((2, ROWS, TILE), wide),
             pltpu.SemaphoreType.DMA((4,)),
-            pltpu.SemaphoreType.DMA((2,)),
-            pltpu.SemaphoreType.DMA((2,)),
+            pltpu.SemaphoreType.DMA((3,)),
+            pltpu.SemaphoreType.DMA((3,)),
             pltpu.SemaphoreType.DMA((2,)),
             pltpu.SemaphoreType.DMA((2,)),
             pltpu.SemaphoreType.DMA((4,)),
@@ -712,7 +775,7 @@
         n, _ = normed(tokens[rows, :].astype(jnp.float32))
         norm1[rows, :] = (n * vectors[0:1, :] + vectors[1:2, :]).astype(jnp.bfloat16)
 
-    row_blocks(first_norm)
+    row_blocks(first_norm, 64)
     save(norm1, norm1_out)
 
     def project(block):
@@ -780,7 +843,7 @@
         norm2[rows, :] = (n * vectors[2:3, :] + vectors[3:4, :]).astype(jnp.bfloat16)
         parted[rows, :WIDTH] = (residual[rows, :] - teacher[rows, :].astype(jnp.float32)).astype(jnp.bfloat16)
 
-    row_blocks(second_norm)
+    row_blocks(second_norm, 64)
     save(norm2, norm2_out)
     logits = dot_nn(norm2[...], weights[:, pl.ds(4096, 128)])
     ids = lane_ids(GROUP, 128)
@@ -802,10 +865,10 @@
     placing[...] = (lane_ids(GROUP, SLOTS).astype(jnp.float32) == slot).astype(jnp.float32).astype(jnp.bfloat16)
     save(placing, placing_out)
     for half in range(2):
-        spread = placing[:, half * 256 : (half + 1) * 256].astype(jnp.float32).T.astype(jnp.bfloat16)
-        sent = dot_nn(spread, norm2[...])
+        to_slots = placing[:, half * 256 : (half + 1) * 256].astype(jnp.float32).T.astype(jnp.bfloat16)
+        sent = dot_nn(to_slots, norm2[...])
         packed_x[half * 32 : (half + 1) * 32] = sent.reshape(32, 8, WIDTH).astype(jnp.bfloat16)
-        sent = dot_nn(spread, parted[...])
+        sent = dot_nn(to_slots, parted[...])
         packed_r[half * 32 : (half + 1) * 32] = sent.reshape(32, 8, WIDTH + EXTRA).astype(jnp.bfloat16)
     save(packed_x, x_out)
     save(packed_r, parting_out)
@@ -864,14 +927,34 @@
 
 
 def backward_kernel(
-    y_back, d_back, teacher, lengths, layer, qkv, kv_other, norm2, residual, lse, probs,
-    placing, vectors, g1, g2,
-    mixed_out, d_resid, dq, dkv_own, dkv_other, d_branch, grad_router, norm_grads, g1_out, g2_out,
+    y_back, d_back, teacher_in, lengths, layer, qkv_in, kv_other_in, norm2_in, residual_in, lse_in, probs_in,
+    placing_in, vectors_in, g1, g2,
+    mixed_to, d_resid_to, dq_to, dkv_own_to, dkv_other_to, d_branch_to, grad_router_to, norm_grads_to, g1_out, g2_out,
+    y_in, d_in, teacher, qkv, kv_other, norm2, residual, lse, probs, placing, vectors,
+    mixed_out, d_resid, dq, dkv_own, dkv_other, d_branch, grad_router, norm_grads,
     w_out, w_router, eo, dn, sums, d_attended, logit_parts,
-    held1, held2, pass_sems, load_sems,
+    held1, held2, pass_sems, load_sems, out_sems,
 ):
     core = lax.axis_index("dp")
     length = lengths[0]
+    spans = (
+        (y_back, y_in),
+        (placing_in, placing),
+        (d_back, d_in),
+        (probs_in, probs),
+        (residual_in, residual),
+        (teacher_in, teacher),
+        (layer.at[:, pl.ds(4096, 128)], w_router),
+        (norm2_in, norm2),
+        (vectors_in, vectors),
+        (layer.at[:, pl.ds(3072, 1024)], w_out),
+        (qkv_in, qkv),
+        (kv_other_in, kv_other),
+        (lse_in, lse),
+    )
+    loads = [pltpu.make_async_copy(src, dst, load_sems.at[n]) for n, (src, dst) in enumerate(spans)]
+    for load in loads:
+        load.start()
     passing = [
         pltpu.make_async_copy(g1, held1, pass_sems.at[0]),
         pltpu.make_async_copy(g2, held2, pass_sems.at[1]),
@@ -880,17 +963,23 @@
         pltpu.make_async_copy(held1, g1_out, pass_sems.at[2]),
         pltpu.make_async_copy(held2, g2_out, pass_sems.at[3]),
     ]
-    loads = [
-        pltpu.make_async_copy(layer.at[:, pl.ds(3072, 1024)], w_out, load_sems.at[0]),
-        pltpu.make_async_copy(layer.at[:, pl.ds(4096, 128)], w_router, load_sems.at[1]),
-    ]
-    for copy in loads + passing:
+    outs = []
+
+    def save(src, dst):
+        copy = pltpu.make_async_copy(src, dst, out_sems.at[len(outs)])
         copy.start()
-    rows_back = y_back[...].astype(jnp.float32).reshape(SLOTS, WIDTH).astype(jnp.bfloat16)
+        outs.append(copy)
+
+    loads[0].wait()
+    loads[1].wait()
+    rows_back = y_in[...].astype(jnp.float32).reshape(SLOTS, WIDTH).astype(jnp.bfloat16)
     eo[...] = dot_nn(placing[...], rows_back)
-    rows_back = d_back[...].astype(jnp.float32).reshape(SLOTS, WIDTH).astype(jnp.bfloat16)
+    loads[2].wait()
+    rows_back = d_in[...].astype(jnp.float32).reshape(SLOTS, WIDTH).astype(jnp.bfloat16)
     dn[...] = dot_nn(placing[...], rows_back)
     sums[...] = jnp.zeros_like(sums)
+    for load in loads[3:6]:
+        load.wait()
 
     def loss(rows, first):
         ids = lane_ids(BLOCK, 128)
@@ -913,8 +1002,11 @@
         sums[0] += square
 
     row_blocks(loss)
-    loads[0].wait()
-    loads[1].wait()
+    save(mixed_out, mixed_to)
+    for load in loads[6:9]:
+        load.wait()
+    for copy in passing:
+        copy.start()
     dn[...] += dot_nt(logit_parts[:, :128], w_router[...]) + dot_nt(logit_parts[:, 128:], w_router[...])
     both = dot_tn(norm2[...], logit_parts[...])
     grad_router[...] = both[:, :128] + both[:, 128:]
@@ -932,6 +1024,9 @@
         sums[2] += jnp.sum(u.reshape(BLOCK // 8, 8, WIDTH), 0)
 
     row_blocks(norm_back)
+    save(grad_router, grad_router_to)
+    save(d_resid, d_resid_to)
+    save(d_branch, d_branch_to)
     valid_all = jnp.clip(length - core * GROUP, 0, GROUP).astype(jnp.float32)
     ids = row_ids(8, WIDTH)
     square = jnp.sum(sums[0])
@@ -944,6 +1039,8 @@
             jnp.where(ids == 4, square, jnp.where(ids == 5, valid_all, 0.0)),
         ),
     )
+    save(norm_grads, norm_grads_to)
+    loads[9].wait()
 
     @pl.loop(0, 2)
     def _(i):
@@ -952,12 +1049,17 @@
         d_attended[:, cols] = dot_nt(d_branch[...], w_out[rows, :]).astype(jnp.bfloat16)
 
     own, other = allowed_keys(core, length)
-    for copy, onward in zip(passing, passed_on):
-        copy.wait()
-        onward.start()
+    for load in loads[10:]:
+        load.wait()
 
     @pl.loop(0, PAIRS)
     def _(pair):
+        @pl.when(pair == 3)
+        def _():
+            for copy, onward in zip(passing, passed_on):
+                copy.wait()
+                onward.start()
+
         q, do = qkv[:, lanes(pair * 128, 128)], d_attended[:, lanes(pair * 128, 128)]
         k_own, v_own = qkv[:, lanes(1024 + pair * 128, 128)], qkv[:, lanes(2048 + pair * 128, 128)]
         k_other, v_other = kv_other[:, lanes(pair * 128, 128)], kv_other[:, lanes(1024 + pair * 128, 128)]
@@ -989,15 +1091,17 @@
         dkv_other[:, lanes(pair * 128, 128)] = (d_k_other * 0.125).astype(jnp.bfloat16)
         dkv_other[:, lanes(1024 + pair * 128, 128)] = d_v_other.astype(jnp.bfloat16)
 
-    for onward in passed_on:
-        onward.wait()
+    save(dkv_other, dkv_other_to)
+    save(dkv_own, dkv_own_to)
+    save(dq, dq_to)
+    for copy in passed_on + outs:
+        copy.wait()
 
 
 def backward(y_back, d_back, teacher, lengths, layer, qkv, kv_other, norm2, residual, lse, probs,
              placing, vectors, g1, g2):
     low, wide = jnp.bfloat16, jnp.float32
     anywhere = pl.BlockSpec(memory_space=pl.ANY)
-    vmem = pl.BlockSpec(memory_space=pltpu.VMEM)
     made = [
         ((GROUP, WIDTH), low),
         ((GROUP, WIDTH), wide),
@@ -1013,9 +1117,12 @@
     return pl.pallas_call(
         backward_kernel,
         out_shape=tuple(jax.ShapeDtypeStruct(s, t) for s, t in made),
-        in_specs=[vmem, vmem, vmem, pl.BlockSpec(memory_space=pltpu.SMEM), anywhere] + [vmem] * 8 + [anywhere] * 2,
-        out_specs=(vmem,) * 8 + (anywhere,) * 2,
+        in_specs=[anywhere] * 3 + [pl.BlockSpec(memory_space=pltpu.SMEM)] + [anywhere] * 11,
+        out_specs=(anywhere,) * 10,
         scratch_shapes=[
+            *[pltpu.VMEM(t.shape, t.dtype) for t in (y_back, d_back, teacher, qkv, kv_other, norm2, residual)],
+            *[pltpu.VMEM(t.shape, t.dtype) for t in (lse, probs, placing, vectors)],
+            *[pltpu.VMEM(shape, kind) for shape, kind in made[:8]],
             pltpu.VMEM((WIDTH, WIDTH), low),
             pltpu.VMEM((WIDTH, 128), low),
             pltpu.VMEM((GROUP, WIDTH), wide),
@@ -1026,7 +1133,8 @@
             pltpu.VMEM(g1.shape, wide),
             pltpu.VMEM(g2.shape, wide),
             pltpu.SemaphoreType.DMA((4,)),
-            pltpu.SemaphoreType.DMA((2,)),
+            pltpu.SemaphoreType.DMA((13,)),
+            pltpu.SemaphoreType.DMA((8,)),
         ],
         compiler_params=pltpu.CompilerParams(vmem_limit_bytes=56 * 1024 * 1024),
         name="backward",

time: 207 us -> 191 us (0.923)
  Pallas kernels: 202 us -> 187 us
    pallas_call x1, Pallas kernels: 70.8 us -> 64.9 us  [experts(): pl.pallas_call(expert_kernel, out_shape=(jax.ShapeDtypeStruct((64, 8, WID...]
    pallas_call x1, Pallas kernels: 47 us -> 42.3 us  [finish(): pl.pallas_call(finish_kernel, out_shape=tuple((jax.ShapeDtypeStruct((8, c...]
    pallas_call x1, Pallas kernels: 24.6 us -> 21 us  [backward(): pl.pallas_call(backward_kernel, out_shape=tuple((jax.ShapeDtypeStruct(s,...]
where the time goes in v3:
time: 191 us
  Pallas kernels  187 us (98%)
  local copies, waits for them, and re-layouts  2.25 us (1%)
    pallas_call x1, Pallas kernels, experts(): pl.pallas_call(expert_kernel, out_shape=(jax.ShapeDtypeStruct((64, 8, WID...  64.9 us
    pallas_call x1, Pallas kernels, finish(): pl.pallas_call(finish_kernel, out_shape=tuple((jax.ShapeDtypeStruct((8, c...  42.3 us
    pallas_call x1, Pallas kernels, gather_layer(): pl.pallas_call(gather_kernel, out_shape=(jax.ShapeDtypeStruct((2, SIDE, S...  35.8 us
    pallas_call x1, Pallas kernels, backward(): pl.pallas_call(backward_kernel, out_shape=tuple((jax.ShapeDtypeStruct(s,...  21 us
    pallas_call x1, Pallas kernels, forward(): pl.pallas_call(forward_kernel, out_shape=tuple((jax.ShapeDtypeStruct(s, t...  20.4 us

profile of v3, /device:TPU:0, one launch (start us, length us, event | category | flops | bytes accessed | tf_op | source)
XLA Modules:
  0.0 191.1 jit_solution(7769189930311377485)
XLA Ops:
  1.3 0.8 stack.23
  2.1 0.1 tile.10
  2.2 0.6 broadcast_select_fusion.vectors
  2.8 35.8 %gather_layer.1 = (bf16[2,4,4,4,8,4224]{5,4,3,2,1,0:T(8,128)(2,1)}, bf16[512,4096]{1,0:T(8,128)(2,1)}, bf16[2048,1024]{1,0:T(8,128)(2,1)}) custom-call(bf16[8,3072]{1,0:T(8,128)(2,1)} %q.1, bf16[8,1024]{1,0:T(8,128)(2,1)} %o.1, bf16[8,64]{1,0:T(8,128)(2,1)} %r.1, f32[8,64]{1,0:T(8,128)} %broadcast_select_fusion.vectors, bf16[512,4096]{1,0:T(8,128)(2,1)} %bitcast.26, ...), custom_call_target="tpu_custom_call" | custom-call | tf_op jit(solution)/shard_map/gather_layer/pallas_call | solution.py:157
  38.6 20.4 %forward.1 = (bf16[64,8,1024]{2,1,0:T(8,128)(2,1)}, bf16[64,8,1152]{2,1,0:T(8,128)(2,1)}, bf16[256,3072]{1,0:T(8,128)(2,1)}, bf16[256,2048]{1,0:T(8,128)(2,1)}, ...) custom-call(bf16[256,1024]{1,0:T(8,128)(2,1)} %bitcast.32, ...), custom_call_target="tpu_custom_call" | custom-call | tf_op jit(solution)/shard_map/forward/pallas_call | solution.py:898
  59.0 64.9 %experts.1 = (bf16[64,8,1024]{2,1,0:T(8,128)(2,1)}, bf16[64,8,1024]{2,1,0:T(8,128)(2,1)}, f32[512,4096]{1,0:T(8,128)}, f32[2048,1024]{1,0:T(8,128)}) custom-call(bf16[64,8,1024]{2,1,0:T(8,128)(2,1)} %get-tuple-element.52.x, bf16[64,8,1152]{2,1,0:T(8,128)(2,1)} %get-tuple-element.53.r, bf16[512,4096]{1,0:T(8,128)(2,1)} %bitcast.27, ...), custom_call_target="tpu_custom_call" | custom-call | tf_op jit(solution)/shard_map/experts/pallas_call | solution.py:647
  123.9 21.0 %backward.1 = (bf16[256,1024]{1,0:T(8,128)(2,1)}, f32[256,1024]{1,0:T(8,128)}, bf16[256,1024]{1,0:T(8,128)(2,1)}, bf16[256,2048]{1,0:T(8,128)(2,1)}, bf16[256,20...) custom-call(bf16[64,8,1024]{2,1,0:T(8,128)(2,1)} %get-tuple-element., ...), custom_call_target="tpu_custom_call" | custom-call | tf_op jit(solution)/shard_map/backward/pallas_call | solution.py:1117
  145.0 42.3 %finish.1 = (f32[8,3072]{1,0:T(8,128)}, f32[8,1024]{1,0:T(8,128)}, f32[8,256]{1,0:T(8,128)}, f32[256,1024]{1,0:T(8,128)}) custom-call(bf16[256,1024]{1,0:T(8,128)(2,1)} %bitcast.33, bf16[256,1024]{1,0:T(8,128)(2,1)} %get-tuple-element.69.norm1, bf16[256,1024]{1,0:T(8,128)(2,1)} %get-tuple-element.70.attended, ...), custom_call_target="tpu_custom_call" | custom-call | tf_op jit(solution)/shard_map/finish/pallas_call | solution.py:1309
  187.3 2.4 %results.1 = (f32[8,3072]{1,0:T(8,128)}, f32[8,1024]{1,0:T(8,128)}, f32[8,64]{1,0:T(8,128)}, f32[8,128]{1,0:T(8,128)}, f32[1,1]{1,0:T(1,128)}, /*index=5*/f32[256,1024]{1,0:T(8,128)}) custom-call(f32[8,3072]{1,0:T(8,128)} %get-tuple-element.78.sum_qkv, f32[8,1024]{1,0:T(8,128)} %get-tuple-element.79.sum_out, f32[8,256]{1,0:T(8,128)} %get-tuple-element.80.side, ...), custom_call_target="tpu_custom_call" | custom-call | tf_op jit(solution)/shard_map/results/pallas_call | solution.py:1361
  189.7 1.4 slice_bitcast_fusion
  (2 shorter events, 0.0 us)

commit v4 on v3

--- a/solution.py
+++ b/solution.py
@@ -61,14 +61,23 @@
 
 
 def gather_kernel(
-    q, o, r, vectors, w_in, w_down, whole, in_other, down_other, shard, own_sem, send_sems, recv_sems
+    q, o, r, gain_one, bias_one, gain_two, bias_two, w_in, w_down, whole, in_other, down_other, shard, own_sem, send_sems, recv_sems
 ):
     pos = coords()
     core = lax.axis_index("dp")
     partner = {"dp": 1 - core}
     shard[:, :3072] = q[...]
     shard[:, 3072:4096] = o[...]
-    shard[:, 4096:] = jnp.concatenate([r[...].astype(jnp.float32), vectors[...]], 1).astype(jnp.bfloat16)
+    lane = lax.broadcasted_iota(jnp.int32, (8, 64), 1)
+    row = lax.broadcasted_iota(jnp.int32, (8, 64), 0)
+    here = (lane == row + lax.axis_index("expert") % 8 * 8).astype(jnp.float32)
+    vectors = jnp.zeros((8, 64), jnp.float32)
+    same = (lax.broadcasted_iota(jnp.int32, (8, 8), 0) == lax.broadcasted_iota(jnp.int32, (8, 8), 1)).astype(jnp.float32)
+    for n, vector in enumerate((gain_one, bias_one, gain_two, bias_two)):
+        column = jnp.sum(same * vector[...].astype(jnp.float32), 1, keepdims=True)
+        spread_out = jnp.sum(here * column, 0, keepdims=True)
+        vectors = jnp.where(row == n, spread_out, vectors)
+    shard[:, 4096:] = jnp.concatenate([r[...].astype(jnp.float32), vectors], 1).astype(jnp.bfloat16)
     own = pltpu.make_async_copy(shard, whole.at[(core, *pos)], own_sem)
     own.start()
     greet(pos, core)
@@ -161,7 +170,7 @@
             jax.ShapeDtypeStruct(w_in.shape, w_in.dtype),
             jax.ShapeDtypeStruct(w_down.shape, w_down.dtype),
         ),
-        in_specs=[vmem] * 4 + [anywhere] * 2,
+        in_specs=[vmem] * 7 + [anywhere] * 2,
         out_specs=(anywhere,) * 3,
         scratch_shapes=[
             pltpu.VMEM((8, AG_COLS), jnp.bfloat16),
@@ -171,7 +180,7 @@
         ],
         compiler_params=pltpu.CompilerParams(collective_id=0, has_side_effects=True),
         name="gather_layer",
-    )(q, o, r, vectors, w_in, w_down)
+    )(q, o, r, *vectors, w_in, w_down)
     return whole.reshape(1024, AG_COLS), in_other, down_other
 
 
@@ -730,8 +739,8 @@
 
 
 def head_scores(q, k_own, k_other, own, other):
-    s_own = jnp.where(own, dot_nt(q, k_own) * 0.125, MASKED)
-    s_other = jnp.where(other, dot_nt(q, k_other) * 0.125, MASKED)
+    s_own = jnp.where(own, dot_nt(q, k_own), MASKED)
+    s_other = jnp.where(other, dot_nt(q, k_other), MASKED)
     return s_own, s_other
 
 
@@ -761,6 +770,11 @@
     barrier = pltpu.get_barrier_semaphore()
     pl.semaphore_signal(barrier, inc=1, device_id={"dp": 1 - core}, device_id_type=MESH)
 
+    def statistics(rows, _):
+        n, _ = normed(tokens[rows, :].astype(jnp.float32))
+        residual[rows, :] = n
+
+    row_blocks(statistics, 64)
     loads[0].wait()
     for g in range(16):
         part = weights[pl.ds(g * 64, 64), pl.ds(4096, 128)].astype(jnp.float32)
@@ -772,8 +786,7 @@
     route = jnp.sum(routes.astype(jnp.float32), -1, keepdims=True)
 
     def first_norm(rows, _):
-        n, _ = normed(tokens[rows, :].astype(jnp.float32))
-        norm1[rows, :] = (n * vectors[0:1, :] + vectors[1:2, :]).astype(jnp.bfloat16)
+        norm1[rows, :] = (residual[rows, :] * vectors[0:1, :] + vectors[1:2, :]).astype(jnp.bfloat16)
 
     row_blocks(first_norm, 64)
     save(norm1, norm1_out)
@@ -809,7 +822,7 @@
 
     @pl.loop(0, PAIRS)
     def _(pair):
-        q = qkv[:, lanes(pair * 128, 128)]
+        q = qkv[:, lanes(pair * 128, 128)] * 0.125
         k_own, v_own = qkv[:, lanes(1024 + pair * 128, 128)], qkv[:, lanes(2048 + pair * 128, 128)]
         k_other, v_other = kv_other[:, lanes(pair * 128, 128)], kv_other[:, lanes(1024 + pair * 128, 128)]
         left = lane_ids(GROUP, 128) < 64
@@ -820,9 +833,8 @@
             top = jnp.max(jnp.maximum(s_own, s_other), -1, keepdims=True)
             e_own, e_other = jnp.exp(s_own - top), jnp.exp(s_other - top)
             total = jnp.sum(e_own + e_other, -1, keepdims=True)
-            scale = 1.0 / total
-            p_own, p_other = (e_own * scale).astype(jnp.bfloat16), (e_other * scale).astype(jnp.bfloat16)
-            results.append(dot_nn(p_own, v_own) + dot_nn(p_other, v_other))
+            e_own, e_other = e_own.astype(jnp.bfloat16), e_other.astype(jnp.bfloat16)
+            results.append((dot_nn(e_own, v_own) + dot_nn(e_other, v_other)) * (1.0 / total))
             lse[...] = jnp.where(lane_ids(GROUP, 128) == pair * 2 + h, top + jnp.log(total), lse[...])
         attended[:, lanes(pair * 128, 128)] = jnp.where(left, results[0], results[1]).astype(jnp.bfloat16)
 
@@ -1067,7 +1079,7 @@
         zero = jnp.zeros_like(q)
         parts = []
         for h in range(2):
-            qh = jnp.where(left == (h == 0), q, zero)
+            qh = jnp.where(left == (h == 0), q * 0.125, zero)
             doh = jnp.where(left == (h == 0), do, zero)
             s_own, s_other = head_scores(qh, k_own, k_other, own, other)
             log_total = jnp.sum(jnp.where(lane_ids(GROUP, 128) == pair * 2 + h, lse[...], 0.0), -1, keepdims=True)
@@ -1181,9 +1193,9 @@
     send = Sender(*rest[-2:])
     to_left = send(attended.at[:, give], got_left.at[1], partner)
     to_branch = send(d_branch, d_both.at[other, :], partner)
-    to_other = send(dkv_other, theirs.at[1], partner)
     to_norm = send(norm1.at[:, give], got_left.at[0], partner)
     to_query = send(dq, dqkv.at[other, pl.ds(0, WIDTH)], partner)
+    to_other = send(dkv_other, theirs.at[1], partner)
     to_own = send(dkv_own, theirs.at[0], partner)
     bufs, groups = list(rest[:-2]), []
     for piece in RS_PIECES + (SMALL,):
@@ -1225,10 +1237,8 @@
             cols = lanes(first + i * 512, 512)
             grad_qkv[:, :, :, :, cols] = dot_nn(left_t[0], dqkv[:, cols]).reshape(SIDE, SIDE, SIDE, 8, 512)
 
-    back(0, 2)
     loads[5].wait()
     loads[6].wait()
-    to_other.wait_recv()
 
     def join(first, a, b):
         def add(rows, start):
@@ -1239,10 +1249,11 @@
 
         row_blocks(add)
 
-    join(0, mine.at[0], theirs.at[1])
     to_norm.wait_recv()
     left_t[0, :, other] = transposed(got_left[0])
     to_query.wait_recv()
+    to_other.wait_recv()
+    join(0, mine.at[0], theirs.at[1])
     to_own.wait_recv()
     join(GROUP, theirs.at[0], mine.at[1])
     grads(0, 3)
@@ -1250,7 +1261,7 @@
     branch.second()
     grads(1536, 3)
     value.first()
-    back(1024, 4)
+    back(0, 6)
     query.second()
     for load in loads[7:]:
         load.wait()
@@ -1343,26 +1354,29 @@
     )(tokens, norm1, attended, vectors, d_resid, dq, dkv_own, dkv_other, d_branch, grad_router, norm_grads, layer)
 
 
-def results_kernel(sum_qkv, sum_out, side, given_tokens, qkv, out, router, vectors, loss, tokens):
+def results_kernel(sum_qkv, sum_out, side, given_tokens, qkv, out, router, *rest):
+    vectors, (loss, tokens) = rest[:4], rest[4:]
     place = (lax.axis_index("dp") * 64 + lax.axis_index("expert")) % 16
     qkv[...] = sum_qkv[...]
     out[...] = sum_out[...]
     tokens[...] = given_tokens[...]
     router[...] = side[:, :64]
     sums = side[:, 128:256]
-    vectors[...] = pltpu.roll(sums, (16 - place) * 8 % 128, 1)
+    sums_here = pltpu.roll(sums, (16 - place) * 8 % 128, 1)
+    for n in range(4):
+        vectors[n][...] = sums_here[n : n + 1, :8]
     loss[...] = sums[4:5, 0:1] / (sums[5:6, 0:1] * WIDTH)
 
 
 def results(*sums):
     wide = jnp.float32
-    shapes = ((8, 3072), (8, 1024), (8, 64), (8, 128), (1, 1), (GROUP, WIDTH))
+    shapes = ((8, 3072), (8, 1024), (8, 64), (1, 8), (1, 8), (1, 8), (1, 8), (1, 1), (GROUP, WIDTH))
     vmem = pl.BlockSpec(memory_space=pltpu.VMEM)
     return pl.pallas_call(
         results_kernel,
         out_shape=tuple(jax.ShapeDtypeStruct(s, wide) for s in shapes),
         in_specs=[vmem] * 4,
-        out_specs=(vmem,) * 6,
+        out_specs=(vmem,) * 9,
         name="results",
     )(*sums)
 
@@ -1382,9 +1396,7 @@
     w_in,
     w_down,
 ):
-    device = lax.axis_index("dp") * 64 + lax.axis_index("expert")
-    vectors = jnp.tile(jnp.stack([ln1_gain, ln1_bias, ln2_gain, ln2_bias] * 2).astype(jnp.float32), (1, 8))
-    vectors = jnp.where(jnp.arange(64)[None, :] // 8 == device % 8, vectors, 0)
+    vectors = [vector.reshape(1, 8) for vector in (ln1_gain, ln1_bias, ln2_gain, ln2_bias)]
     layer, in_other, down_other = gather_layer(
         query_key_value_weight, output_weight, router_weight, vectors, w_in[0], w_down[0]
     )
@@ -1400,17 +1412,17 @@
         tokens[0], norm1, attended, vectors, d_resid, dq, dkv_own, dkv_other, d_branch, grad_router, norm_grads,
         layer,
     )
-    grad_qkv, grad_out, grad_router, vector_grads, loss_value, grad_tokens = results(*sums)
+    grad_qkv, grad_out, grad_router, *vector_grads, loss_value, grad_tokens = results(*sums)
     return (
         mixed[None],
         loss_value[0, 0],
         grad_tokens[None],
-        vector_grads[0, :8],
-        vector_grads[1, :8],
+        vector_grads[0][0],
+        vector_grads[1][0],
         grad_qkv,
         grad_out,
-        vector_grads[2, :8],
-        vector_grads[3, :8],
+        vector_grads[2][0],
+        vector_grads[3][0],
         grad_router,
         g1[None],
         g2[None],

time: 191 us -> 186 us (0.974)
  local copies, waits for them, and re-layouts: 2.25 us -> 0 us
  Pallas kernels: 187 us -> 185 us
    pallas_call x1, Pallas kernels: 20.4 us -> 18.1 us  [forward(): pl.pallas_call(forward_kernel, out_shape=tuple((jax.ShapeDtypeStruct(s, t...]
where the time goes in v4:
time: 186 us
  Pallas kernels  185 us (99%)
    pallas_call x1, Pallas kernels, experts(): pl.pallas_call(expert_kernel, out_shape=(jax.ShapeDtypeStruct((64, 8, WID...  64.9 us
    pallas_call x1, Pallas kernels, finish(): pl.pallas_call(finish_kernel, out_shape=tuple((jax.ShapeDtypeStruct((8, c...  42.3 us
    pallas_call x1, Pallas kernels, gather_layer(): pl.pallas_call(gather_kernel, out_shape=(jax.ShapeDtypeStruct((2, SIDE, S...  36 us
    pallas_call x1, Pallas kernels, backward(): pl.pallas_call(backward_kernel, out_shape=tuple((jax.ShapeDtypeStruct(s,...  20.9 us
    pallas_call x1, Pallas kernels, forward(): pl.pallas_call(forward_kernel, out_shape=tuple((jax.ShapeDtypeStruct(s, t...  18.1 us

profile of v4, /device:TPU:0, one launch (start us, length us, event | category | flops | bytes accessed | tf_op | source)
XLA Modules:
  0.0 185.9 jit_solution(1265284730502000593)
XLA Ops:
  1.3 36.0 %gather_layer.1 = (bf16[2,4,4,4,8,4224]{5,4,3,2,1,0:T(8,128)(2,1)}, bf16[512,4096]{1,0:T(8,128)(2,1)}, bf16[2048,1024]{1,0:T(8,128)(2,1)}) custom-call(bf16[8,3072]{1,0:T(8,128)(2,1)} %q.1, bf16[8,1024]{1,0:T(8,128)(2,1)} %o.1, bf16[8,64]{1,0:T(8,128)(2,1)} %r.1, bf16[1,8]{1,0:T(2,128)(2,1)} %bitcast.31, bf16[1,8]{1,0:T(2,128)(2,1)} %bitcast.32, ...), custom_call_target="tpu_custom_call" | custom-call | tf_op jit(solution)/shard_map/gather_layer/pallas_call | solution.py:166
  37.3 18.1 %forward.1 = (bf16[64,8,1024]{2,1,0:T(8,128)(2,1)}, bf16[64,8,1152]{2,1,0:T(8,128)(2,1)}, bf16[256,3072]{1,0:T(8,128)(2,1)}, bf16[256,2048]{1,0:T(8,128)(2,1)}, ...) custom-call(bf16[256,1024]{1,0:T(8,128)(2,1)} %bitcast.28, ...), custom_call_target="tpu_custom_call" | custom-call | tf_op jit(solution)/shard_map/forward/pallas_call | solution.py:910
  55.4 64.9 %experts.1 = (bf16[64,8,1024]{2,1,0:T(8,128)(2,1)}, bf16[64,8,1024]{2,1,0:T(8,128)(2,1)}, f32[512,4096]{1,0:T(8,128)}, f32[2048,1024]{1,0:T(8,128)}) custom-call(bf16[64,8,1024]{2,1,0:T(8,128)(2,1)} %get-tuple-element.55.x, bf16[64,8,1152]{2,1,0:T(8,128)(2,1)} %get-tuple-element.56.r, bf16[512,4096]{1,0:T(8,128)(2,1)} %bitcast.23, ...), custom_call_target="tpu_custom_call" | custom-call | tf_op jit(solution)/shard_map/experts/pallas_call | solution.py:656
  120.3 20.9 %backward.1 = (bf16[256,1024]{1,0:T(8,128)(2,1)}, f32[256,1024]{1,0:T(8,128)}, bf16[256,1024]{1,0:T(8,128)(2,1)}, bf16[256,2048]{1,0:T(8,128)(2,1)}, bf16[256,20...) custom-call(bf16[64,8,1024]{2,1,0:T(8,128)(2,1)} %get-tuple-element., ...), custom_call_target="tpu_custom_call" | custom-call | tf_op jit(solution)/shard_map/backward/pallas_call | solution.py:1129
  141.2 42.3 %finish.1 = (f32[8,3072]{1,0:T(8,128)}, f32[8,1024]{1,0:T(8,128)}, f32[8,256]{1,0:T(8,128)}, f32[256,1024]{1,0:T(8,128)}) custom-call(bf16[256,1024]{1,0:T(8,128)(2,1)} %bitcast.29, bf16[256,1024]{1,0:T(8,128)(2,1)} %get-tuple-element.72.norm1, bf16[256,1024]{1,0:T(8,128)(2,1)} %get-tuple-element.73.attended, ...), custom_call_target="tpu_custom_call" | custom-call | tf_op jit(solution)/shard_map/finish/pallas_call | solution.py:1320
  183.5 2.4 %results.1 = (f32[8,3072]{1,0:T(8,128)}, f32[8,1024]{1,0:T(8,128)}, f32[8,64]{1,0:T(8,128)}, f32[1,8]{1,0:T(1,128)}, f32[1,8]{1,0:T(1,128)}, /*index=5*/f32[1,8]...) custom-call(f32[8,3072]{1,0:T(8,128)} %get-tuple-element.81.sum_qkv, ...), custom_call_target="tpu_custom_call" | custom-call | tf_op jit(solution)/shard_map/results/pallas_call | solution.py:1375

commit v5 on v4

--- a/solution.py
+++ b/solution.py
@@ -702,7 +702,7 @@
 HEADS = 16
 PAIRS = HEADS // 2
 SLOTS = 512
-BLOCK = 32
+BLOCK = 64
 EPS = 1e-05
 MASKED = -1e30
 

time: 186 us -> 183 us (0.984)
  Pallas kernels: 185 us -> 182 us
where the time goes in v5:
time: 183 us
  Pallas kernels  182 us (99%)
    pallas_call x1, Pallas kernels, experts(): pl.pallas_call(expert_kernel, out_shape=(jax.ShapeDtypeStruct((64, 8, WID...  64.9 us
    pallas_call x1, Pallas kernels, finish(): pl.pallas_call(finish_kernel, out_shape=tuple((jax.ShapeDtypeStruct((8, c...  41.3 us
    pallas_call x1, Pallas kernels, gather_layer(): pl.pallas_call(gather_kernel, out_shape=(jax.ShapeDtypeStruct((2, SIDE, S...  36 us
    pallas_call x1, Pallas kernels, backward(): pl.pallas_call(backward_kernel, out_shape=tuple((jax.ShapeDtypeStruct(s,...  19.1 us
    pallas_call x1, Pallas kernels, forward(): pl.pallas_call(forward_kernel, out_shape=tuple((jax.ShapeDtypeStruct(s, t...  18.1 us

profile of v5, /device:TPU:0, one launch (start us, length us, event | category | flops | bytes accessed | tf_op | source)
XLA Modules:
  0.0 183.0 jit_solution(17278818837867114318)
XLA Ops:
  1.3 36.0 %gather_layer.1 = (bf16[2,4,4,4,8,4224]{5,4,3,2,1,0:T(8,128)(2,1)}, bf16[512,4096]{1,0:T(8,128)(2,1)}, bf16[2048,1024]{1,0:T(8,128)(2,1)}) custom-call(bf16[8,3072]{1,0:T(8,128)(2,1)} %q.1, bf16[8,1024]{1,0:T(8,128)(2,1)} %o.1, bf16[8,64]{1,0:T(8,128)(2,1)} %r.1, bf16[1,8]{1,0:T(2,128)(2,1)} %bitcast.31, bf16[1,8]{1,0:T(2,128)(2,1)} %bitcast.32, ...), custom_call_target="tpu_custom_call" | custom-call | tf_op jit(solution)/shard_map/gather_layer/pallas_call | solution.py:166
  37.3 18.1 %forward.1 = (bf16[64,8,1024]{2,1,0:T(8,128)(2,1)}, bf16[64,8,1152]{2,1,0:T(8,128)(2,1)}, bf16[256,3072]{1,0:T(8,128)(2,1)}, bf16[256,2048]{1,0:T(8,128)(2,1)}, ...) custom-call(bf16[256,1024]{1,0:T(8,128)(2,1)} %bitcast.28, ...), custom_call_target="tpu_custom_call" | custom-call | tf_op jit(solution)/shard_map/forward/pallas_call | solution.py:910
  55.4 64.9 %experts.1 = (bf16[64,8,1024]{2,1,0:T(8,128)(2,1)}, bf16[64,8,1024]{2,1,0:T(8,128)(2,1)}, f32[512,4096]{1,0:T(8,128)}, f32[2048,1024]{1,0:T(8,128)}) custom-call(bf16[64,8,1024]{2,1,0:T(8,128)(2,1)} %get-tuple-element.55.x, bf16[64,8,1152]{2,1,0:T(8,128)(2,1)} %get-tuple-element.56.r, bf16[512,4096]{1,0:T(8,128)(2,1)} %bitcast.23, ...), custom_call_target="tpu_custom_call" | custom-call | tf_op jit(solution)/shard_map/experts/pallas_call | solution.py:656
  120.3 19.1 %backward.1 = (bf16[256,1024]{1,0:T(8,128)(2,1)}, f32[256,1024]{1,0:T(8,128)}, bf16[256,1024]{1,0:T(8,128)(2,1)}, bf16[256,2048]{1,0:T(8,128)(2,1)}, bf16[256,20...) custom-call(bf16[64,8,1024]{2,1,0:T(8,128)(2,1)} %get-tuple-element., ...), custom_call_target="tpu_custom_call" | custom-call | tf_op jit(solution)/shard_map/backward/pallas_call | solution.py:1129
  139.3 41.3 %finish.1 = (f32[8,3072]{1,0:T(8,128)}, f32[8,1024]{1,0:T(8,128)}, f32[8,256]{1,0:T(8,128)}, f32[256,1024]{1,0:T(8,128)}) custom-call(bf16[256,1024]{1,0:T(8,128)(2,1)} %bitcast.29, bf16[256,1024]{1,0:T(8,128)(2,1)} %get-tuple-element.72.norm1, bf16[256,1024]{1,0:T(8,128)(2,1)} %get-tuple-element.73.attended, ...), custom_call_target="tpu_custom_call" | custom-call | tf_op jit(solution)/shard_map/finish/pallas_call | solution.py:1320
  180.6 2.4 %results.1 = (f32[8,3072]{1,0:T(8,128)}, f32[8,1024]{1,0:T(8,128)}, f32[8,64]{1,0:T(8,128)}, f32[1,8]{1,0:T(1,128)}, f32[1,8]{1,0:T(1,128)}, /*index=5*/f32[1,8]...) custom-call(f32[8,3072]{1,0:T(8,128)} %get-tuple-element.81.sum_qkv, ...), custom_call_target="tpu_custom_call" | custom-call | tf_op jit(solution)/shard_map/results/pallas_call | solution.py:1375
